TPU v7x, 128 devices: a whole 4x4x4 slice. The times are simulated.
128 devices in a mesh: px: 8 (over x, core), py: 16 (over y, z).
Axes of the slice: x: 4, y: 4, z: 4, core: 2. Of those that a mesh axis runs over, the one named last changes fastest.
Arguments:
- root_density: float32 [384, 384, 384], P('px', 'py'), may hold values from -6 to 6
- subgrid_density: float32 [2048, 32, 1024], P(('px', 'py')), may hold values from -24 to 24
- velocity: float32 [3, 2048, 32, 1024], P(None, ('px', 'py')), may hold values from -6 to 6
- slot_anchor: int32 [3, 2048], replicated, may hold values from 0 to 376, as said below
- slot_count: int32 [128], replicated, may hold values from 1 to 16, as said below
- neighbour: int32 [2, 2048], replicated, may hold values from -1 to 2047, as said below
Outputs:
- coarse_potential: float32 [384, 384, 384], P('px', 'py')
- subgrid_potential: float32 [2048, 32, 1024], P(('px', 'py'))
- kicked_velocity: float32 [3, 2048, 32, 1024], P(None, ('px', 'py'))
Inputs may be any that keep to these rules, and one draw needn't show every extreme that they name: Slot j of device d is slot d * 16 + j, devices numbered in the order of px+py; it is live when j < slot_count[d]. Some device has every slot live. `slot_anchor`: entries are multiples of 8; live slots cover distinct regions of 8^3 root cells; empty slots hold 0. The region of live slot j of the device at px = p, py = q has its lower corner among the root cells that the device at px = p, py = (q + j) mod 16 holds of root_density. neighbour[0, s] is s - 16 or -1 and neighbour[1, s] is s + 16 or -1, the same slot of the device one index lower or higher along py with the same px; where set, both slots are live and the two regions lie next to each other along the second dimension, the lower one below. Empty slots hold -1.
All inputs are finite; a program needn't handle non-finite values.
Results may differ from a plain program's by a relative error of at most 0.000094.
Values sent between devices are 32-bit elements; how exact they have to be, the bound alone decides.
No kernel may reach another device: no remote copies, remote signals or barrier semaphores. Data moves between devices by JAX's collectives and lax.ppermute only.
A program may use at most 128 MiB of HBM per device.

v0:
```python
import jax
import jax.numpy as jnp
from jax import lax
from jax.sharding import PartitionSpec as P

NR = 384
REG = 8
REF = 4
SWEEPS = 4


HIGHEST_PRECISION = lax.Precision.HIGHEST
RELAXATION = 6.0 / 7.0
EINSUM_FORMS = ("abc,ad->dbc", "abc,bd->adc", "abc,cd->abd")


def from_behind(value, axis, steps):
    count = lax.axis_size(axis)
    initial, last = (max(0, -steps), min(count, count - steps))
    return lax.ppermute(value, axis, [(source, source + steps) for source in range(initial, last)])


def extended(block, sides, width):
    for axis, dim in sides:
        count = lax.axis_size(axis)
        forward = [(i, i + 1) for i in range(count - 1)]
        forward.append((count - 1, 0))
        backward = [(target, source) for source, target in forward]
        low = lax.ppermute(
            lax.slice_in_dim(block, block.shape[dim] - width, None, axis=dim), axis, forward
        )
        high = lax.ppermute(lax.slice_in_dim(block, 0, width, axis=dim), axis, backward)
        block = jnp.concatenate([low, block, high], axis=dim)
    return block


def tables(length):
    positions = jnp.arange(length, dtype=jnp.int32)
    angle_table = (
        2.0
        * jnp.pi
        / length
        * (positions[:, None] * positions[None, :] % length).astype(jnp.float32)
    )
    return (jnp.cos(angle_table), jnp.sin(angle_table))


def transform_along(values_in, matrix, axis_number):
    return jnp.einsum(EINSUM_FORMS[axis_number], values_in, matrix, precision=HIGHEST_PRECISION)


def forward(complex_pair, axis_number, cosine_table, sine_table):
    real_part, imag_part = complex_pair
    return (
        transform_along(real_part, cosine_table, axis_number)
        + transform_along(imag_part, sine_table, axis_number),
        transform_along(imag_part, cosine_table, axis_number)
        - transform_along(real_part, sine_table, axis_number),
    )


def inverse(complex_pair, axis_number, cosine_table, sine_table):
    real_part, imag_part = complex_pair
    scale_factor = 1.0 / cosine_table.shape[0]
    return (
        (
            transform_along(real_part, cosine_table, axis_number)
            - transform_along(imag_part, sine_table, axis_number)
        )
        * scale_factor,
        (
            transform_along(imag_part, cosine_table, axis_number)
            + transform_along(real_part, sine_table, axis_number)
        )
        * scale_factor,
    )


def eigenvalue(wavenumber):
    return -4.0 * jnp.sin(jnp.pi / NR * wavenumber.astype(jnp.float32)) ** 2


def green_block(wave_first, wave_second, wave_third):
    total = (
        eigenvalue(wave_first)[:, None, None]
        + eigenvalue(wave_second)[None, :, None]
        + eigenvalue(wave_third)[None, None, :]
    )
    zero_mode = (
        (wave_first[:, None, None] == 0)
        & (wave_second[None, :, None] == 0)
        & (wave_third[None, None, :] == 0)
    )
    safe_total = jnp.where(zero_mode, -1.0, total)
    return jnp.where(zero_mode, 0.0, 1.0 / safe_total)


def weights_table():
    cells = jnp.arange(REG * REF + 2, dtype=jnp.int32)
    marks = 2 * cells - 1 + REF
    lower_cell = jnp.minimum(marks // (2 * REF), REG)
    fraction = (marks - 2 * REF * lower_cell).astype(jnp.float32) / (2 * REF)
    columns = jnp.arange(REG + 2, dtype=jnp.int32)
    return jnp.where(
        columns[None, :] == lower_cell[:, None], 1.0 - fraction[:, None], 0.0
    ) + jnp.where(columns[None, :] == lower_cell[:, None] + 1, fraction[:, None], 0.0)


def coarse_parts(patch_flat, weights):
    inner = weights[1:-1]
    cells = inner.shape[0]
    width = weights.shape[1]
    both_inner = jnp.einsum("jb,kc->jkbc", inner, inner, precision=HIGHEST_PRECISION).reshape(
        cells * cells, width * width
    )
    second_low = jnp.einsum("b,kc->kbc", weights[0], inner, precision=HIGHEST_PRECISION).reshape(
        cells, width * width
    )
    second_high = jnp.einsum("b,kc->kbc", weights[-1], inner, precision=HIGHEST_PRECISION).reshape(
        cells, width * width
    )
    third_low = jnp.einsum("jb,c->jbc", inner, weights[0], precision=HIGHEST_PRECISION).reshape(
        cells, width * width
    )
    third_high = jnp.einsum("jb,c->jbc", inner, weights[-1], precision=HIGHEST_PRECISION).reshape(
        cells, width * width
    )
    plane_values = jnp.einsum("sam,nm->san", patch_flat, both_inner, precision=HIGHEST_PRECISION)
    interior = jnp.einsum("san,ia->sin", plane_values, inner, precision=HIGHEST_PRECISION)
    first_low_face = jnp.einsum("san,a->sn", plane_values, weights[0], precision=HIGHEST_PRECISION)
    first_high_face = jnp.einsum(
        "san,a->sn", plane_values, weights[-1], precision=HIGHEST_PRECISION
    )

    def face_of(table):
        partial_face = jnp.einsum("sam,km->sak", patch_flat, table, precision=HIGHEST_PRECISION)
        return jnp.einsum("sak,ia->sik", partial_face, inner, precision=HIGHEST_PRECISION)

    return (
        interior,
        first_low_face,
        first_high_face,
        face_of(second_low),
        face_of(second_high),
        face_of(third_low),
        face_of(third_high),
    )


def spread_third(face_values, cells, corner):
    positions = jnp.arange(cells * cells, dtype=jnp.int32)
    rows = jnp.arange(cells, dtype=jnp.int32)
    placer = (positions[None, :] == rows[:, None] * cells + corner).astype(jnp.float32)
    return jnp.einsum("sij,jn->sin", face_values, placer, precision=HIGHEST_PRECISION)


def beside_values(interior, first_faces, second_faces, third_full, third_place):
    cells = interior.shape[1]
    slots = interior.shape[0]
    first_low, first_high = first_faces
    second_low, second_high = second_faces
    third_low, third_high = third_full
    below_first = jnp.concatenate([first_low[:, None, :], interior[:, :-1]], axis=1)
    above_first = jnp.concatenate([interior[:, 1:], first_high[:, None, :]], axis=1)
    below_second = jnp.concatenate([second_low, interior[:, :, :-cells]], axis=2)
    above_second = jnp.concatenate([interior[:, :, cells:], second_high], axis=2)
    zero_column = jnp.zeros((slots, cells, 1), jnp.float32)
    below_third = jnp.where(
        third_place == 0, third_low, jnp.concatenate([zero_column, interior[:, :, :-1]], axis=2)
    )
    above_third = jnp.where(
        third_place == cells - 1,
        third_high,
        jnp.concatenate([interior[:, :, 1:], zero_column], axis=2),
    )
    return ((below_first, above_first), (below_second, above_second), (below_third, above_third))


def cut_patches(padded, anchors, corner_first, corner_second):
    offsets = jnp.arange(REG + 2, dtype=jnp.int32)
    index_first = jnp.clip(
        anchors[0][:, None] - corner_first + offsets[None, :], 0, padded.shape[0] - 1
    )
    index_second = jnp.clip(
        anchors[1][:, None] - corner_second + offsets[None, :], 0, padded.shape[1] - 1
    )
    index_third = (anchors[2][:, None] - 1 + offsets[None, :]) % NR
    picked = padded[
        index_first[:, :, None, None], index_second[:, None, :, None], index_third[:, None, None, :]
    ]
    return picked.reshape(anchors.shape[1], -1)


def neighbour_faces(interior):
    cells = interior.shape[1]
    top_layer = interior[:, :, (cells - 1) * cells :]
    bottom_layer = interior[:, :, :cells]
    from_below = from_behind(top_layer, "py", 1)
    from_above = from_behind(bottom_layer, "py", -1)
    return (from_below, from_above)


def local(root_density, subgrid_density, velocity, slot_anchor, slot_count, neighbour):
    cosine_table, sine_table = tables(NR)
    first_rows = root_density.shape[0]
    second_rows = root_density.shape[1]
    size_second = lax.axis_size("py")
    place_first = lax.axis_index("px")
    place_second = lax.axis_index("py")
    device = place_first * size_second + place_second
    every_wave = jnp.arange(NR, dtype=jnp.int32)
    real_part = transform_along(root_density, cosine_table, 2)
    imag_part = -transform_along(root_density, sine_table, 2)
    spectrum = (
        lax.all_to_all(real_part, "py", split_axis=0, concat_axis=1, tiled=True),
        lax.all_to_all(imag_part, "py", split_axis=0, concat_axis=1, tiled=True),
    )
    spectrum = forward(spectrum, 1, cosine_table, sine_table)
    spectrum = (
        lax.all_to_all(spectrum[0], ("px", "py"), split_axis=1, concat_axis=0, tiled=True),
        lax.all_to_all(spectrum[1], ("px", "py"), split_axis=1, concat_axis=0, tiled=True),
    )
    band = spectrum[0].shape[1]
    band_start = device * band
    spectrum = forward(spectrum, 0, cosine_table, sine_table)
    factor = green_block(every_wave, band_start + jnp.arange(band, dtype=jnp.int32), every_wave)
    spectrum = inverse((spectrum[0] * factor, spectrum[1] * factor), 0, cosine_table, sine_table)
    spectrum = (
        lax.all_to_all(spectrum[0], ("px", "py"), split_axis=0, concat_axis=1, tiled=True),
        lax.all_to_all(spectrum[1], ("px", "py"), split_axis=0, concat_axis=1, tiled=True),
    )
    spectrum = inverse(spectrum, 1, cosine_table, sine_table)
    spectrum = (
        lax.all_to_all(spectrum[0], "py", split_axis=1, concat_axis=0, tiled=True),
        lax.all_to_all(spectrum[1], "py", split_axis=1, concat_axis=0, tiled=True),
    )
    coarse_potential = (
        transform_along(spectrum[0], cosine_table, 2) - transform_along(spectrum[1], sine_table, 2)
    ) * (1.0 / NR)
    per_device = subgrid_density.shape[0]
    cells = subgrid_density.shape[1]
    positions = jnp.arange(per_device, dtype=jnp.int32)
    corner_first = place_first * first_rows
    corner_second = place_second * second_rows
    padded = extended(coarse_potential, (("px", 0), ("py", 1)), 1)
    targets = jnp.arange(size_second, dtype=jnp.int32)
    owner_devices = place_first * size_second + targets
    wanted_slot = (place_second - targets) % size_second
    global_slot = owner_devices * per_device + wanted_slot
    sending_live = wanted_slot < slot_count[owner_devices]
    sending = cut_patches(padded, slot_anchor[:, global_slot], corner_first, corner_second)
    sending = jnp.where(sending_live[:, None], sending, 0.0)
    arrived = lax.all_to_all(sending, "py", split_axis=0, concat_axis=0, tiled=True)
    patch = arrived[(place_second + positions) % size_second]
    patch_flat = patch.reshape(per_device, REG + 2, (REG + 2) * (REG + 2))
    interior, first_low, first_high, second_low, second_high, third_low, third_high = coarse_parts(
        patch_flat, weights_table()
    )
    third_full = (spread_third(third_low, cells, 0), spread_third(third_high, cells, cells - 1))
    third_place = jnp.arange(cells * cells, dtype=jnp.int32) % cells
    own_live = positions < slot_count[device]
    first_slot = device * per_device
    nearby = lax.dynamic_slice_in_dim(neighbour, first_slot, per_device, 1)
    use_below = (nearby[0] >= 0)[:, None, None]
    use_above = (nearby[1] >= 0)[:, None, None]

    def all_beside(current):
        from_below, from_above = neighbour_faces(current)
        second_faces = (
            jnp.where(use_below, from_below, second_low),
            jnp.where(use_above, from_above, second_high),
        )
        return beside_values(
            current, (first_low, first_high), second_faces, third_full, third_place
        )

    for sweep_index in range(SWEEPS):
        along_first, along_second, along_third = all_beside(interior)
        beside_all = (
            along_first[1]
            + along_first[0]
            + along_second[1]
            + along_second[0]
            + along_third[1]
            + along_third[0]
        )
        interior = (1.0 - RELAXATION) * interior + RELAXATION * (
            beside_all - subgrid_density * (1.0 / (REF * REF))
        ) / 6.0
    along_first, along_second, along_third = all_beside(interior)
    scale_factor = REF / 2.0
    slopes = jnp.stack(
        [
            (along_first[1] - along_first[0]) * scale_factor,
            (along_second[1] - along_second[0]) * scale_factor,
            (along_third[1] - along_third[0]) * scale_factor,
        ]
    )
    subgrid_potential = jnp.where(own_live[:, None, None], interior, 0.0)
    velocity_after_kick = jnp.where(own_live[None, :, None, None], velocity - slopes, 0.0)
    return (coarse_potential, subgrid_potential, velocity_after_kick)


def solution(mesh):
    return jax.shard_map(
        local,
        mesh=mesh,
        in_specs=(
            P("px", "py", None),
            P(("px", "py"), None, None),
            P(None, ("px", "py"), None, None),
            P(),
            P(),
            P(),
        ),
        out_specs=(
            P("px", "py", None),
            P(("px", "py"), None, None),
            P(None, ("px", "py"), None, None),
        ),
        check_vma=False,
    )
```

profile of v0, /device:TPU:96, one launch (start us, length us, event | category | flops | bytes accessed | tf_op | source)
XLA Modules:
  0.0 679.2 jit_solution(3072733215062630244)
XLA Ops:
  2.1 5.8 negate_bitcast_fusion
  9.6 7.8 %all-to-all-start.1 = ((f32[48,24,384]{2,1,0:T(8,128)}), f32[48,24,384]{2,1,0:T(8,128)S(1)}, u32[]{:S(2)}, u32[]{:S(2)}) async-start(f32[48,24,384]{2,1,0:T(8,128)} %copy.93), calls=%async_computation.1 | async-start | bytes 3538944 | tf_op jit(solution)/shard_map/all_to_all | solution.py:216
  17.4 5.8 fusion.38
  24.9 15.3 %all-to-all-done.1 = f32[48,24,384]{2,1,0:T(8,128)S(1)} async-done(((f32[48,24,384]{2,1,0:T(8,128)}), f32[48,24,384]{2,1,0:T(8,128)S(1)}, u32[]{:S(2)}, u32[]{:S(2)}) %all-to-all-start.1) | async-done | bytes 1769504 | tf_op jit(solution)/shard_map/all_to_all | solution.py:216
  40.2 7.7 %all-to-all-start = ((f32[48,24,384]{2,1,0:T(8,128)}), f32[48,24,384]{2,1,0:T(8,128)}, u32[]{:S(2)}, u32[]{:S(2)}) async-start(f32[48,24,384]{2,1,0:T(8,128)} %copy.89), calls=%async_computation | async-start | bytes 3538944 | tf_op jit(solution)/shard_map/all_to_all | solution.py:215
  48.1 21.4 %all-to-all-done = f32[48,24,384]{2,1,0:T(8,128)} async-done(((f32[48,24,384]{2,1,0:T(8,128)}), f32[48,24,384]{2,1,0:T(8,128)}, u32[]{:S(2)}, u32[]{:S(2)}) %all-to-all-start) | async-done | bytes 1769504 | tf_op jit(solution)/shard_map/all_to_all | solution.py:215
  71.0 5.3 fusion.71
  76.3 5.4 add_bitcast_fusion
  84.7 9.3 %all-to-all-start.2 = ((f32[3,384,384]{2,0,1:T(4,128)}), f32[3,384,384]{2,0,1:T(4,128)}, u32[]{:S(2)}, u32[]{:S(2)}) async-start(f32[3,384,384]{2,0,1:T(4,128)} %copy.96), calls=%async_computation.2 | async-start | bytes 4718592 | tf_op jit(solution)/shard_map/all_to_all | solution.py:220
  94.1 5.3 fusion.66
  99.4 5.4 subtract_bitcast_fusion
  107.6 17.3 %all-to-all-done.2 = f32[3,384,384]{2,0,1:T(4,128)} async-done(((f32[3,384,384]{2,0,1:T(4,128)}), f32[3,384,384]{2,0,1:T(4,128)}, u32[]{:S(2)}, u32[]{:S(2)}) %all-to-all-start.2) | async-done | bytes 1769504 | tf_op jit(solution)/shard_map/all_to_all | solution.py:220
  124.8 6.2 all-to-all-start.3
  134.8 4.1 all_to_all.121
  138.9 23.2 %all-to-all-done.3 = f32[3,384,384]{2,0,1:T(4,128)S(1)} async-done(((f32[3,384,384]{2,0,1:T(4,128)}), f32[3,384,384]{2,0,1:T(4,128)S(1)}, u32[]{:S(2)}, u32[]{:S(2)}) %all-to-all-start.3) | async-done | bytes 1769504 | tf_op jit(solution)/shard_map/all_to_all | solution.py:221
  166.7 5.3 fusion.64
  172.1 5.3 fusion.73
  177.4 6.2 subtract_multiply_fusion.2
  183.6 5.8 add_multiply_fusion.1
  189.4 5.5 fusion.62
  194.9 5.4 add_multiply_fusion
  202.9 6.6 all-to-all-start.5
  209.5 6.9 %fusion.75 = f32[384,3,384]{2,0,1:T(8,128)S(1)} fusion(f32[384,3,384]{2,0,1:T(8,128)} %copy-done.8), kind=kOutput, calls=%fused_computation.115 | convolution fusion | flops 2039758848 | bytes 3538944 | tf_op jit(solution)/shard_map/abc,ad->dbc/dot_general | solution.py:49
  216.4 5.4 subtract_multiply_fusion.1
  224.6 15.5 %all-to-all-done.5 = f32[384,3,384]{2,1,0:T(4,128)S(1)} async-done(((f32[384,3,384]{2,1,0:T(4,128)}), f32[384,3,384]{2,1,0:T(4,128)S(1)}, u32[]{:S(2)}, u32[]{:S(2)}) %all-to-all-start.5) | async-done | bytes 1769504 | tf_op jit(solution)/shard_map/all_to_all | solution.py:230
  240.1 7.0 %all-to-all-start.4 = ((f32[384,3,384]{2,1,0:T(4,128)}), f32[384,3,384]{2,1,0:T(4,128)}, u32[]{:S(2)}, u32[]{:S(2)}) async-start(f32[384,3,384]{2,1,0:T(4,128)} %copy.110), calls=%async_computation.4 | async-start | bytes 4718592 | tf_op jit(solution)/shard_map/all_to_all | solution.py:229
  255.7 22.1 %all-to-all-done.4 = f32[384,3,384]{2,1,0:T(4,128)} async-done(((f32[384,3,384]{2,1,0:T(4,128)}), f32[384,3,384]{2,1,0:T(4,128)}, u32[]{:S(2)}, u32[]{:S(2)}) %all-to-all-start.4) | async-done | bytes 1769504 | tf_op jit(solution)/shard_map/all_to_all | solution.py:229
  284.2 5.3 fusion.60
  289.5 5.4 multiply_bitcast_fusion.1
  297.9 5.9 all-to-all-start.7
  309.2 5.3 fusion.77
  314.5 5.4 multiply_bitcast_fusion.2
  322.7 11.2 %all-to-all-done.7 = f32[3,384,384]{2,0,1:T(4,128)} async-done(((f32[3,384,384]{2,0,1:T(4,128)}), f32[3,384,384]{2,0,1:T(4,128)}, u32[]{:S(2)}, u32[]{:S(2)}) %all-to-all-start.7) | async-done | bytes 1769504 | tf_op jit(solution)/shard_map/all_to_all | solution.py:235
  333.9 6.9 %all-to-all-start.6 = ((f32[3,384,384]{2,0,1:T(4,128)}), f32[3,384,384]{2,0,1:T(4,128)S(1)}, u32[]{:S(2)}, u32[]{:S(2)}) async-start(f32[3,384,384]{2,0,1:T(4,128)} %copy.120), calls=%async_computation.6 | async-start | bytes 4718592 | tf_op jit(solution)/shard_map/all_to_all | solution.py:234
  348.4 20.7 %all-to-all-done.6 = f32[3,384,384]{2,0,1:T(4,128)S(1)} async-done(((f32[3,384,384]{2,0,1:T(4,128)}), f32[3,384,384]{2,0,1:T(4,128)S(1)}, u32[]{:S(2)}, u32[]{:S(2)}) %all-to-all-start.6) | async-done | bytes 1769504 | tf_op jit(solution)/shard_map/all_to_all | solution.py:234
  369.2 5.8 fusion.68
  375.0 6.3 subtract_multiply_fusion
  402.2 151.5 %gather_fusion.2 = f32[16000]{0:T(1024)S(1)} fusion(f32[50,26,384]{2,1,0:T(8,128)S(1)} %pad_maximum_fusion.8, s32[16000]{0:T(1024)S(1)} %reshape.573), kind=kCustom, calls=%fused_computation.2 | custom fusion | bytes 320000 | tf_op jit(solution)/shard_map/gather | solution.py:188
  554.6 9.3 %all-to-all-start.8 = ((f32[16,1,1000]{2,1,0:T(1,128)}), f32[16,1,1000]{2,1,0:T(1,128)S(1)}, u32[]{:S(2)}, u32[]{:S(2)}) async-start(f32[16,1,1000]{2,1,0:T(1,128)} %broadcast_select_fusion.1), calls=%async_computation.8 | async-start | bytes 131072 | tf_op jit(solution)/shard_map/all_to_all | solution.py:253
  564.5 5.1 all-to-all-done.8
  584.9 5.5 collective-permute-start.5
  599.0 6.5 collective-permute-start.7
  609.4 7.3 %collective-permute-done.6 = f32[16,32,32]{2,1,0:T(8,128)S(1)} collective-permute-done((f32[16,32,32]{2,1,0:T(8,128)S(1)}, f32[16,32,32]{2,1,0:T(8,128)S(1)}, u32[]{:S(2)}, u32[]{:S(2)}) %collective-permute-start.6) | collective-permute-done | bytes 65568 | tf_op jit(solution)/shard_map/ppermute | solution.py:20
  623.9 6.0 collective-permute-start.9
  641.0 6.7 collective-permute-start.11
  651.4 4.0 broadcast_select_fusion
  657.7 6.5 collective-permute-start.13
  668.2 6.4 collective-permute-done.12
  (213 shorter events, 142.2 us)
Async XLA Ops:
  9.6 30.6 %all-to-all-start.1 = ((f32[48,24,384]{2,1,0:T(8,128)}), f32[48,24,384]{2,1,0:T(8,128)S(1)}, u32[]{:S(2)}, u32[]{:S(2)}) async-start(f32[48,24,384]{2,1,0:T(8,128)} %copy.93), calls=%async_computation.1 | async-start | bytes 3538944 | tf_op jit(solution)/shard_map/all_to_all | solution.py:216
  40.2 29.3 %all-to-all-start = ((f32[48,24,384]{2,1,0:T(8,128)}), f32[48,24,384]{2,1,0:T(8,128)}, u32[]{:S(2)}, u32[]{:S(2)}) async-start(f32[48,24,384]{2,1,0:T(8,128)} %copy.89), calls=%async_computation | async-start | bytes 3538944 | tf_op jit(solution)/shard_map/all_to_all | solution.py:215
  84.7 40.1 %all-to-all-start.2 = ((f32[3,384,384]{2,0,1:T(4,128)}), f32[3,384,384]{2,0,1:T(4,128)}, u32[]{:S(2)}, u32[]{:S(2)}) async-start(f32[3,384,384]{2,0,1:T(4,128)} %copy.96), calls=%async_computation.2 | async-start | bytes 4718592 | tf_op jit(solution)/shard_map/all_to_all | solution.py:220
  124.8 37.2 %all-to-all-start.3 = ((f32[3,384,384]{2,0,1:T(4,128)}), f32[3,384,384]{2,0,1:T(4,128)S(1)}, u32[]{:S(2)}, u32[]{:S(2)}) async-start(f32[3,384,384]{2,0,1:T(4,128)} %copy.102), calls=%async_computation.3 | async-start | bytes 4718592 | tf_op jit(solution)/shard_map/all_to_all | solution.py:221
  183.6 5.8 copy-start.6
  202.9 37.2 %all-to-all-start.5 = ((f32[384,3,384]{2,1,0:T(4,128)}), f32[384,3,384]{2,1,0:T(4,128)S(1)}, u32[]{:S(2)}, u32[]{:S(2)}) async-start(f32[384,3,384]{2,1,0:T(4,128)} %copy.116), calls=%async_computation.5 | async-start | bytes 4718592 | tf_op jit(solution)/shard_map/all_to_all | solution.py:230
  209.5 6.9 %copy-start.7 = (f32[384,3,384]{2,0,1:T(8,128)S(1)}, f32[384,3,384]{2,0,1:T(8,128)}, u32[]{:S(2)}) copy-start(f32[384,3,384]{2,0,1:T(8,128)} %copy-done.6) | copy-start | bytes 5308420
  224.6 22.5 %copy-start.19 = (s32[3,2048]{1,0:T(4,128)S(1)}, s32[3,2048]{1,0:T(4,128)}, u32[]{:S(2)}) copy-start(s32[3,2048]{1,0:T(4,128)} %param.9) | copy-start | bytes 73732
  224.6 22.9 %copy-start.2 = (s32[128]{0:T(128)S(1)}, s32[128]{0:T(128)}, u32[]{:S(2)}) copy-start(s32[128]{0:T(128)} %param.10) | copy-start | bytes 1540
  240.1 37.7 %all-to-all-start.4 = ((f32[384,3,384]{2,1,0:T(4,128)}), f32[384,3,384]{2,1,0:T(4,128)}, u32[]{:S(2)}, u32[]{:S(2)}) async-start(f32[384,3,384]{2,1,0:T(4,128)} %copy.110), calls=%async_computation.4 | async-start | bytes 4718592 | tf_op jit(solution)/shard_map/all_to_all | solution.py:229
  297.9 36.0 %all-to-all-start.7 = ((f32[3,384,384]{2,0,1:T(4,128)}), f32[3,384,384]{2,0,1:T(4,128)}, u32[]{:S(2)}, u32[]{:S(2)}) async-start(f32[3,384,384]{2,0,1:T(4,128)} %copy.124), calls=%async_computation.7 | async-start | bytes 4718592 | tf_op jit(solution)/shard_map/all_to_all | solution.py:235
  305.7 35.9 %copy-start.11 = (f32[34,10]{0,1:T(8,128)}, f32[34,10]{0,1:T(8,128)S(1)}, u32[]{:S(2)}) copy-start(f32[34,10]{0,1:T(8,128)S(1)} %select_add_fusion) | copy-start | bytes 4084
  306.5 36.0 %copy-start.22 = (f32[10]{0:T(128)}, f32[10]{0:T(128)S(1)}, u32[]{:S(2)}) copy-start(f32[10]{0:T(128)S(1)} %get-tuple-element.4) | copy-start | bytes 124
  322.7 19.5 %copy-start.28 = (s32[16]{0:T(128)S(1)}, s32[16]{0:T(128)}, u32[]{:S(2)}) copy-start(s32[16]{0:T(128)} %get-tuple-element.5) | copy-start | bytes 196
  322.7 19.6 %copy-start.27 = (s32[16]{0:T(128)S(1)}, s32[16]{0:T(128)}, u32[]{:S(2)}) copy-start(s32[16]{0:T(128)} %get-tuple-element.6) | copy-start | bytes 196
  322.7 19.6 %copy-start.26 = (s32[16]{0:T(128)S(1)}, s32[16]{0:T(128)}, u32[]{:S(2)}) copy-start(s32[16]{0:T(128)} %get-tuple-element.7) | copy-start | bytes 196
  322.7 19.8 %copy-start.24 = (f32[10]{0:T(128)S(1)}, f32[10]{0:T(128)}, u32[]{:S(2)}) copy-start(f32[10]{0:T(128)} %get-tuple-element.3) | copy-start | bytes 124
  333.9 35.2 %all-to-all-start.6 = ((f32[3,384,384]{2,0,1:T(4,128)}), f32[3,384,384]{2,0,1:T(4,128)S(1)}, u32[]{:S(2)}, u32[]{:S(2)}) async-start(f32[3,384,384]{2,0,1:T(4,128)} %copy.120), calls=%async_computation.6 | async-start | bytes 4718592 | tf_op jit(solution)/shard_map/all_to_all | solution.py:234
  369.2 5.8 copy-start.9
  381.3 16.0 %copy-start.4 = (f32[48,24,384]{2,1,0:T(8,128)}, f32[48,24,384]{2,1,0:T(8,128)S(1)}, u32[]{:S(2)}) copy-start(f32[48,24,384]{2,1,0:T(8,128)S(1)} %subtract_multiply_fusion) | copy-start | bytes 5308420
  381.3 11.4 %collective-permute-start = (f32[1,24,384]{2,1,0:T(8,128)S(1)}, f32[1,24,384]{2,1,0:T(8,128)S(1)}, u32[]{:S(2)}, u32[]{:S(2)}) collective-permute-start(f32[1,24,384]{2,1,0:T(8,128)S(1)} %get-tuple-element.56), channel_id=1, source_target_pairs={{0,16},{16,32},{32,48},{48,64},{64,80},{80,96},{96,112},{112,0},{1... | collective-permute-start | bytes 110600 | tf_op jit(solution)/shard_map/ppermute | solution.py:29
  381.4 11.4 %collective-permute-start.1 = (f32[1,24,384]{2,1,0:T(8,128)S(1)}, f32[1,24,384]{2,1,0:T(8,128)S(1)}, u32[]{:S(2)}, u32[]{:S(2)}) collective-permute-start(f32[1,24,384]{2,1,0:T(8,128)S(1)} %get-tuple-element.57), channel_id=1, source_target_pairs={{16,0},{32,16},{48,32},{64,48},{80,64},{96,80},{112,96},{0,112},{1... | collective-permute-start | bytes 110600 | tf_op jit(solution)/shard_map/ppermute | solution.py:32
  392.9 4.5 collective-permute-start.2
  393.8 6.5 collective-permute-start.3
  402.1 151.7 %copy-start.29 = (pred[16]{0:T(512)(128)(4,1)S(1)}, pred[16]{0:T(512)(128)(4,1)}, u32[]{:S(2)}) copy-start(pred[16]{0:T(512)(128)(4,1)} %fusion.206) | copy-start | bytes 52
  402.2 168.5 %copy-start.10 = (f32[1024,100,1]{0,1,2:T(8,128)S(1)}, f32[1024,100,1]{0,1,2:T(8,128)}, u32[]{:S(2)}) copy-start(f32[1024,100,1]{0,1,2:T(8,128)} %reshape.606) | copy-start | bytes 1228804
  553.7 17.7 %copy-start.25 = (f32[10]{0:T(128)S(1)}, f32[10]{0:T(128)}, u32[]{:S(2)}) copy-start(f32[10]{0:T(128)} %get-tuple-element.3) | copy-start | bytes 124
  553.7 19.0 %copy-start.23 = (f32[10]{0:T(128)S(1)}, f32[10]{0:T(128)}, u32[]{:S(2)}) copy-start(f32[10]{0:T(128)} %copy-done.22) | copy-start | bytes 124
  554.6 15.1 %all-to-all-start.8 = ((f32[16,1,1000]{2,1,0:T(1,128)}), f32[16,1,1000]{2,1,0:T(1,128)S(1)}, u32[]{:S(2)}, u32[]{:S(2)}) async-start(f32[16,1,1000]{2,1,0:T(1,128)} %broadcast_select_fusion.1), calls=%async_computation.8 | async-start | bytes 131072 | tf_op jit(solution)/shard_map/all_to_all | solution.py:253
  578.7 5.6 copy-start.13
  579.5 11.6 %copy-start.20 = (pred[16]{0:T(512)(128)(4,1)S(1)}, pred[16]{0:T(512)(128)(4,1)}, u32[]{:S(2)}) copy-start(pred[16]{0:T(512)(128)(4,1)} %get-tuple-element.68) | copy-start | bytes 52
  580.5 13.7 %copy-start.21 = (pred[16]{0:T(512)(128)(4,1)S(1)}, pred[16]{0:T(512)(128)(4,1)}, u32[]{:S(2)}) copy-start(pred[16]{0:T(512)(128)(4,1)} %get-tuple-element.69) | copy-start | bytes 52
  580.5 14.1 %copy-start.3 = (f32[16,32,1024]{2,1,0:T(8,128)S(1)}, f32[16,32,1024]{2,1,0:T(8,128)}, u32[]{:S(2)}) copy-start(f32[16,32,1024]{2,1,0:T(8,128)} %param.7) | copy-start | bytes 6291460
  580.5 14.1 %copy-start.17 = (pred[1024]{0:T(1024)(128)(4,1)S(1)}, pred[1024]{0:T(1024)(128)(4,1)}, u32[]{:S(2)}) copy-start(pred[1024]{0:T(1024)(128)(4,1)} %get-tuple-element.81) | copy-start | bytes 3076
  580.5 14.1 %copy-start.18 = (pred[1024]{0:T(1024)(128)(4,1)S(1)}, pred[1024]{0:T(1024)(128)(4,1)}, u32[]{:S(2)}) copy-start(pred[1024]{0:T(1024)(128)(4,1)} %get-tuple-element.82) | copy-start | bytes 3076
  580.6 14.1 %copy-start.31 = (s32[32]{0:T(128)S(1)}, s32[32]{0:T(128)}, u32[]{:S(2)}) copy-start(s32[32]{0:T(128)} %iota_multiply_fusion) | copy-start | bytes 388
  580.6 10.5 %collective-permute-start.4 = (f32[16,32,32]{2,1,0:T(8,128)S(1)}, f32[16,32,32]{2,1,0:T(8,128)S(1)}, u32[]{:S(2)}, u32[]{:S(2)}) collective-permute-start(f32[16,32,32]{2,1,0:T(8,128)S(1)} %get-tuple-element.50), channel_id=1, source_target_pairs={{1,0},{2,1},{3,2},{4,3},{5,4},{6,5},{7,6},{8,7},{9,8},{10,9},{11,1... | collective-permute-start | bytes 196616 | tf_op jit(solution)/shard_map/ppermute | solution.py:20
  584.9 9.2 %collective-permute-start.5 = (f32[16,32,32]{2,1,0:T(8,128)S(1)}, f32[16,32,32]{2,1,0:T(8,128)S(1)}, u32[]{:S(2)}, u32[]{:S(2)}) collective-permute-start(f32[16,32,32]{2,1,0:T(8,128)S(1)} %get-tuple-element.51), channel_id=1, source_target_pairs={{0,1},{1,2},{2,3},{3,4},{4,5},{5,6},{6,7},{7,8},{8,9},{9,10},{10,1... | collective-permute-start | bytes 196616 | tf_op jit(solution)/shard_map/ppermute | solution.py:20
  599.0 10.4 %collective-permute-start.7 = (f32[16,32,32]{2,1,0:T(8,128)S(1)}, f32[16,32,32]{2,1,0:T(8,128)S(1)}, u32[]{:S(2)}, u32[]{:S(2)}) collective-permute-start(f32[16,32,32]{2,1,0:T(8,128)S(1)} %get-tuple-element.40), channel_id=1, source_target_pairs={{0,1},{1,2},{2,3},{3,4},{4,5},{5,6},{6,7},{7,8},{8,9},{9,10},{10,1... | collective-permute-start | bytes 196616 | tf_op jit(solution)/shard_map/ppermute | solution.py:20
  606.3 10.4 %collective-permute-start.6 = (f32[16,32,32]{2,1,0:T(8,128)S(1)}, f32[16,32,32]{2,1,0:T(8,128)S(1)}, u32[]{:S(2)}, u32[]{:S(2)}) collective-permute-start(f32[16,32,32]{2,1,0:T(8,128)S(1)} %get-tuple-element.41), channel_id=1, source_target_pairs={{1,0},{2,1},{3,2},{4,3},{5,4},{6,5},{7,6},{8,7},{9,8},{10,9},{11,1... | collective-permute-start | bytes 196616 | tf_op jit(solution)/shard_map/ppermute | solution.py:20
  621.5 10.4 %collective-permute-start.8 = (f32[16,32,32]{2,1,0:T(8,128)S(1)}, f32[16,32,32]{2,1,0:T(8,128)S(1)}, u32[]{:S(2)}, u32[]{:S(2)}) collective-permute-start(f32[16,32,32]{2,1,0:T(8,128)S(1)} %get-tuple-element.34), channel_id=1, source_target_pairs={{1,0},{2,1},{3,2},{4,3},{5,4},{6,5},{7,6},{8,7},{9,8},{10,9},{11,1... | collective-permute-start | bytes 196616 | tf_op jit(solution)/shard_map/ppermute | solution.py:20
  623.9 9.9 %collective-permute-start.9 = (f32[16,32,32]{2,1,0:T(8,128)S(1)}, f32[16,32,32]{2,1,0:T(8,128)S(1)}, u32[]{:S(2)}, u32[]{:S(2)}) collective-permute-start(f32[16,32,32]{2,1,0:T(8,128)S(1)} %get-tuple-element.35), channel_id=1, source_target_pairs={{0,1},{1,2},{2,3},{3,4},{4,5},{5,6},{6,7},{7,8},{8,9},{9,10},{10,1... | collective-permute-start | bytes 196616 | tf_op jit(solution)/shard_map/ppermute | solution.py:20
  638.3 10.8 %collective-permute-start.10 = (f32[16,32,32]{2,1,0:T(8,128)S(1)}, f32[16,32,32]{2,1,0:T(8,128)S(1)}, u32[]{:S(2)}, u32[]{:S(2)}) collective-permute-start(f32[16,32,32]{2,1,0:T(8,128)S(1)} %get-tuple-element.26), channel_id=1, source_target_pairs={{1,0},{2,1},{3,2},{4,3},{5,4},{6,5},{7,6},{8,7},{9,8},{10,9},{11,1... | collective-permute-start | bytes 196616 | tf_op jit(solution)/shard_map/ppermute | solution.py:20
  641.0 10.4 %collective-permute-start.11 = (f32[16,32,32]{2,1,0:T(8,128)S(1)}, f32[16,32,32]{2,1,0:T(8,128)S(1)}, u32[]{:S(2)}, u32[]{:S(2)}) collective-permute-start(f32[16,32,32]{2,1,0:T(8,128)S(1)} %get-tuple-element.27), channel_id=1, source_target_pairs={{0,1},{1,2},{2,3},{3,4},{4,5},{5,6},{6,7},{7,8},{8,9},{9,10},{10,1... | collective-permute-start | bytes 196616 | tf_op jit(solution)/shard_map/ppermute | solution.py:20
  657.7 10.4 %collective-permute-start.13 = (f32[16,32,32]{2,1,0:T(8,128)S(1)}, f32[16,32,32]{2,1,0:T(8,128)S(1)}, u32[]{:S(2)}, u32[]{:S(2)}) collective-permute-start(f32[16,32,32]{2,1,0:T(8,128)S(1)} %get-tuple-element.16), channel_id=1, source_target_pairs={{0,1},{1,2},{2,3},{3,4},{4,5},{5,6},{6,7},{7,8},{8,9},{9,10},{10,1... | collective-permute-start | bytes 196616 | tf_op jit(solution)/shard_map/ppermute | solution.py:20
  664.2 10.4 %collective-permute-start.12 = (f32[16,32,32]{2,1,0:T(8,128)S(1)}, f32[16,32,32]{2,1,0:T(8,128)S(1)}, u32[]{:S(2)}, u32[]{:S(2)}) collective-permute-start(f32[16,32,32]{2,1,0:T(8,128)S(1)} %get-tuple-element.17), channel_id=1, source_target_pairs={{1,0},{2,1},{3,2},{4,3},{5,4},{6,5},{7,6},{8,7},{9,8},{10,9},{11,1... | collective-permute-start | bytes 196616 | tf_op jit(solution)/shard_map/ppermute | solution.py:20
  667.2 8.2 %slice-start = ((s8[6291456]{0:T(1024)(128)(4,1)}), s8[4194304]{0:T(1024)(128)(4,1)S(1)}, s32[]{:S(2)}) async-start(s8[6291456]{0:T(1024)(128)(4,1)} %bitcast.255), calls=%async_computation.9 | async-start | bytes 8388608
  668.2 7.2 %slice-start.1 = ((s8[6291456]{0:T(1024)(128)(4,1)}), s8[2097152]{0:T(1024)(128)(4,1)S(1)}, s32[]{:S(2)}) async-start(s8[6291456]{0:T(1024)(128)(4,1)} %bitcast.255), calls=%async_computation.10 | async-start | bytes 4194304
  (9 other events, 28.8 us)
where the time goes:
time: 686 us; the launch traced here: 679 us
  local copies, waits for them, and re-layouts  227 us (33%)
  waiting for transfers between devices  182 us (27%)
  matrix products  124 us (18%)
  starting transfers between devices  113 us (16%)
  other arithmetic  30.8 us (4%)
    gather x1, local copies, waits for them, and re-layouts, cut_patches(): padded[index_first[:, :, None, None], index_second[:, None, :, None], ind...  151 us
    dot_general x20, matrix products, transform_along(): jnp.einsum(EINSUM_FORMS[axis_number], values_in, matrix, precision=HIGHES...  112 us
    ppermute x10, starting transfers between devices, from_behind(): lax.ppermute(value, axis, [(source, source + steps) for source in range(i...  41.7 us
    ppermute x10, waiting for transfers between devices, from_behind(): lax.ppermute(value, axis, [(source, source + steps) for source in range(i...  25.6 us
    all_to_all x1, waiting for transfers between devices, local(): lax.all_to_all(spectrum[1], ('px', 'py'), split_axis=1, concat_axis=0, ti...  23.2 us
    all_to_all x1, waiting for transfers between devices, local(): lax.all_to_all(spectrum[0], ('px', 'py'), split_axis=0, concat_axis=1, ti...  22.1 us
    all_to_all x1, waiting for transfers between devices, local(): lax.all_to_all(real_part, 'py', split_axis=0, concat_axis=1, tiled=True)  21.4 us
    all_to_all x1, waiting for transfers between devices, local(): lax.all_to_all(spectrum[0], 'py', split_axis=1, concat_axis=0, tiled=True)  20.7 us
  transfers between devices with their start and end apart: 23, of which 21 were waited for; matrix products, arithmetic and copies ran while one was open for 13% of the time, Pallas kernels for 0%

commit v1 on v0

v1 whole, which is shorter than its diff:
```python
import numpy as np
import jax
import jax.numpy as jnp
from jax import lax
from jax.experimental import pallas as pl
from jax.experimental.pallas import tpu as pltpu
from jax.sharding import PartitionSpec as P

NR = 384
REG = 8
REF = 4
SWEEPS = 4
CELLS = REG * REF
PX = 8
PY = 16
DEV = PX * PY
MODES = NR // DEV
XB = NR // PX
YB = NR // PY
XE = XB + 2
YE = YB + 4
PLANE = 1408
EDGE = 4
LANES = (CELLS + 2 * EDGE) * CELLS
RELAX = 6.0 / 7.0
HIGH = lax.Precision.HIGH


def fourier_basis():
    n = np.arange(NR)
    k = np.concatenate([[0, NR // 2], np.repeat(np.arange(1, NR // 2), 2)])
    phase = 2.0 * np.pi * ((n[:, None] * k[None, :]) % NR) / NR
    odd = np.zeros(NR, bool)
    odd[3::2] = True
    q = np.where(odd[None, :], np.sin(phase), np.cos(phase)) * np.sqrt(2.0 / NR)
    q[:, :2] *= np.sqrt(0.5)
    eig = -4.0 * np.sin(np.pi * k / NR) ** 2
    return q, eig


def line_weights(first, last, offset):
    cells = np.arange(first, last)
    marks = 2 * cells + 1 - REF
    low = marks // (2 * REF)
    frac = (marks - 2 * REF * low) / (2.0 * REF)
    table = np.zeros((len(cells), 16))
    rows = np.arange(len(cells))
    table[rows, low + offset] += 1.0 - frac
    table[rows, low + 1 + offset] += frac
    return table


def interpolation_tables():
    wi = line_weights(0, CELLS, 1)[:, :10]
    wlow = line_weights(-1, 0, 1)[:, :10]
    whigh = line_weights(CELLS, CELLS + 1, 1)[:, :10]
    wj = line_weights(-EDGE, CELLS + EDGE, 2)[:, :12]
    jlow = line_weights(-EDGE - 1, -EDGE, 2)[0, :12]
    jhigh = line_weights(CELLS + EDGE, CELLS + EDGE + 1, 2)[0, :12]
    inner = np.einsum("jb,kc->bcjk", wj, wi)
    edge = np.zeros_like(inner)
    edge[:, :, :, 0] += np.einsum("jb,c->bcj", wj, wlow[0])
    edge[:, :, :, -1] += np.einsum("jb,c->bcj", wj, whigh[0])
    edge[:, :, 0, :] += np.einsum("b,kc->bck", jlow, wi)
    edge[:, :, -1, :] += np.einsum("b,kc->bck", jhigh, wi)
    cols = np.zeros((128, 2 * LANES))
    cols[:120, :LANES] = inner.reshape(120, LANES)
    cols[:120, LANES:] = edge.reshape(120, LANES)
    rows = np.zeros((40, 16))
    rows[:32, :10] = wi
    rows[32, :10] = wlow[0]
    rows[33, :10] = whigh[0]
    return rows, cols


def from_behind(value, axis, steps):
    count = lax.axis_size(axis)
    initial, last = (max(0, -steps), min(count, count - steps))
    return lax.ppermute(value, axis, [(source, source + steps) for source in range(initial, last)])


def split3(x):
    hi = x.astype(jnp.bfloat16)
    rest = x - hi.astype(jnp.float32)
    mid = rest.astype(jnp.bfloat16)
    low = (rest - mid.astype(jnp.float32)).astype(jnp.bfloat16)
    return hi, mid, low


def dot(a, b):
    return jnp.dot(a, b, preferred_element_type=jnp.float32)


def cut_kernel(start_ref, s_ref, g_ref, out_ref, p_ref):
    cells = lax.dot_general(
        s_ref[...], g_ref[...], (((0,), (0,)), ((), ())),
        precision=lax.Precision.HIGHEST, preferred_element_type=jnp.float32)
    for y in range(YE):
        p_ref[y, :XE, :] = cells[y * XE:(y + 1) * XE, :]
    lane = lax.broadcasted_iota(jnp.int32, (16, 128), 1)
    for t in range(PY):
        acc = jnp.zeros((16, 128), jnp.float32)
        for b in range(12):
            first = pl.multiple_of(start_ref[0, t], 8)
            tile = p_ref[start_ref[1, t] + b, pl.ds(first, 16), (t // 8) * 128:(t // 8 + 1) * 128]
            shift = (b * 10 - (t % 8) * 16) % 128
            if shift:
                tile = pltpu.roll(tile, shift, 1)
            acc = jnp.where((lane >= b * 10) & (lane < b * 10 + 10), tile, acc)
        out_ref[t * 16:(t + 1) * 16, :] = acc


def cut_patches(spectrum, columns, starts):
    return pl.pallas_call(
        cut_kernel,
        out_shape=jax.ShapeDtypeStruct((PY * 16, 128), jnp.float32),
        in_specs=[pl.BlockSpec(memory_space=pltpu.SMEM),
                  pl.BlockSpec(memory_space=pltpu.VMEM),
                  pl.BlockSpec(memory_space=pltpu.VMEM)],
        out_specs=pl.BlockSpec(memory_space=pltpu.VMEM),
        scratch_shapes=[pltpu.VMEM((YE, 56, 256), jnp.float32)],
        compiler_params=pltpu.CompilerParams(vmem_limit_bytes=48 << 20),
        name="cut_patches",
    )(starts, spectrum, columns)


def relax_kernel(flag_ref, patch_ref, rows_ref, cols_ref, dens_ref, low_ref, high_ref, vel_ref,
                 pot_ref, out_ref, grid_ref):
    step = pl.program_id(0)

    @pl.when(step == 0)
    def _():
        rows = rows_ref[...]
        expanded = jnp.zeros((640, 128), jnp.float32)
        ordered = jnp.concatenate(
            [patch_ref[pl.ds(pl.multiple_of(flag_ref[j, 5] * 16, 16), 16), :] for j in range(PY)], axis=0)
        for part in split3(ordered):
            expanded += dot(rows, part)
        parts = split3(expanded)
        for n in range(0, 2 * LANES, 256):
            table = cols_ref[:, n:n + 256]
            acc = dot(parts[0], table) + dot(parts[1], table) + dot(parts[2], table)
            grid_ref[:, n:n + 256] = acc

    base = pl.multiple_of(step * 40, 8)
    v0 = grid_ref[pl.ds(base, 32), :LANES]
    edge = grid_ref[pl.ds(base, 32), LANES:]
    faces = grid_ref[pl.ds(base + 32, 8), :LANES]
    lane = lax.broadcasted_iota(jnp.int32, (32, LANES), 1)
    row = lax.broadcasted_iota(jnp.int32, (32, LANES), 0)
    third = lane % CELLS
    low_face = jnp.broadcast_to(faces[0:1], (32, LANES))
    high_face = jnp.broadcast_to(faces[1:2], (32, LANES))
    first_row = row == 0
    last_row = row == CELLS - 1
    zero = jnp.zeros((32, LANES), jnp.float32)
    density = jnp.concatenate([low_ref[0], dens_ref[0], high_ref[0]], axis=1)
    fixed = edge + jnp.where(first_row, low_face, zero) + jnp.where(last_row, high_face, zero)
    c = RELAX / 6.0
    fixed = c * (fixed - density * (1.0 / (REF * REF)))
    use_low = flag_ref[step, 0] > 0
    use_high = flag_ref[step, 1] > 0
    same_low = flag_ref[step, 2] > 0
    same_high = flag_ref[step, 3] > 0
    live = flag_ref[step, 4] > 0
    in_low = lane < EDGE * CELLS
    in_high = lane >= (EDGE + CELLS) * CELLS
    held = (in_low & jnp.logical_not(use_low)) | (in_high & jnp.logical_not(use_high))
    frozen_next = (lane >= (EDGE - 1) * CELLS) & in_low & jnp.logical_not(same_low)
    frozen_prev = in_high & (lane < (EDGE + CELLS + 1) * CELLS) & jnp.logical_not(same_high)

    def beside(v):
        prev_third = jnp.where(third == 0, zero, pltpu.roll(v, 1, 1))
        next_third = jnp.where(third == CELLS - 1, zero, pltpu.roll(v, LANES - 1, 1))
        prev_first = jnp.where(first_row, zero, pltpu.roll(v, 1, 0))
        next_first = jnp.where(last_row, zero, pltpu.roll(v, CELLS - 1, 0))
        prev_second = pltpu.roll(v, CELLS, 1)
        next_second = pltpu.roll(v, LANES - CELLS, 1)
        return prev_first, next_first, prev_second, next_second, prev_third, next_third

    start_prev = pltpu.roll(v0, CELLS, 1)
    start_next = pltpu.roll(v0, LANES - CELLS, 1)
    outer_low = lane < CELLS
    outer_high = lane >= LANES - CELLS
    v = v0
    for _ in range(SWEEPS):
        pf, nf, ps, ns, pt, nt = beside(v)
        ps = jnp.where(outer_low, zero, jnp.where(frozen_prev, start_prev, ps))
        ns = jnp.where(outer_high, zero, jnp.where(frozen_next, start_next, ns))
        new = (1.0 - RELAX) * v + c * (pf + nf + ps + ns + pt + nt) + fixed
        v = jnp.where(held, v, new)
    pf, nf, ps, ns, pt, nt = beside(v)
    own = slice(EDGE * CELLS, (EDGE + CELLS) * CELLS)
    scale = REF / 2.0
    slope_first = (nf + jnp.where(last_row, high_face, zero)) - (pf + jnp.where(first_row, low_face, zero))
    slope_second = ns - ps
    slope_third = (nt + jnp.where(third == CELLS - 1, edge, zero)) - (pt + jnp.where(third == 0, edge, zero))
    pot_ref[0] = jnp.where(live, v[:, own], 0.0)
    for q, slope in enumerate((slope_first, slope_second, slope_third)):
        out_ref[q, 0] = jnp.where(live, vel_ref[q, 0] - slope[:, own] * scale, 0.0)


def relax(flags, patch, density, low, high, velocity):
    slots = density.shape[0]
    rows, cols = interpolation_tables()
    block_rows = jnp.asarray(np.kron(np.eye(slots), rows), jnp.bfloat16)
    table = jnp.asarray(cols, jnp.bfloat16)
    whole = lambda shape: pl.BlockSpec(shape, lambda s, f: (0,) * len(shape), pipeline_mode=pl.Buffered(1))
    return pl.pallas_call(
        relax_kernel,
        grid_spec=pltpu.PrefetchScalarGridSpec(
            num_scalar_prefetch=1,
            grid=(slots,),
            in_specs=[
                whole((slots * 16, 128)),
                whole((slots * 40, slots * 16)),
                whole((128, 2 * LANES)),
                pl.BlockSpec((1, CELLS, CELLS * CELLS), lambda s, f: (s, 0, 0)),
                pl.BlockSpec((1, CELLS, EDGE * CELLS), lambda s, f: (s, 0, 0)),
                pl.BlockSpec((1, CELLS, EDGE * CELLS), lambda s, f: (s, 0, 0)),
                pl.BlockSpec((3, 1, CELLS, CELLS * CELLS), lambda s, f: (0, s, 0, 0)),
            ],
            out_specs=[
                pl.BlockSpec((1, CELLS, CELLS * CELLS), lambda s, f: (s, 0, 0)),
                pl.BlockSpec((3, 1, CELLS, CELLS * CELLS), lambda s, f: (0, s, 0, 0)),
            ],
            scratch_shapes=[pltpu.VMEM((slots * 40, 2 * LANES), jnp.float32)],
        ),
        out_shape=[
            jax.ShapeDtypeStruct(density.shape, jnp.float32),
            jax.ShapeDtypeStruct(velocity.shape, jnp.float32),
        ],
        compiler_params=pltpu.CompilerParams(vmem_limit_bytes=48 << 20),
        name="relax_and_kick",
    )(flags, patch, block_rows, table, density, low, high, velocity)


def local(root_density, subgrid_density, velocity, slot_anchor, slot_count, neighbour):
    place_first = lax.axis_index("px")
    place_second = lax.axis_index("py")
    device = place_first * PY + place_second
    slots = subgrid_density.shape[0]
    q, eig = fourier_basis()
    basis = jnp.asarray(q, jnp.float32)
    eigen = jnp.asarray(eig, jnp.float32)
    low = from_behind(subgrid_density[:, :, -EDGE * CELLS:], "py", 1)
    high = from_behind(subgrid_density[:, :, :EDGE * CELLS], "py", -1)

    packed = jnp.einsum("xyz,zmt->tmyx", root_density, basis.reshape(NR, MODES, DEV), precision=HIGH)
    got = lax.all_to_all(packed.reshape(DEV, MODES * YB * XB), ("px", "py"), 0, 0, tiled=True)
    planes = got.reshape(PX, PY, MODES, YB, XB).transpose(2, 3, 1, 0, 4).reshape(MODES, NR, NR)
    n = np.arange(NR)
    order = (n % PY) * YB + n // PY
    wide = ((np.arange(YE)[:, None] - 2 + np.arange(PY)[None, :] * YB) % NR).reshape(-1)
    wide_x = ((np.arange(PX)[:, None] * XB + np.arange(XE)[None, :] - 1) % NR).reshape(-1)
    z = jnp.einsum("myx,xk->myk", planes, basis, precision=HIGH)
    z = jnp.einsum("myk,yl->mlk", z, jnp.asarray(q[order], jnp.float32), precision=HIGH)
    own_eig = eigen[jnp.arange(MODES) * DEV + device]
    total = own_eig[:, None, None] + eigen[None, :, None] + eigen[None, None, :]
    is_zero = total == 0.0
    z = z * jnp.where(is_zero, 0.0, 1.0 / jnp.where(is_zero, -1.0, total))
    z = jnp.einsum("mlk,yl->myk", z, jnp.asarray(q[wide], jnp.float32), precision=HIGH)
    z = jnp.einsum("myk,xk->myx", z, jnp.asarray(q[wide_x], jnp.float32), precision=HIGH)
    z = z.reshape(MODES, YE, PY, PX, XE).transpose(3, 2, 0, 1, 4).reshape(DEV, MODES, YE * XE)
    z = jnp.pad(z, ((0, 0), (0, 0), (0, PLANE - YE * XE))).reshape(DEV, MODES * PLANE)
    back = lax.all_to_all(z, ("px", "py"), 0, 0, tiled=True)
    spectrum = back.reshape(DEV, MODES, PLANE).transpose(1, 0, 2).reshape(NR, PLANE)

    targets = jnp.arange(PY, dtype=jnp.int32)
    wanted = (place_first * PY + targets) * slots + (place_second - targets) % PY
    anchors = slot_anchor[:, wanted]
    third = (anchors[2][:, None] - 1 + jnp.arange(16, dtype=jnp.int32)[None, :]) % NR
    columns = basis[third.reshape(-1)].T
    start_first = jnp.clip(anchors[0] - place_first * XB, 0, XB - REG)
    start_second = jnp.clip(anchors[1] - place_second * YB, 0, YB - REG)
    sending = cut_patches(spectrum, columns, jnp.stack([start_first, start_second]))
    arrived = lax.all_to_all(sending, "py", 0, 0, tiled=True)
    positions = jnp.arange(slots, dtype=jnp.int32)

    block = jnp.einsum("nc,zn->cz", spectrum, basis, precision=HIGH)
    block = block[:YE * XE].reshape(YE, XE, NR)[2:-2, 1:-1]
    coarse_potential = block.transpose(1, 0, 2)

    first_slot = device * slots
    padded = jnp.pad(neighbour, ((0, 0), (slots, slots)), constant_values=-1)
    nearby = lax.dynamic_slice_in_dim(neighbour, first_slot, slots, 1)
    below = lax.dynamic_slice_in_dim(padded, first_slot, slots, 1)
    above = lax.dynamic_slice_in_dim(padded, first_slot + 2 * slots, slots, 1)
    flags = jnp.stack([
        nearby[0] >= 0, nearby[1] >= 0, below[1] >= 0, above[0] >= 0,
        positions < slot_count[device], (place_second + positions) % PY,
    ], axis=1).astype(jnp.int32)
    subgrid_potential, kicked = relax(flags, arrived, subgrid_density, low, high, velocity)
    return coarse_potential, subgrid_potential, kicked


def solution(mesh):
    return jax.shard_map(
        local,
        mesh=mesh,
        in_specs=(
            P("px", "py", None),
            P(("px", "py"), None, None),
            P(None, ("px", "py"), None, None),
            P(),
            P(),
            P(),
        ),
        out_specs=(
            P("px", "py", None),
            P(("px", "py"), None, None),
            P(None, ("px", "py"), None, None),
        ),
        check_vma=False,
    )
```

time: 686 us -> 203 us (0.30)
  the two profiles are of different devices: /device:TPU:96 before, /device:TPU:1 now
where the time goes in v1:
time: 203 us; the launch traced here: 200 us
  local copies, waits for them, and re-layouts  70 us (34%)
  waiting for transfers between devices  40.3 us (20%)
  Pallas kernels  31.1 us (15%)
  starting transfers between devices  26.2 us (13%)
  matrix products  16.8 us (8%)
  other arithmetic  14 us (7%)
    pallas_call x1, Pallas kernels, relax(): pl.pallas_call(relax_kernel, grid_spec=pltpu.PrefetchScalarGridSpec(num_s...  26.7 us
    all_to_all x1, waiting for transfers between devices, local(): lax.all_to_all(packed.reshape(DEV, MODES * YB * XB), ('px', 'py'), 0, 0,...  25.2 us
    all_to_all x1, waiting for transfers between devices, local(): back = lax.all_to_all(z, ('px', 'py'), 0, 0, tiled=True)  15.1 us
    all_to_all x1, starting transfers between devices, local(): lax.all_to_all(packed.reshape(DEV, MODES * YB * XB), ('px', 'py'), 0, 0,...  11.8 us
    reshape x2, local copies, waits for them, and re-layouts, local(): z.reshape(MODES, YE, PY, PX, XE).transpose(3, 2, 0, 1, 4)  9.96 us
    reshape x2, local copies, waits for them, and re-layouts, local(): got.reshape(PX, PY, MODES, YB, XB).transpose(2, 3, 1, 0, 4)  8.96 us
    transpose x1, local copies, waits for them, and re-layouts, local(): z.reshape(MODES, YE, PY, PX, XE).transpose(3, 2, 0, 1, 4)  8.5 us
    all_to_all x2, local copies, waits for them, and re-layouts, local(): back = lax.all_to_all(z, ('px', 'py'), 0, 0, tiled=True)  7.79 us
  transfers between devices with their start and end apart: 5, of which 2 were waited for; matrix products, arithmetic and copies ran while one was open for 19% of the time, Pallas kernels for 2%

profile of v1, /device:TPU:1, one launch (start us, length us, event | category | flops | bytes accessed | tf_op | source)
XLA Modules:
  0.0 199.7 jit_solution(14108958923424628140)
XLA Ops:
  0.6 3.5 %fusion.11 = f32[3,128,48,24]{1,2,3,0:T(8,128)S(1)} fusion(f32[384,3,128,1]{2,0,3,1:T(8,128)} %constant.108, f32[48,24,384]{2,1,0:T(8,128)} %param.13), kind=kOutput, calls=%fused_computation.15 | convolution fusion | flops 1019215872 | bytes 4128768 | tf_op jit(solution)/shard_map/xyz,zmt->tmyx/dot_general | solution.py:249
  4.1 3.3 %copy.59 = f32[128,1,3456]{2,1,0:T(1,128)} copy(f32[128,1,3456]{0,2,1:T(8,128)S(1)} %bitcast.68) | data formatting | bytes 3538944 | tf_op jit(solution)/shard_map/all_to_all | solution.py:250
  7.4 11.8 %all-to-all-start = ((f32[128,1,3456]{2,1,0:T(1,128)}), f32[128,1,3456]{2,1,0:T(1,128)S(1)}, u32[]{:S(2)}, u32[]{:S(2)}) async-start(f32[128,1,3456]{2,1,0:T(1,128)} %copy.59), calls=%async_computation | async-start | bytes 3538944 | tf_op jit(solution)/shard_map/all_to_all | solution.py:250
  19.3 0.6 gather_fusion
  20.0 25.2 %all-to-all-done = f32[128,1,3456]{2,1,0:T(1,128)S(1)} async-done(((f32[128,1,3456]{2,1,0:T(1,128)}), f32[128,1,3456]{2,1,0:T(1,128)S(1)}, u32[]{:S(2)}, u32[]{:S(2)}) %all-to-all-start) | async-done | bytes 1769504 | tf_op jit(solution)/shard_map/all_to_all | solution.py:250
  45.2 5.9 %reduce = f32[128,3456]{1,0:T(8,128)} reduce(f32[128,1,3456]{2,1,0:T(1,128)S(1)} %all-to-all-done, f32[]{:T(128)} %constant.113), dimensions={1}, to_apply=%all_to_all.20.reduce_sub_computation | reduce | bytes 3538948 | tf_op jit(solution)/shard_map/all_to_all | solution.py:250
  51.0 4.7 %reshape.333 = f32[8,16,3,24,48]{4,3,2,1,0:T(8,128)} reshape(f32[128,3456]{1,0:T(8,128)} %reduce) | data formatting | bytes 3538944 | tf_op jit(solution)/shard_map/reshape | solution.py:251
  55.7 7.2 %copy.60 = f32[3,24,16,8,48]{4,3,2,1,0:T(8,128)} copy(f32[3,24,16,8,48]{4,1,0,2,3:T(8,128)} %bitcast.65) | data formatting | bytes 3538944 | tf_op jit(solution)/shard_map/transpose | solution.py:251
  62.9 4.3 %reshape.334 = f32[3,384,384]{2,1,0:T(8,128)S(1)} reshape(f32[3,24,16,8,48]{4,3,2,1,0:T(8,128)} %copy.60) | data formatting | bytes 3538944 | tf_op jit(solution)/shard_map/reshape | solution.py:251
  67.2 1.7 fusion.39
  69.0 1.8 fusion.40
  70.8 2.2 %fusion.6 = f32[3,384,448]{1,2,0:T(8,128)S(1)} fusion(f32[448,384,1]{1,0,2:T(8,128)S(1)} %copy-done.12, f32[3,384,384]{2,1,0:T(8,128)S(1)} %fusion.40, f32[384]{0:T(512)S(1)} %copy-done.3, f32[3,384]{1,0:T(4,128)S(1)} %broadcast_add_fusion), kind=kOutput, calls=%fused_computation.11 | convolution fusion | flops 1191739392 | bytes 4528128 | tf_op jit(solution)/shard_map/mlk,yl->myk/dot_general | solution.py:262
  73.0 2.3 %fusion.2 = f32[3,448,400]{2,1,0:T(8,128)S(1)} fusion(f32[400,384,1]{1,0,2:T(8,128)S(1)} %copy-done.5, f32[3,384,448]{1,2,0:T(8,128)S(1)} %fusion.6), kind=kOutput, calls=%fused_computation.7 | convolution fusion | flops 1238630400 | bytes 4829184 | tf_op jit(solution)/shard_map/myk,xk->myx/dot_general | solution.py:263
  75.3 4.1 %reshape.335 = f32[3,28,16,8,50]{4,3,2,1,0:T(8,128)} reshape(f32[3,448,400]{2,1,0:T(8,128)S(1)} %fusion.2) | data formatting | bytes 4300800 | tf_op jit(solution)/shard_map/reshape | solution.py:264
  79.5 8.5 %copy.64 = f32[8,16,3,28,50]{4,3,1,0,2:T(8,128)} copy(f32[8,16,3,28,50]{4,0,1,3,2:T(8,128)} %bitcast.64) | data formatting | bytes 4300800 | tf_op jit(solution)/shard_map/transpose | solution.py:264
  88.0 5.8 %reshape.336 = f32[128,3,1400]{2,0,1:T(8,128)S(1)} reshape(f32[8,16,3,28,50]{4,3,1,0,2:T(8,128)} %copy.64) | data formatting | bytes 4300800 | tf_op jit(solution)/shard_map/reshape | solution.py:264
  93.8 1.9 copy.82
  95.7 1.7 pad.8.clone
  97.5 4.0 %copy.66 = f32[128,1,4224]{2,1,0:T(1,128)} copy(f32[128,1,4224]{0,2,1:T(8,128)S(1)} %bitcast.66) | data formatting | bytes 4325376 | tf_op jit(solution)/shard_map/all_to_all | solution.py:266
  101.4 5.0 %all-to-all-start.1 = ((f32[128,1,4224]{2,1,0:T(1,128)}), f32[128,1,4224]{2,1,0:T(1,128)S(1)}, u32[]{:S(2)}, u32[]{:S(2)}) async-start(f32[128,1,4224]{2,1,0:T(1,128)} %copy.66), calls=%async_computation.1 | async-start | bytes 4325376 | tf_op jit(solution)/shard_map/all_to_all | solution.py:266
  106.5 1.9 fusion.38
  108.4 3.6 %collective-permute-start = (f32[16,32,128]{2,1,0:T(8,128)}, f32[16,32,128]{2,1,0:T(8,128)S(1)}, u32[]{:S(2)}, u32[]{:S(2)}) collective-permute-start(f32[16,32,128]{2,1,0:T(8,128)} %get-tuple-element.8), channel_id=1, source_target_pairs={{0,1},{1,2},{2,3},{3,4},{4,5},{5,6},{6,7},{7,8},{8,9},{9,10},{10,1... | collective-permute-start | bytes 786440 | tf_op jit(solution)/shard_map/ppermute | solution.py:79
  111.9 1.5 collective-permute-start.1
  113.4 0.1 pad_dynamic-slice_fusion
  113.5 0.1 copy.68
  113.6 0.1 copy.69
  113.8 0.1 copy.71
  113.9 1.3 copy.72
  115.2 0.1 fusion.22
  115.3 1.8 gather_fusion.1
  117.4 1.7 gather_fusion.2
  119.2 1.2 copy.76
  120.3 0.6 dynamic_slice.15
  120.9 0.7 fusion.29
  121.7 15.1 %all-to-all-done.1 = f32[128,1,4224]{2,1,0:T(1,128)S(1)} async-done(((f32[128,1,4224]{2,1,0:T(1,128)}), f32[128,1,4224]{2,1,0:T(1,128)S(1)}, u32[]{:S(2)}, u32[]{:S(2)}) %all-to-all-start.1) | async-done | bytes 2162720 | tf_op jit(solution)/shard_map/all_to_all | solution.py:266
  136.8 7.2 %reduce.1 = f32[128,4224]{1,0:T(8,128)} reduce(f32[128,1,4224]{2,1,0:T(1,128)S(1)} %all-to-all-done.1, f32[]{:T(128)} %constant.113), dimensions={1}, to_apply=%all_to_all.22.reduce_sub_computation | reduce | bytes 4325380 | tf_op jit(solution)/shard_map/all_to_all | solution.py:266
  143.9 2.8 %reshape.340 = f32[384,1408]{1,0:T(8,128)} reshape(f32[128,4224]{1,0:T(8,128)} %reduce.1) | data formatting | bytes 4325376 | tf_op jit(solution)/shard_map/nc,zn->cz/dot_general | solution.py:280
  146.8 3.8 %copy.74 = f32[128,1,4224]{0,2,1:T(8,128)} copy(f32[128,1,4224]{2,1,0:T(1,128)S(1)} %all-to-all-done.1) | data formatting | bytes 4325376 | tf_op jit(solution)/shard_map/all_to_all | solution.py:266
  150.6 2.2 %copy.75 = f32[3,128,1408]{2,1,0:T(8,128)S(1)} copy(f32[3,128,1408]{1,2,0:T(8,128)} %bitcast.67) | data formatting | bytes 4325376 | tf_op jit(solution)/shard_map/transpose | solution.py:267
  152.8 4.3 %cut_patches.1 = f32[256,128]{1,0:T(8,128)} custom-call(s32[2,16]{1,0:T(2,128)S(1)} %pad_add_fusion.start_ref, f32[384,1408]{1,0:T(8,128)S(1)} %bitcast.61, f32[384,256]{1,0:T(8,128)S(1)} %bitcast.62), custom_call_target="tpu_custom_call" | custom-call | tf_op jit(solution)/shard_map/cut_patches/pallas_call | solution.py:114
  157.2 4.4 %all-to-all-start.2 = ((f32[16,16,128]{2,1,0:T(8,128)}), f32[16,16,128]{2,1,0:T(8,128)S(1)}, u32[]{:S(2)}, u32[]{:S(2)}) async-start(f32[16,16,128]{2,1,0:T(8,128)} %bitcast.28), calls=%async_computation.2 | async-start | bytes 262144 | tf_op jit(solution)/shard_map/all_to_all | solution.py:277
  161.6 5.3 %fusion = f32[1400,384]{1,0:T(8,128)S(1)} fusion(f32[384,384]{1,0:T(8,128)S(1)} %copy-done.6, f32[384,1408]{1,0:T(8,128)} %reshape.340), kind=kOutput, calls=%fused_computation.5 | convolution fusion | flops 1238630400 | bytes 4902912 | tf_op jit(solution)/shard_map/nc,zn->cz/dot_general | solution.py:280
  166.8 1.7 reshape.339
  168.5 1.7 slice.52
  170.3 1.7 copy.88
  172.0 0.5 copy-done.1
  172.5 0.1 copy-done.2
  172.7 26.7 %relax_and_kick.1 = (f32[16,32,1024]{2,1,0:T(8,128)}, f32[3,16,32,1024]{3,2,1,0:T(8,128)}) custom-call(s32[16,6]{1,0:T(8,128)S(1)} %stack.4.flag_ref, f32[256,128]{1,0:T(8,128)S(1)} %bitcast.63, bf16[640,256]{1,0:T(8,128)(2,1)S(1)} %copy-done.2, bf16[128,2560]{1,0:T(8,128)(2,1)S(1)} %copy-done.1, f32[16,32,1024]{2,1,0:T(8,128)S(1)} %copy-done, ...), custom_call_target="tpu_custom_call" | custom-call | tf_op jit(solution)/shard_map/relax_and_kick/pallas_call | solution.py:209
  (43 shorter events, 0.6 us)
Async XLA Ops:
  7.4 11.9 %copy-start.3 = (f32[384]{0:T(512)S(1)}, f32[384]{0:T(512)}, u32[]{:S(2)}) copy-start(f32[384]{0:T(512)} %constant.92.clone) | copy-start | bytes 4612
  7.4 37.8 %all-to-all-start = ((f32[128,1,3456]{2,1,0:T(1,128)}), f32[128,1,3456]{2,1,0:T(1,128)S(1)}, u32[]{:S(2)}, u32[]{:S(2)}) async-start(f32[128,1,3456]{2,1,0:T(1,128)} %copy.59), calls=%async_computation | async-start | bytes 3538944 | tf_op jit(solution)/shard_map/all_to_all | solution.py:250
  62.9 4.3 %copy-start.8 = (f32[384,384,1]{1,0,2:T(8,128)S(1)}, f32[384,384,1]{1,0,2:T(8,128)}, u32[]{:S(2)}) copy-start(f32[384,384,1]{1,0,2:T(8,128)} %constant.109) | copy-start | bytes 1769476
  67.2 1.7 copy-start.7
  69.0 1.9 copy-start.12
  70.8 2.2 %copy-start.5 = (f32[400,384,1]{1,0,2:T(8,128)S(1)}, f32[400,384,1]{1,0,2:T(8,128)}, u32[]{:S(2)}) copy-start(f32[400,384,1]{1,0,2:T(8,128)} %constant.112) | copy-start | bytes 1843204
  101.4 12.0 %copy-start.10 = (s32[2,2048]{1,0:T(2,128)S(1)}, s32[2,2048]{1,0:T(2,128)}, u32[]{:S(2)}) copy-start(s32[2,2048]{1,0:T(2,128)} %param.18) | copy-start | bytes 49156
  101.4 12.4 %copy-start.9 = (s32[3,2048]{1,0:T(4,128)S(1)}, s32[3,2048]{1,0:T(4,128)}, u32[]{:S(2)}) copy-start(s32[3,2048]{1,0:T(4,128)} %param.16) | copy-start | bytes 73732
  101.4 35.3 %all-to-all-start.1 = ((f32[128,1,4224]{2,1,0:T(1,128)}), f32[128,1,4224]{2,1,0:T(1,128)S(1)}, u32[]{:S(2)}, u32[]{:S(2)}) async-start(f32[128,1,4224]{2,1,0:T(1,128)} %copy.66), calls=%async_computation.1 | async-start | bytes 4325376 | tf_op jit(solution)/shard_map/all_to_all | solution.py:266
  106.5 11.0 %copy-start.4 = (f32[384,384]{1,0:T(8,128)S(1)}, f32[384,384]{1,0:T(8,128)}, u32[]{:S(2)}) copy-start(f32[384,384]{1,0:T(8,128)} %constant.91.clone) | copy-start | bytes 1769476
  108.4 63.6 %collective-permute-start = (f32[16,32,128]{2,1,0:T(8,128)}, f32[16,32,128]{2,1,0:T(8,128)S(1)}, u32[]{:S(2)}, u32[]{:S(2)}) collective-permute-start(f32[16,32,128]{2,1,0:T(8,128)} %get-tuple-element.8), channel_id=1, source_target_pairs={{0,1},{1,2},{2,3},{3,4},{4,5},{5,6},{6,7},{7,8},{8,9},{9,10},{10,1... | collective-permute-start | bytes 786440 | tf_op jit(solution)/shard_map/ppermute | solution.py:79
  111.9 60.1 %collective-permute-start.1 = (f32[16,32,128]{2,1,0:T(8,128)}, f32[16,32,128]{2,1,0:T(8,128)}, u32[]{:S(2)}, u32[]{:S(2)}) collective-permute-start(f32[16,32,128]{2,1,0:T(8,128)} %get-tuple-element.7), channel_id=1, source_target_pairs={{1,0},{2,1},{3,2},{4,3},{5,4},{6,5},{7,6},{8,7},{9,8},{10,9},{11,1... | collective-permute-start | bytes 786440 | tf_op jit(solution)/shard_map/ppermute | solution.py:79
  117.4 2.9 %copy-start.11 = (s32[128]{0:T(128)S(1)}, s32[128]{0:T(128)}, u32[]{:S(2)}) copy-start(s32[128]{0:T(128)} %param.17) | copy-start | bytes 1540
  152.8 8.8 %copy-start.6 = (f32[384,384]{1,0:T(8,128)S(1)}, f32[384,384]{1,0:T(8,128)}, u32[]{:S(2)}) copy-start(f32[384,384]{1,0:T(8,128)} %constant.107) | copy-start | bytes 1769476
  157.2 14.9 %all-to-all-start.2 = ((f32[16,16,128]{2,1,0:T(8,128)}), f32[16,16,128]{2,1,0:T(8,128)S(1)}, u32[]{:S(2)}, u32[]{:S(2)}) async-start(f32[16,16,128]{2,1,0:T(8,128)} %bitcast.28), calls=%async_computation.2 | async-start | bytes 262144 | tf_op jit(solution)/shard_map/all_to_all | solution.py:277
  170.2 1.8 copy-start
  170.2 2.3 %copy-start.1 = (bf16[128,2560]{1,0:T(8,128)(2,1)S(1)}, bf16[128,2560]{1,0:T(8,128)(2,1)}, u32[]{:S(2)}) copy-start(bf16[128,2560]{1,0:T(8,128)(2,1)} %constant.97.clone.cols_ref) | copy-start | bytes 1966084
  170.3 2.4 %copy-start.2 = (bf16[640,256]{1,0:T(8,128)(2,1)S(1)}, bf16[640,256]{1,0:T(8,128)(2,1)}, u32[]{:S(2)}) copy-start(bf16[640,256]{1,0:T(8,128)(2,1)} %constant.96.clone.rows_ref) | copy-start | bytes 983044

commit v2 on v1

--- a/solution.py
+++ b/solution.py
@@ -1,3 +1,4 @@
+import ml_dtypes
 import numpy as np
 import jax
 import jax.numpy as jnp
@@ -91,10 +92,111 @@
     return jnp.dot(a, b, preferred_element_type=jnp.float32)
 
 
+def split2(x):
+    hi = x.astype(jnp.bfloat16)
+    return hi, (x - hi.astype(jnp.float32)).astype(jnp.bfloat16)
+
+
+def table_pair(table):
+    hi = np.asarray(table, np.float32).astype(ml_dtypes.bfloat16)
+    low = (np.asarray(table) - hi.astype(np.float64)).astype(ml_dtypes.bfloat16)
+    return jnp.asarray(np.stack([hi, low]))
+
+
+def right_product(x, pair):
+    hi, low = split2(x)
+    return dot(hi, pair[0]) + dot(low, pair[0]) + dot(hi, pair[1])
+
+
+def left_product(pair, x):
+    hi, low = split2(x)
+    return dot(pair[0], hi) + dot(pair[0], low) + dot(pair[1], hi)
+
+
+def moved(tiles, source, target, width, lane, out):
+    shift = (target - source) % 128
+    rolled = {}
+    begin = 0
+    while begin < width:
+        src, dst = source + begin, target + begin
+        end = min(width, begin + 128 - src % 128, begin + 128 - dst % 128)
+        if src // 128 not in rolled:
+            tile = tiles(src // 128)
+            rolled[src // 128] = pltpu.roll(tile, shift, 1) if shift else tile
+        tile = rolled[src // 128]
+        first, last = dst % 128, dst % 128 + end - begin
+        old = out[dst // 128]
+        if old is None or first == 0:
+            out[dst // 128] = tile
+        else:
+            out[dst // 128] = jnp.where(lane >= first, tile, old)
+        begin = end
+
+
+def plane_kernel(mode_ref, in_ref, ax_ref, ay_ref, by_ref, bx_ref, ey_ref, ex_ref, out_ref, x_ref, o_ref):
+    lane = lax.broadcasted_iota(jnp.int32, (PY, 128), 1)
+    for y in range(YB):
+        out = [None] * 3
+        for p in range(PX):
+            rows = slice(p * PY, (p + 1) * PY)
+            moved(lambda t: in_ref[rows, t * 128:(t + 1) * 128], y * XB, p * XB, XB, lane, out)
+        for t in range(3):
+            x_ref[y * PY:(y + 1) * PY, t * 128:(t + 1) * 128] = out[t]
+    z = right_product(x_ref[...], ax_ref)
+    z = left_product(ay_ref, z)
+    total = mode_ref[pl.program_id(0)] + ey_ref[...] + ex_ref[...]
+    is_zero = total == 0.0
+    z = jnp.where(is_zero, 0.0, z / jnp.where(is_zero, -1.0, total))
+    z = left_product(by_ref, z)
+    o_ref[...] = right_product(z, bx_ref)
+    for p in range(PX):
+        out = [None] * (PLANE // 128)
+        for y in range(YE):
+            rows = slice(y * PY, (y + 1) * PY)
+            moved(lambda t: o_ref[rows, t * 128:(t + 1) * 128], p * 64, y * XE, XE, lane, out)
+        for t in range(PLANE // 128):
+            out_ref[p * PY:(p + 1) * PY, t * 128:(t + 1) * 128] = out[t]
+
+
+def solve_planes(own_eig, got, q, eig):
+    n = np.arange(NR)
+    order = (n % PY) * YB + n // PY
+    wide = ((np.arange(YE)[:, None] - 2 + np.arange(PY)[None, :] * YB) % NR).reshape(-1)
+    wide_x = np.zeros((PX, 64, NR))
+    for p in range(PX):
+        wide_x[p, :XE] = q[(p * XB + np.arange(XE) - 1) % NR]
+    tables = [q, q[order].T, q[wide], wide_x.reshape(PX * 64, NR).T]
+    tables = [table_pair(table) for table in tables]
+    ey = jnp.asarray(eig[:, None], jnp.float32)
+    ex = jnp.asarray(eig[None, :], jnp.float32)
+    whole = lambda shape: pl.BlockSpec(shape, lambda m: (0,) * len(shape), pipeline_mode=pl.Buffered(1))
+    return pl.pallas_call(
+        plane_kernel,
+        grid=(MODES,),
+        out_shape=jax.ShapeDtypeStruct((DEV, MODES * PLANE), jnp.float32),
+        in_specs=[pl.BlockSpec(memory_space=pltpu.SMEM),
+                  pl.BlockSpec((DEV, XB * YB), lambda m: (0, m))]
+        + [whole(table.shape) for table in tables] + [whole(ey.shape), whole(ex.shape)],
+        out_specs=pl.BlockSpec((DEV, PLANE), lambda m: (0, m)),
+        scratch_shapes=[pltpu.VMEM((NR, NR), jnp.float32), pltpu.VMEM((YE * PY, PX * 64), jnp.float32)],
+        compiler_params=pltpu.CompilerParams(vmem_limit_bytes=48 << 20),
+        name="solve_planes",
+    )(own_eig, got, *tables, ey, ex)
+
+
+def columns_of(s_ref, pair):
+    total = None
+    for m in range(MODES):
+        hi, low = split2(s_ref[:, m * PLANE:(m + 1) * PLANE])
+        rows = slice(m * DEV, (m + 1) * DEV)
+        for left, right in ((hi, pair[0, rows]), (low, pair[0, rows]), (hi, pair[1, rows])):
+            part = lax.dot_general(left, right, (((0,), (0,)), ((), ())), preferred_element_type=jnp.float32)
+            total = part if total is None else total + part
+    return total
+
+
 def cut_kernel(start_ref, s_ref, g_ref, out_ref, p_ref):
-    cells = lax.dot_general(
-        s_ref[...], g_ref[...], (((0,), (0,)), ((), ())),
-        precision=lax.Precision.HIGHEST, preferred_element_type=jnp.float32)
+    cells = columns_of(s_ref, jnp.stack(split2(g_ref[...])))
     for y in range(YE):
         p_ref[y, :XE, :] = cells[y * XE:(y + 1) * XE, :]
     lane = lax.broadcasted_iota(jnp.int32, (16, 128), 1)
@@ -122,6 +224,24 @@
         compiler_params=pltpu.CompilerParams(vmem_limit_bytes=48 << 20),
         name="cut_patches",
     )(starts, spectrum, columns)
+
+
+def block_kernel(s_ref, q_ref, out_ref):
+    cells = columns_of(s_ref, q_ref)
+    for y in range(YB):
+        first = (y + 2) * XE + 1
+        out_ref[:, y, :] = cells[first:first + XB, :]
+
+
+def block_of(spectrum, q):
+    return pl.pallas_call(
+        block_kernel,
+        out_shape=jax.ShapeDtypeStruct((XB, YB, NR), jnp.float32),
+        in_specs=[pl.BlockSpec(memory_space=pltpu.VMEM), pl.BlockSpec(memory_space=pltpu.VMEM)],
+        out_specs=pl.BlockSpec(memory_space=pltpu.VMEM),
+        compiler_params=pltpu.CompilerParams(vmem_limit_bytes=48 << 20),
+        name="block_of",
+    )(spectrum, table_pair(q.T))
 
 
 def relax_kernel(flag_ref, patch_ref, rows_ref, cols_ref, dens_ref, low_ref, high_ref, vel_ref,
@@ -248,23 +368,8 @@
 
     packed = jnp.einsum("xyz,zmt->tmyx", root_density, basis.reshape(NR, MODES, DEV), precision=HIGH)
     got = lax.all_to_all(packed.reshape(DEV, MODES * YB * XB), ("px", "py"), 0, 0, tiled=True)
-    planes = got.reshape(PX, PY, MODES, YB, XB).transpose(2, 3, 1, 0, 4).reshape(MODES, NR, NR)
-    n = np.arange(NR)
-    order = (n % PY) * YB + n // PY
-    wide = ((np.arange(YE)[:, None] - 2 + np.arange(PY)[None, :] * YB) % NR).reshape(-1)
-    wide_x = ((np.arange(PX)[:, None] * XB + np.arange(XE)[None, :] - 1) % NR).reshape(-1)
-    z = jnp.einsum("myx,xk->myk", planes, basis, precision=HIGH)
-    z = jnp.einsum("myk,yl->mlk", z, jnp.asarray(q[order], jnp.float32), precision=HIGH)
     own_eig = eigen[jnp.arange(MODES) * DEV + device]
-    total = own_eig[:, None, None] + eigen[None, :, None] + eigen[None, None, :]
-    is_zero = total == 0.0
-    z = z * jnp.where(is_zero, 0.0, 1.0 / jnp.where(is_zero, -1.0, total))
-    z = jnp.einsum("mlk,yl->myk", z, jnp.asarray(q[wide], jnp.float32), precision=HIGH)
-    z = jnp.einsum("myk,xk->myx", z, jnp.asarray(q[wide_x], jnp.float32), precision=HIGH)
-    z = z.reshape(MODES, YE, PY, PX, XE).transpose(3, 2, 0, 1, 4).reshape(DEV, MODES, YE * XE)
-    z = jnp.pad(z, ((0, 0), (0, 0), (0, PLANE - YE * XE))).reshape(DEV, MODES * PLANE)
-    back = lax.all_to_all(z, ("px", "py"), 0, 0, tiled=True)
-    spectrum = back.reshape(DEV, MODES, PLANE).transpose(1, 0, 2).reshape(NR, PLANE)
+    back = lax.all_to_all(solve_planes(own_eig, got, q, eig), ("px", "py"), 0, 0, tiled=True)
 
     targets = jnp.arange(PY, dtype=jnp.int32)
     wanted = (place_first * PY + targets) * slots + (place_second - targets) % PY
@@ -273,13 +378,11 @@
     columns = basis[third.reshape(-1)].T
     start_first = jnp.clip(anchors[0] - place_first * XB, 0, XB - REG)
     start_second = jnp.clip(anchors[1] - place_second * YB, 0, YB - REG)
-    sending = cut_patches(spectrum, columns, jnp.stack([start_first, start_second]))
+    sending = cut_patches(back, columns, jnp.stack([start_first, start_second]))
     arrived = lax.all_to_all(sending, "py", 0, 0, tiled=True)
     positions = jnp.arange(slots, dtype=jnp.int32)
 
-    block = jnp.einsum("nc,zn->cz", spectrum, basis, precision=HIGH)
-    block = block[:YE * XE].reshape(YE, XE, NR)[2:-2, 1:-1]
-    coarse_potential = block.transpose(1, 0, 2)
+    coarse_potential = block_of(back, q)
 
     first_slot = device * slots
     padded = jnp.pad(neighbour, ((0, 0), (slots, slots)), constant_values=-1)

time: 203 us -> 147 us (0.72); the launches traced: 200 us -> 146 us
  local copies, waits for them, and re-layouts: 70 us -> 20.3 us
  Pallas kernels: 31.1 us -> 47.5 us
  matrix products: 16.8 us -> 3.49 us
  other arithmetic: 14 us -> 0.93 us
  waiting for transfers between devices: 40.3 us -> 44.9 us
  starting transfers between devices: 26.2 us -> 28.3 us
    reshape x5 -> x0, local copies, waits for them, and re-layouts: 20.6 us -> none  [the longest x2 9.96 us: local(): z.reshape(MODES, YE, PY, PX, XE).transpose(3, 2, 0, 1, 4)]
    transpose x3 -> x0, local copies, waits for them, and re-layouts: 17.9 us -> none  [the longest x1 8.5 us: local(): z.reshape(MODES, YE, PY, PX, XE).transpose(3, 2, 0, 1, 4)]
    pallas_call x0 -> x2, Pallas kernels: none -> 17.2 us  [the longest x1 12.8 us: solve_planes(): pl.pallas_call(plane_kernel, grid=(MODES,), out_shape=jax.ShapeDtypeStruc...]
    dot_general x5 -> x0, matrix products: 13.3 us -> none  [the longest x1 5.25 us: local(): block = jnp.einsum('nc,zn->cz', spectrum, basis, precision=HIGH)]
    all_to_all x2 -> x0, other arithmetic: 13 us -> none  [the longest x1 7.16 us: local(): back = lax.all_to_all(z, ('px', 'py'), 0, 0, tiled=True)]
    all_to_all x1, waiting for transfers between devices: 15.1 us -> 19.3 us  [local(): lax.all_to_all(solve_planes(own_eig, got, q, eig), ('px', 'py'), 0, 0, ti...]
    dot_general x1 -> x0, local copies, waits for them, and re-layouts: 2.82 us -> none  [local(): block = jnp.einsum('nc,zn->cz', spectrum, basis, precision=HIGH)]
    all_to_all x2 -> x1, local copies, waits for them, and re-layouts: 7.79 us -> 5.17 us  [local(): lax.all_to_all(solve_planes(own_eig, got, q, eig), ('px', 'py'), 0, 0, ti...]
  transfers between devices with their start and end apart: 5 -> 5, of which waited for: 2 -> 3; matrix products, arithmetic and copies ran while one was open for 19% -> 6% of each run, Pallas kernels for 2% -> 5%
where the time goes in v2:
time: 147 us; the launch traced here: 146 us
  Pallas kernels  47.5 us (32%)
  waiting for transfers between devices  44.9 us (31%)
  starting transfers between devices  28.3 us (19%)
  local copies, waits for them, and re-layouts  20.3 us (14%)
  matrix products  3.49 us (2%)
    pallas_call x1, Pallas kernels, relax(): pl.pallas_call(relax_kernel, grid_spec=pltpu.PrefetchScalarGridSpec(num_s...  26.8 us
    all_to_all x1, waiting for transfers between devices, local(): lax.all_to_all(packed.reshape(DEV, MODES * YB * XB), ('px', 'py'), 0, 0,...  25 us
    all_to_all x1, waiting for transfers between devices, local(): lax.all_to_all(solve_planes(own_eig, got, q, eig), ('px', 'py'), 0, 0, ti...  19.3 us
    pallas_call x1, Pallas kernels, solve_planes(): pl.pallas_call(plane_kernel, grid=(MODES,), out_shape=jax.ShapeDtypeStruc...  12.8 us
    all_to_all x1, starting transfers between devices, local(): lax.all_to_all(packed.reshape(DEV, MODES * YB * XB), ('px', 'py'), 0, 0,...  11.9 us
    unnamed x33, local copies, waits for them, and re-layouts  6.33 us
    ppermute x2, starting transfers between devices, from_behind(): lax.ppermute(value, axis, [(source, source + steps) for source in range(i...  6.17 us
    all_to_all x1, starting transfers between devices, local(): lax.all_to_all(solve_planes(own_eig, got, q, eig), ('px', 'py'), 0, 0, ti...  6 us
  transfers between devices with their start and end apart: 5, of which 3 were waited for; matrix products, arithmetic and copies ran while one was open for 6% of the time, Pallas kernels for 5%

profile of v2, /device:TPU:1, one launch (start us, length us, event | category | flops | bytes accessed | tf_op | source)
XLA Modules:
  0.0 146.3 jit_solution(3619675412917127608)
XLA Ops:
  0.6 3.5 %fusion = f32[3,128,48,24]{1,2,3,0:T(8,128)S(1)} fusion(f32[384,3,128,1]{2,0,3,1:T(8,128)} %constant.108, f32[48,24,384]{2,1,0:T(8,128)} %param.17), kind=kOutput, calls=%fused_computation.5 | convolution fusion | flops 1019215872 | bytes 4128768 | tf_op jit(solution)/shard_map/xyz,zmt->tmyx/dot_general | solution.py:369
  4.1 3.3 %copy.39 = f32[128,1,3456]{2,1,0:T(1,128)} copy(f32[128,1,3456]{0,2,1:T(8,128)S(1)} %bitcast.41) | data formatting | bytes 3538944 | tf_op jit(solution)/shard_map/all_to_all | solution.py:370
  7.4 11.9 %all-to-all-start = ((f32[128,1,3456]{2,1,0:T(1,128)}), f32[128,1,3456]{2,1,0:T(1,128)}, u32[]{:S(2)}, u32[]{:S(2)}) async-start(f32[128,1,3456]{2,1,0:T(1,128)} %copy.39), calls=%async_computation | async-start | bytes 3538944 | tf_op jit(solution)/shard_map/all_to_all | solution.py:370
  19.3 0.6 gather_fusion
  20.0 0.0 copy-start.6
  20.0 0.0 copy-start.8
  20.0 0.0 copy-start.9
  20.0 25.0 %all-to-all-done = f32[128,1,3456]{2,1,0:T(1,128)} async-done(((f32[128,1,3456]{2,1,0:T(1,128)}), f32[128,1,3456]{2,1,0:T(1,128)}, u32[]{:S(2)}, u32[]{:S(2)}) %all-to-all-start) | async-done | bytes 1769504 | tf_op jit(solution)/shard_map/all_to_all | solution.py:370
  45.1 1.6 %copy.58 = f32[128,1,3456]{2,0,1:T(8,128)S(1)} copy(f32[128,1,3456]{2,1,0:T(1,128)} %all-to-all-done) | data formatting | bytes 3538944
  46.7 0.0 copy-done.1
  46.7 12.8 %solve_planes.1 = f32[128,4224]{1,0:T(8,128)} custom-call(f32[3]{0:T(128)S(1)} %gather_fusion, f32[128,3456]{1,0:T(8,128)S(1)} %bitcast.37, bf16[2,384,384]{2,1,0:T(8,128)(2,1)S(1)} %copy-done.6, bf16[2,384,384]{2,1,0:T(8,128)(2,1)S(1)} %copy-done.5, bf16[2,448,384]{2,1,0:T(8,128)(2,1)S(1)} %copy-done.2, bf16[2,384,512]{2,1,0:T(8,128)(2,1)S(1)} %copy-done.1, ...), custom_call_target="tpu_custom_call" | custom-call | tf_op jit(solution)/shard_map/solve_planes/pallas_call | solution.py:173
  59.5 5.2 %copy.40 = f32[128,1,4224]{2,1,0:T(1,128)} copy(f32[128,1,4224]{2,0,1:T(8,128)} %bitcast.40) | data formatting | bytes 4325376 | tf_op jit(solution)/shard_map/all_to_all | solution.py:372
  64.7 6.0 %all-to-all-start.1 = ((f32[128,1,4224]{2,1,0:T(1,128)}), f32[128,1,4224]{2,1,0:T(1,128)}, u32[]{:S(2)}, u32[]{:S(2)}) async-start(f32[128,1,4224]{2,1,0:T(1,128)} %copy.40), calls=%async_computation.1 | async-start | bytes 4325376 | tf_op jit(solution)/shard_map/all_to_all | solution.py:372
  70.7 0.0 copy-start.13
  70.7 0.0 copy-start.11
  70.7 1.9 %fusion.19 = (f32[16,32,128]{2,1,0:T(8,128)}, f32[16,32,128]{2,1,0:T(8,128)}) fusion(f32[16,32,1024]{2,1,0:T(8,128)} %dens_ref.1), kind=kLoop, calls=%fused_computation.50 | loop fusion | bytes 1048576 | tf_op jit(solution)/shard_map/slice | solution.py:367
  72.6 1.3 collective-permute-start.1
  73.9 4.9 %collective-permute-start = (f32[16,32,128]{2,1,0:T(8,128)}, f32[16,32,128]{2,1,0:T(8,128)}, u32[]{:S(2)}, u32[]{:S(2)}) collective-permute-start(f32[16,32,128]{2,1,0:T(8,128)} %get-tuple-element.8), channel_id=1, source_target_pairs={{0,1},{1,2},{2,3},{3,4},{4,5},{5,6},{6,7},{7,8},{8,9},{9,10},{10,1... | collective-permute-start | bytes 786440 | tf_op jit(solution)/shard_map/ppermute | solution.py:80
  78.8 0.4 copy.45
  79.2 0.1 fusion.6
  79.3 0.6 gather_fusion.1
  79.9 0.1 copy.46
  80.0 0.1 add_remainder_fusion
  80.1 0.1 rem.73
  80.2 0.1 pad_dynamic-slice_fusion
  80.3 1.0 gather_fusion.2
  81.3 0.2 copy.47
  81.5 19.3 %all-to-all-done.1 = f32[128,1,4224]{2,1,0:T(1,128)} async-done(((f32[128,1,4224]{2,1,0:T(1,128)}), f32[128,1,4224]{2,1,0:T(1,128)}, u32[]{:S(2)}, u32[]{:S(2)}) %all-to-all-start.1) | async-done | bytes 2162720 | tf_op jit(solution)/shard_map/all_to_all | solution.py:372
  100.7 1.7 %copy.57 = f32[128,1,4224]{2,0,1:T(8,128)S(1)} copy(f32[128,1,4224]{2,1,0:T(1,128)} %all-to-all-done.1) | data formatting | bytes 4325376
  102.5 0.0 copy-start.14
  102.5 0.0 copy-start.4
  102.5 3.5 %cut_patches.1 = f32[256,128]{1,0:T(8,128)} custom-call(s32[2,16]{1,0:T(2,128)S(1)} %pad_add_fusion.start_ref, f32[128,4224]{1,0:T(8,128)S(1)} %bitcast.35, f32[384,256]{1,0:T(8,128)S(1)} %bitcast.38), custom_call_target="tpu_custom_call" | custom-call | tf_op jit(solution)/shard_map/cut_patches/pallas_call | solution.py:216
  106.1 4.2 %all-to-all-start.2 = ((f32[16,16,128]{2,1,0:T(8,128)}), f32[16,16,128]{2,1,0:T(8,128)S(1)}, u32[]{:S(2)}, u32[]{:S(2)}) async-start(f32[16,16,128]{2,1,0:T(8,128)} %bitcast.16), calls=%async_computation.2 | async-start | bytes 262144 | tf_op jit(solution)/shard_map/all_to_all | solution.py:382
  110.3 0.1 copy.42
  110.4 0.1 copy.44
  110.4 0.1 copy.41
  110.5 0.1 copy.43
  110.6 0.6 dynamic_slice.15
  111.2 0.6 fusion.13
  111.8 0.1 stack.4.flag_ref
  111.9 0.0 copy-start.3
  112.0 4.4 %block_of.1 = f32[48,24,384]{2,1,0:T(8,128)} custom-call(f32[128,4224]{1,0:T(8,128)S(1)} %bitcast.36, bf16[2,384,384]{2,1,0:T(8,128)(2,1)S(1)} %copy-done.4), custom_call_target="tpu_custom_call" | custom-call | tf_op jit(solution)/shard_map/block_of/pallas_call | solution.py:237
  116.3 0.0 collective-permute-done.1.high_ref
  116.3 0.0 collective-permute-done.low_ref
  116.3 0.6 all-to-all-done.2
  116.9 1.6 %copy-done = f32[16,32,1024]{2,1,0:T(8,128)S(1)} copy-done((f32[16,32,1024]{2,1,0:T(8,128)S(1)}, f32[16,32,1024]{2,1,0:T(8,128)}, u32[]{:S(2)}) %copy-start) | copy-done | bytes 2097176
  118.5 1.0 copy-done.7
  119.5 26.8 %relax_and_kick.1 = (f32[16,32,1024]{2,1,0:T(8,128)}, f32[3,16,32,1024]{3,2,1,0:T(8,128)}) custom-call(s32[16,6]{1,0:T(8,128)S(1)} %stack.4.flag_ref, f32[256,128]{1,0:T(8,128)S(1)} %bitcast.39, bf16[640,256]{1,0:T(8,128)(2,1)S(1)} %copy-done.7, bf16[128,2560]{1,0:T(8,128)(2,1)S(1)} %copy-done.3, f32[16,32,1024]{2,1,0:T(8,128)S(1)} %copy-done, ...), custom_call_target="tpu_custom_call" | custom-call | tf_op jit(solution)/shard_map/relax_and_kick/pallas_call | solution.py:329
  (29 shorter events, 0.1 us)
Async XLA Ops:
  7.4 11.9 %copy-start.10 = (f32[384]{0:T(512)S(1)}, f32[384]{0:T(512)}, u32[]{:S(2)}) copy-start(f32[384]{0:T(512)} %constant.92.clone) | copy-start | bytes 4612
  7.4 37.7 %all-to-all-start = ((f32[128,1,3456]{2,1,0:T(1,128)}), f32[128,1,3456]{2,1,0:T(1,128)}, u32[]{:S(2)}, u32[]{:S(2)}) async-start(f32[128,1,3456]{2,1,0:T(1,128)} %copy.39), calls=%async_computation | async-start | bytes 3538944 | tf_op jit(solution)/shard_map/all_to_all | solution.py:370
  20.0 26.7 %copy-start.1 = (bf16[2,384,512]{2,1,0:T(8,128)(2,1)S(1)}, bf16[2,384,512]{2,1,0:T(8,128)(2,1)}, u32[]{:S(2)}) copy-start(bf16[2,384,512]{2,1,0:T(8,128)(2,1)} %constant.96.clone.bx_ref) | copy-start | bytes 2359300
  20.0 26.7 %copy-start.2 = (bf16[2,448,384]{2,1,0:T(8,128)(2,1)S(1)}, bf16[2,448,384]{2,1,0:T(8,128)(2,1)}, u32[]{:S(2)}) copy-start(bf16[2,448,384]{2,1,0:T(8,128)(2,1)} %constant.95.clone.by_ref) | copy-start | bytes 2064388
  20.0 26.7 %copy-start.5 = (bf16[2,384,384]{2,1,0:T(8,128)(2,1)S(1)}, bf16[2,384,384]{2,1,0:T(8,128)(2,1)}, u32[]{:S(2)}) copy-start(bf16[2,384,384]{2,1,0:T(8,128)(2,1)} %constant.94.clone.ay_ref) | copy-start | bytes 1769476
  20.0 26.7 %copy-start.6 = (bf16[2,384,384]{2,1,0:T(8,128)(2,1)S(1)}, bf16[2,384,384]{2,1,0:T(8,128)(2,1)}, u32[]{:S(2)}) copy-start(bf16[2,384,384]{2,1,0:T(8,128)(2,1)} %constant.93.clone.ax_ref) | copy-start | bytes 1769476
  20.0 26.7 %copy-start.8 = (f32[384,1]{1,0:T(8,128)S(1)}, f32[384,1]{1,0:T(8,128)}, u32[]{:S(2)}) copy-start(f32[384,1]{1,0:T(8,128)} %constant.97.clone.ey_ref) | copy-start | bytes 4612
  20.0 26.7 %copy-start.9 = (f32[1,384]{1,0:T(1,128)S(1)}, f32[1,384]{1,0:T(1,128)}, u32[]{:S(2)}) copy-start(f32[1,384]{1,0:T(1,128)} %constant.98.clone.ex_ref) | copy-start | bytes 4612
  64.7 14.1 %copy-start.12 = (s32[3,2048]{1,0:T(4,128)S(1)}, s32[3,2048]{1,0:T(4,128)}, u32[]{:S(2)}) copy-start(s32[3,2048]{1,0:T(4,128)} %param.20) | copy-start | bytes 73732
  64.7 36.0 %all-to-all-start.1 = ((f32[128,1,4224]{2,1,0:T(1,128)}), f32[128,1,4224]{2,1,0:T(1,128)}, u32[]{:S(2)}, u32[]{:S(2)}) async-start(f32[128,1,4224]{2,1,0:T(1,128)} %copy.40), calls=%async_computation.1 | async-start | bytes 4325376 | tf_op jit(solution)/shard_map/all_to_all | solution.py:372
  70.7 9.5 %copy-start.13 = (s32[2,2048]{1,0:T(2,128)S(1)}, s32[2,2048]{1,0:T(2,128)}, u32[]{:S(2)}) copy-start(s32[2,2048]{1,0:T(2,128)} %param.22) | copy-start | bytes 49156
  70.7 9.6 %copy-start.11 = (f32[384,384]{1,0:T(8,128)S(1)}, f32[384,384]{1,0:T(8,128)}, u32[]{:S(2)}) copy-start(f32[384,384]{1,0:T(8,128)} %constant.91.clone) | copy-start | bytes 1769476
  72.6 43.7 %collective-permute-start.1 = (f32[16,32,128]{2,1,0:T(8,128)}, f32[16,32,128]{2,1,0:T(8,128)}, u32[]{:S(2)}, u32[]{:S(2)}) collective-permute-start(f32[16,32,128]{2,1,0:T(8,128)} %get-tuple-element.7), channel_id=1, source_target_pairs={{1,0},{2,1},{3,2},{4,3},{5,4},{6,5},{7,6},{8,7},{9,8},{10,9},{11,1... | collective-permute-start | bytes 786440 | tf_op jit(solution)/shard_map/ppermute | solution.py:80
  73.9 42.4 %collective-permute-start = (f32[16,32,128]{2,1,0:T(8,128)}, f32[16,32,128]{2,1,0:T(8,128)}, u32[]{:S(2)}, u32[]{:S(2)}) collective-permute-start(f32[16,32,128]{2,1,0:T(8,128)} %get-tuple-element.8), channel_id=1, source_target_pairs={{0,1},{1,2},{2,3},{3,4},{4,5},{5,6},{6,7},{7,8},{8,9},{9,10},{10,1... | collective-permute-start | bytes 786440 | tf_op jit(solution)/shard_map/ppermute | solution.py:80
  102.5 8.1 %copy-start.14 = (s32[128]{0:T(128)S(1)}, s32[128]{0:T(128)}, u32[]{:S(2)}) copy-start(s32[128]{0:T(128)} %param.21) | copy-start | bytes 1540
  102.5 9.4 %copy-start.4 = (bf16[2,384,384]{2,1,0:T(8,128)(2,1)S(1)}, bf16[2,384,384]{2,1,0:T(8,128)(2,1)}, u32[]{:S(2)}) copy-start(bf16[2,384,384]{2,1,0:T(8,128)(2,1)} %constant.99.clone.q_ref) | copy-start | bytes 1769476
  106.1 10.9 %all-to-all-start.2 = ((f32[16,16,128]{2,1,0:T(8,128)}), f32[16,16,128]{2,1,0:T(8,128)S(1)}, u32[]{:S(2)}, u32[]{:S(2)}) async-start(f32[16,16,128]{2,1,0:T(8,128)} %bitcast.16), calls=%async_computation.2 | async-start | bytes 262144 | tf_op jit(solution)/shard_map/all_to_all | solution.py:382
  111.9 5.0 %copy-start.3 = (bf16[128,2560]{1,0:T(8,128)(2,1)S(1)}, bf16[128,2560]{1,0:T(8,128)(2,1)}, u32[]{:S(2)}) copy-start(bf16[128,2560]{1,0:T(8,128)(2,1)} %constant.101.clone.cols_ref) | copy-start | bytes 1966084
  116.9 1.6 %copy-start = (f32[16,32,1024]{2,1,0:T(8,128)S(1)}, f32[16,32,1024]{2,1,0:T(8,128)}, u32[]{:S(2)}) copy-start(f32[16,32,1024]{2,1,0:T(8,128)} %dens_ref.1) | copy-start | bytes 6291460
  118.5 1.0 copy-start.7

commit v3 on v2

--- a/solution.py
+++ b/solution.py
@@ -21,6 +21,9 @@
 XE = XB + 2
 YE = YB + 4
 PLANE = 1408
+ROWS = 48
+TILES_IN = XB * YB // 128
+TILES_OUT = PLANE // 128
 EDGE = 4
 LANES = (CELLS + 2 * EDGE) * CELLS
 RELAX = 6.0 / 7.0
@@ -133,61 +136,126 @@
         begin = end
 
 
+def forward_kernel(in_ref, q_ref, out_ref, rows_ref, sem):
+    copies = [pltpu.make_async_copy(in_ref.at[:, y], rows_ref.at[y], sem.at[y]) for y in range(YB)]
+    for copy in copies:
+        copy.start()
+    for copy in copies:
+        copy.wait()
+    hi, low = split2(rows_ref[...].reshape(YB * XB, NR))
+    contract = (((1,), (1,)), ((), ()))
+    modes = None
+    for left, right in ((q_ref[0], hi), (q_ref[0], low), (q_ref[1], hi)):
+        part = lax.dot_general(left, right, contract, preferred_element_type=jnp.float32)
+        modes = part if modes is None else modes + part
+    for m in range(MODES):
+        for c in range(TILES_IN):
+            out_ref[pl.ds(m * TILES_IN + c, DEV, stride=MODES * TILES_IN), :] = (
+                modes[m * DEV:(m + 1) * DEV, c * 128:(c + 1) * 128])
+
+
+def forward_third(density, q):
+    return pl.pallas_call(
+        forward_kernel,
+        out_shape=jax.ShapeDtypeStruct((DEV * MODES * TILES_IN, 128), jnp.float32),
+        in_specs=[pl.BlockSpec(memory_space=pl.ANY), pl.BlockSpec(memory_space=pltpu.VMEM)],
+        out_specs=pl.BlockSpec(memory_space=pltpu.VMEM),
+        scratch_shapes=[pltpu.VMEM((YB, XB, NR), jnp.float32), pltpu.SemaphoreType.DMA((YB,))],
+        compiler_params=pltpu.CompilerParams(vmem_limit_bytes=48 << 20),
+        name="forward_third",
+    )(density, table_pair(q.T))
+
+
 def plane_kernel(mode_ref, in_ref, ax_ref, ay_ref, by_ref, bx_ref, ey_ref, ex_ref, out_ref, x_ref, o_ref):
-    lane = lax.broadcasted_iota(jnp.int32, (PY, 128), 1)
-    for y in range(YB):
-        out = [None] * 3
+    lane = lax.broadcasted_iota(jnp.int32, (8, 128), 1)
+    stride_in = MODES * TILES_IN
+    stride_out = MODES * TILES_OUT
+    for m in range(MODES):
+        for y in range(YB):
+            for h in range(2):
+                even, odd = [None, None], [None, None]
+                for p in range(PX // 2):
+                    loaded = {}
+
+                    def pair(c):
+                        if c not in loaded:
+                            near = in_ref[pl.ds((p * PY + h * 8) * stride_in + m * TILES_IN + c, 8, stride=stride_in), :]
+                            far = in_ref[pl.ds(((p + PX // 2) * PY + h * 8) * stride_in + m * TILES_IN + c, 8,
+                                               stride=stride_in), :]
+                            loaded[c] = (near + far, near - far)
+                        return loaded[c]
+
+                    moved(lambda c: pair(c)[0], y * XB, p * XB, XB, lane, even)
+                    moved(lambda c: pair(c)[1], y * XB, p * XB, XB, lane, odd)
+                row = y * PY + h * 8
+                for t, tile in enumerate(even + odd):
+                    x_ref[m, row:row + 8, t * 128:(t + 1) * 128] = tile
+    for m in range(MODES):
+        z = jnp.concatenate([right_product(x_ref[m, :, i * 256:(i + 1) * 256], ax_ref.at[i]) for i in range(2)], axis=1)
+        z = z.reshape(YB, PY, 512)
+        near = z[:, :8].reshape(YB * 8, 512)
+        far = z[:, 8:].reshape(YB * 8, 512)
+        halves = []
+        for i, z in enumerate((near + far, near - far)):
+            z = left_product(ay_ref.at[i], z)
+            total = mode_ref[m] + ey_ref[i] + ex_ref[...]
+            is_zero = total == 0.0
+            z = jnp.where(is_zero, 0.0, z / jnp.where(is_zero, -1.0, total))
+            halves.append(left_product(by_ref.at[i], z))
+        z = jnp.concatenate([halves[0] + halves[1], halves[0] - halves[1]], axis=0)
+        even, odd = (right_product(z[:, i * 256:(i + 1) * 256], bx_ref.at[i]) for i in range(2))
+        o_ref[m, :, :256] = even + odd
+        o_ref[m, :, 256:] = even - odd
+    for m in range(MODES):
         for p in range(PX):
-            rows = slice(p * PY, (p + 1) * PY)
-            moved(lambda t: in_ref[rows, t * 128:(t + 1) * 128], y * XB, p * XB, XB, lane, out)
-        for t in range(3):
-            x_ref[y * PY:(y + 1) * PY, t * 128:(t + 1) * 128] = out[t]
-    z = right_product(x_ref[...], ax_ref)
-    z = left_product(ay_ref, z)
-    total = mode_ref[pl.program_id(0)] + ey_ref[...] + ex_ref[...]
-    is_zero = total == 0.0
-    z = jnp.where(is_zero, 0.0, z / jnp.where(is_zero, -1.0, total))
-    z = left_product(by_ref, z)
-    o_ref[...] = right_product(z, bx_ref)
-    for p in range(PX):
-        out = [None] * (PLANE // 128)
-        for y in range(YE):
-            rows = slice(y * PY, (y + 1) * PY)
-            moved(lambda t: o_ref[rows, t * 128:(t + 1) * 128], p * 64, y * XE, XE, lane, out)
-        for t in range(PLANE // 128):
-            out_ref[p * PY:(p + 1) * PY, t * 128:(t + 1) * 128] = out[t]
+            for h in range(2):
+                out = [None] * TILES_OUT
+                for y in range(YE):
+                    row = h * YE * 8 + y * 8
+                    moved(lambda t: o_ref[m, row:row + 8, t * 128:(t + 1) * 128], p * 64, y * XE, XE, lane, out)
+                for t in range(TILES_OUT):
+                    out_ref[pl.ds((p * PY + h * 8) * stride_out + m * TILES_OUT + t, 8, stride=stride_out), :] = out[t]
 
 
 def solve_planes(own_eig, got, q, eig):
-    n = np.arange(NR)
-    order = (n % PY) * YB + n // PY
-    wide = ((np.arange(YE)[:, None] - 2 + np.arange(PY)[None, :] * YB) % NR).reshape(-1)
-    wide_x = np.zeros((PX, 64, NR))
-    for p in range(PX):
-        wide_x[p, :XE] = q[(p * XB + np.arange(XE) - 1) % NR]
-    tables = [q, q[order].T, q[wide], wide_x.reshape(PX * 64, NR).T]
-    tables = [table_pair(table) for table in tables]
-    ey = jnp.asarray(eig[:, None], jnp.float32)
-    ex = jnp.asarray(eig[None, :], jnp.float32)
-    whole = lambda shape: pl.BlockSpec(shape, lambda m: (0,) * len(shape), pipeline_mode=pl.Buffered(1))
+    k = np.rint(np.arcsin(np.sqrt(-eig / 4.0)) * NR / np.pi).astype(int)
+    n = np.arange(NR // 2)
+    order = (n % 8) * YB + n // 8
+    wide = ((np.arange(YE)[:, None] - 2 + np.arange(8)[None, :] * YB) % NR).reshape(-1)
+    half = NR // 2
+    tables = [[], [], [], []]
+    ey = np.zeros((2, half, 1))
+    ex = np.full((1, 512), -1.0)
+    for i in range(2):
+        part = q[:, k % 2 == i]
+        ey[i, :, 0] = eig[k % 2 == i]
+        ex[0, i * 256:i * 256 + half] = eig[k % 2 == i]
+        ax = np.zeros((256, 256))
+        ax[:half, :half] = part[:half]
+        bx = np.zeros((256, PX // 2, 64))
+        for p in range(PX // 2):
+            bx[:half, p, :XE] = part[(p * XB + np.arange(XE) - 1) % NR].T
+        for bucket, table in zip(tables, (ax, part[order].T, part[wide], bx.reshape(256, 256))):
+            bucket.append(table_pair(table))
+    tables = [jnp.stack(bucket) for bucket in tables]
+    vmem = pl.BlockSpec(memory_space=pltpu.VMEM)
     return pl.pallas_call(
         plane_kernel,
-        grid=(MODES,),
-        out_shape=jax.ShapeDtypeStruct((DEV, MODES * PLANE), jnp.float32),
-        in_specs=[pl.BlockSpec(memory_space=pltpu.SMEM),
-                  pl.BlockSpec((DEV, XB * YB), lambda m: (0, m))]
-        + [whole(table.shape) for table in tables] + [whole(ey.shape), whole(ex.shape)],
-        out_specs=pl.BlockSpec((DEV, PLANE), lambda m: (0, m)),
-        scratch_shapes=[pltpu.VMEM((NR, NR), jnp.float32), pltpu.VMEM((YE * PY, PX * 64), jnp.float32)],
+        out_shape=jax.ShapeDtypeStruct((DEV * MODES * TILES_OUT, 128), jnp.float32),
+        in_specs=[pl.BlockSpec(memory_space=pltpu.SMEM)] + [vmem] * 7,
+        out_specs=vmem,
+        scratch_shapes=[pltpu.VMEM((MODES, NR, 512), jnp.float32), pltpu.VMEM((MODES, YE * PY, 512), jnp.float32)],
         compiler_params=pltpu.CompilerParams(vmem_limit_bytes=48 << 20),
         name="solve_planes",
-    )(own_eig, got, *tables, ey, ex)
+    )(own_eig, got, *tables, jnp.asarray(ey, jnp.float32), jnp.asarray(ex, jnp.float32))
 
 
 def columns_of(s_ref, pair):
     total = None
     for m in range(MODES):
-        hi, low = split2(s_ref[:, m * PLANE:(m + 1) * PLANE])
+        rows = jnp.concatenate(
+            [s_ref[pl.ds(m * TILES_OUT + c, DEV, stride=MODES * TILES_OUT), :] for c in range(TILES_OUT)], axis=1)
+        hi, low = split2(rows)
         rows = slice(m * DEV, (m + 1) * DEV)
         for left, right in ((hi, pair[0, rows]), (low, pair[0, rows]), (hi, pair[1, rows])):
             part = lax.dot_general(left, right, (((0,), (0,)), ((), ())), preferred_element_type=jnp.float32)
@@ -200,6 +268,7 @@
     for y in range(YE):
         p_ref[y, :XE, :] = cells[y * XE:(y + 1) * XE, :]
     lane = lax.broadcasted_iota(jnp.int32, (16, 128), 1)
+    inside = lax.broadcasted_iota(jnp.int32, (16, 128), 0) < REG + 2
     for t in range(PY):
         acc = jnp.zeros((16, 128), jnp.float32)
         for b in range(12):
@@ -208,7 +277,7 @@
             shift = (b * 10 - (t % 8) * 16) % 128
             if shift:
                 tile = pltpu.roll(tile, shift, 1)
-            acc = jnp.where((lane >= b * 10) & (lane < b * 10 + 10), tile, acc)
+            acc = jnp.where((lane >= b * 10) & (lane < b * 10 + 10) & inside, tile, acc)
         out_ref[t * 16:(t + 1) * 16, :] = acc
 
 
@@ -245,86 +314,129 @@
 
 
 def relax_kernel(flag_ref, patch_ref, rows_ref, cols_ref, dens_ref, low_ref, high_ref, vel_ref,
-                 pot_ref, out_ref, grid_ref):
+                 pot_ref, out_ref, grid_ref, v_ref, f_ref):
     step = pl.program_id(0)
 
     @pl.when(step == 0)
     def _():
         rows = rows_ref[...]
-        expanded = jnp.zeros((640, 128), jnp.float32)
         ordered = jnp.concatenate(
             [patch_ref[pl.ds(pl.multiple_of(flag_ref[j, 5] * 16, 16), 16), :] for j in range(PY)], axis=0)
+        expanded = jnp.zeros((640, 128), jnp.float32)
         for part in split3(ordered):
             expanded += dot(rows, part)
-        parts = split3(expanded)
+        pair = jnp.concatenate(split2(expanded), axis=1)
         for n in range(0, 2 * LANES, 256):
-            table = cols_ref[:, n:n + 256]
-            acc = dot(parts[0], table) + dot(parts[1], table) + dot(parts[2], table)
-            grid_ref[:, n:n + 256] = acc
+            grid_ref[:, n:n + 256] = dot(pair, cols_ref[:, n:n + 256])
 
     base = pl.multiple_of(step * 40, 8)
-    v0 = grid_ref[pl.ds(base, 32), :LANES]
-    edge = grid_ref[pl.ds(base, 32), LANES:]
-    faces = grid_ref[pl.ds(base + 32, 8), :LANES]
-    lane = lax.broadcasted_iota(jnp.int32, (32, LANES), 1)
-    row = lax.broadcasted_iota(jnp.int32, (32, LANES), 0)
-    third = lane % CELLS
-    low_face = jnp.broadcast_to(faces[0:1], (32, LANES))
-    high_face = jnp.broadcast_to(faces[1:2], (32, LANES))
-    first_row = row == 0
-    last_row = row == CELLS - 1
-    zero = jnp.zeros((32, LANES), jnp.float32)
-    density = jnp.concatenate([low_ref[0], dens_ref[0], high_ref[0]], axis=1)
-    fixed = edge + jnp.where(first_row, low_face, zero) + jnp.where(last_row, high_face, zero)
-    c = RELAX / 6.0
-    fixed = c * (fixed - density * (1.0 / (REF * REF)))
-    use_low = flag_ref[step, 0] > 0
-    use_high = flag_ref[step, 1] > 0
-    same_low = flag_ref[step, 2] > 0
-    same_high = flag_ref[step, 3] > 0
-    live = flag_ref[step, 4] > 0
-    in_low = lane < EDGE * CELLS
-    in_high = lane >= (EDGE + CELLS) * CELLS
-    held = (in_low & jnp.logical_not(use_low)) | (in_high & jnp.logical_not(use_high))
-    frozen_next = (lane >= (EDGE - 1) * CELLS) & in_low & jnp.logical_not(same_low)
-    frozen_prev = in_high & (lane < (EDGE + CELLS + 1) * CELLS) & jnp.logical_not(same_high)
-
-    def beside(v):
-        prev_third = jnp.where(third == 0, zero, pltpu.roll(v, 1, 1))
-        next_third = jnp.where(third == CELLS - 1, zero, pltpu.roll(v, LANES - 1, 1))
-        prev_first = jnp.where(first_row, zero, pltpu.roll(v, 1, 0))
-        next_first = jnp.where(last_row, zero, pltpu.roll(v, CELLS - 1, 0))
-        prev_second = pltpu.roll(v, CELLS, 1)
-        next_second = pltpu.roll(v, LANES - CELLS, 1)
-        return prev_first, next_first, prev_second, next_second, prev_third, next_third
-
-    start_prev = pltpu.roll(v0, CELLS, 1)
-    start_next = pltpu.roll(v0, LANES - CELLS, 1)
-    outer_low = lane < CELLS
-    outer_high = lane >= LANES - CELLS
-    v = v0
-    for _ in range(SWEEPS):
-        pf, nf, ps, ns, pt, nt = beside(v)
-        ps = jnp.where(outer_low, zero, jnp.where(frozen_prev, start_prev, ps))
-        ns = jnp.where(outer_high, zero, jnp.where(frozen_next, start_next, ns))
-        new = (1.0 - RELAX) * v + c * (pf + nf + ps + ns + pt + nt) + fixed
-        v = jnp.where(held, v, new)
-    pf, nf, ps, ns, pt, nt = beside(v)
-    own = slice(EDGE * CELLS, (EDGE + CELLS) * CELLS)
-    scale = REF / 2.0
-    slope_first = (nf + jnp.where(last_row, high_face, zero)) - (pf + jnp.where(first_row, low_face, zero))
-    slope_second = ns - ps
-    slope_third = (nt + jnp.where(third == CELLS - 1, edge, zero)) - (pt + jnp.where(third == 0, edge, zero))
-    pot_ref[0] = jnp.where(live, v[:, own], 0.0)
-    for q, slope in enumerate((slope_first, slope_second, slope_third)):
-        out_ref[q, 0] = jnp.where(live, vel_ref[q, 0] - slope[:, own] * scale, 0.0)
+    tiles = LANES // 128
+    lane = lax.broadcasted_iota(jnp.int32, (8, 128), 1)
+    third_first = lane % CELLS == 0
+    third_last = lane % CELLS == CELLS - 1
+    second_first = lane < CELLS
+    second_last = lane >= 128 - CELLS
+    zero = jnp.zeros((8, 128), jnp.float32)
+    use_low = jnp.broadcast_to(flag_ref[step, 0], (8, 128)) > 0
+    use_high = jnp.broadcast_to(flag_ref[step, 1], (8, 128)) > 0
+    same_low = jnp.broadcast_to(flag_ref[step, 2], (8, 128)) > 0
+    same_high = jnp.broadcast_to(flag_ref[step, 3], (8, 128)) > 0
+    live = jnp.broadcast_to(flag_ref[step, 4], (8, 128)) > 0
+
+    def start(t, r):
+        return grid_ref[pl.ds(base + r * 8, 8), t * 128:(t + 1) * 128]
+
+    def edge(t, r):
+        return grid_ref[pl.ds(base + r * 8, 8), LANES + t * 128:LANES + (t + 1) * 128]
+
+    def row_of(slot, t, r):
+        return (slot * tiles + t) * ROWS + 8 + r * 8
+
+    for t in range(tiles):
+        faces = grid_ref[pl.ds(base + 32, 8), t * 128:(t + 1) * 128]
+        for slot in range(2):
+            row = row_of(slot, t, 0)
+            v_ref[row - 1:row, :] = faces[0:1]
+            v_ref[row + CELLS:row + CELLS + 1, :] = faces[1:2]
+        for r in range(4):
+            rows = slice(r * 8, r * 8 + 8)
+            if t == 0:
+                rho = low_ref[0, rows, :]
+            elif t == tiles - 1:
+                rho = high_ref[0, rows, :]
+            else:
+                rho = dens_ref[0, rows, (t - 1) * 128:t * 128]
+            f_ref[t, r] = edge(t, r) - rho * (1.0 / (REF * REF))
+            row = row_of(0, t, r)
+            v_ref[row:row + 8, :] = start(t, r)
+
+    def second_neighbours(value, t, r):
+        here = value(t, r)
+        if t == 0:
+            before = zero
+        else:
+            before = pltpu.roll(value(t - 1, r), CELLS, 1)
+            if t == tiles - 1:
+                before = jnp.where(same_high, before, pltpu.roll(start(t - 1, r), CELLS, 1))
+        if t == tiles - 1:
+            after = zero
+        else:
+            after = pltpu.roll(value(t + 1, r), 128 - CELLS, 1)
+            if t == 0:
+                after = jnp.where(same_low, after, pltpu.roll(start(t + 1, r), 128 - CELLS, 1))
+        return (jnp.where(second_first, before, pltpu.roll(here, CELLS, 1)),
+                jnp.where(second_last, after, pltpu.roll(here, 128 - CELLS, 1)))
+
+    def first_neighbours(slot, t, r):
+        row = row_of(slot, t, r)
+        return v_ref[row - 1:row + 7, :], v_ref[row + 1:row + 9, :]
+
+    def third_neighbours(here, low, high):
+        return (jnp.where(third_first, low, pltpu.roll(here, 1, 1)),
+                jnp.where(third_last, high, pltpu.roll(here, 127, 1)))
+
+    def reader(slot):
+        return lambda t, r: v_ref[row_of(slot, t, r):row_of(slot, t, r) + 8, :]
+
+    for sweep in range(SWEEPS):
+        slot = sweep % 2
+        value = reader(slot)
+        for r in range(4):
+            for t in range(tiles):
+                here = value(t, r)
+                before, after = second_neighbours(value, t, r)
+                total = here + f_ref[t, r] + (before + after)
+                before, after = first_neighbours(slot, t, r)
+                total += before + after
+                before, after = third_neighbours(here, zero, zero)
+                total += before + after
+                new = total * (1.0 - RELAX)
+                if t == 0:
+                    new = jnp.where(use_low, new, here)
+                if t == tiles - 1:
+                    new = jnp.where(use_high, new, here)
+                row = row_of(1 - slot, t, r)
+                v_ref[row:row + 8, :] = new
+
+    slot = SWEEPS % 2
+    value = reader(slot)
+    for r in range(4):
+        for t in range(1, tiles - 1):
+            here = value(t, r)
+            rows = slice(r * 8, r * 8 + 8)
+            cols = slice((t - 1) * 128, t * 128)
+            pot_ref[0, rows, cols] = jnp.where(live, here, 0.0)
+            wall = edge(t, r)
+            pairs = (first_neighbours(slot, t, r), second_neighbours(value, t, r), third_neighbours(here, wall, wall))
+            for q, (before, after) in enumerate(pairs):
+                out_ref[q, 0, rows, cols] = jnp.where(live, vel_ref[q, 0, rows, cols] - (after - before) * (REF / 2.0), 0.0)
 
 
 def relax(flags, patch, density, low, high, velocity):
     slots = density.shape[0]
     rows, cols = interpolation_tables()
     block_rows = jnp.asarray(np.kron(np.eye(slots), rows), jnp.bfloat16)
-    table = jnp.asarray(cols, jnp.bfloat16)
+    table = jnp.asarray(np.concatenate([cols, cols]), jnp.bfloat16)
     whole = lambda shape: pl.BlockSpec(shape, lambda s, f: (0,) * len(shape), pipeline_mode=pl.Buffered(1))
     return pl.pallas_call(
         relax_kernel,
@@ -334,7 +446,7 @@
             in_specs=[
                 whole((slots * 16, 128)),
                 whole((slots * 40, slots * 16)),
-                whole((128, 2 * LANES)),
+                whole((256, 2 * LANES)),
                 pl.BlockSpec((1, CELLS, CELLS * CELLS), lambda s, f: (s, 0, 0)),
                 pl.BlockSpec((1, CELLS, EDGE * CELLS), lambda s, f: (s, 0, 0)),
                 pl.BlockSpec((1, CELLS, EDGE * CELLS), lambda s, f: (s, 0, 0)),
@@ -344,7 +456,11 @@
                 pl.BlockSpec((1, CELLS, CELLS * CELLS), lambda s, f: (s, 0, 0)),
                 pl.BlockSpec((3, 1, CELLS, CELLS * CELLS), lambda s, f: (0, s, 0, 0)),
             ],
-            scratch_shapes=[pltpu.VMEM((slots * 40, 2 * LANES), jnp.float32)],
+            scratch_shapes=[
+                pltpu.VMEM((slots * 40, 2 * LANES), jnp.float32),
+                pltpu.VMEM((2 * (LANES // 128) * ROWS, 128), jnp.float32),
+                pltpu.VMEM((LANES // 128, 4, 8, 128), jnp.float32),
+            ],
         ),
         out_shape=[
             jax.ShapeDtypeStruct(density.shape, jnp.float32),
@@ -366,10 +482,11 @@
     low = from_behind(subgrid_density[:, :, -EDGE * CELLS:], "py", 1)
     high = from_behind(subgrid_density[:, :, :EDGE * CELLS], "py", -1)
 
-    packed = jnp.einsum("xyz,zmt->tmyx", root_density, basis.reshape(NR, MODES, DEV), precision=HIGH)
-    got = lax.all_to_all(packed.reshape(DEV, MODES * YB * XB), ("px", "py"), 0, 0, tiled=True)
+    packed = forward_third(root_density, q).reshape(DEV, 1, MODES * YB * XB)
+    got = lax.all_to_all(packed, ("px", "py"), 0, 0, tiled=True).reshape(-1, 128)
     own_eig = eigen[jnp.arange(MODES) * DEV + device]
-    back = lax.all_to_all(solve_planes(own_eig, got, q, eig), ("px", "py"), 0, 0, tiled=True)
+    solved = solve_planes(own_eig, got, q, eig).reshape(DEV, 1, MODES * PLANE)
+    back = lax.all_to_all(solved, ("px", "py"), 0, 0, tiled=True).reshape(-1, 128)
 
     targets = jnp.arange(PY, dtype=jnp.int32)
     wanted = (place_first * PY + targets) * slots + (place_second - targets) % PY

time: 147 us -> 139 us (0.946)
  matrix products: 3.49 us -> 0 us
  waiting for transfers between devices: 44.9 us -> 41.5 us
  Pallas kernels: 47.5 us -> 45.1 us
  local copies, waits for them, and re-layouts: 20.3 us -> 22.6 us
    all_to_all x2 -> x0, local copies, waits for them, and re-layouts: 8.44 us -> none  [the longest x1 5.17 us: local(): lax.all_to_all(solve_planes(own_eig, got, q, eig), ('px', 'py'), 0, 0, ti...]
    unnamed x33 -> x43, local copies, waits for them, and re-layouts: 6.33 us -> 14.1 us
    dot_general x1 -> x0, matrix products: 3.49 us -> none  [local(): jnp.einsum('xyz,zmt->tmyx', root_density, basis.reshape(NR, MODES, DEV),...]
    all_to_all x2, waiting for transfers between devices: 44.3 us -> 40.9 us  [the longest x1 25.4 us: local(): lax.all_to_all(packed, ('px', 'py'), 0, 0, tiled=True).reshape(-1, 128)]
    pallas_call x1 -> x2, Pallas kernels: 12.8 us -> 11 us  [the longest x1 7.85 us: solve_planes(): pl.pallas_call(plane_kernel, out_shape=jax.ShapeDtypeStruct((DEV * MODES...]
    gather x2, local copies, waits for them, and re-layouts: 1.15 us -> 2.94 us  [local(): columns = basis[third.reshape(-1)].T]
  transfers between devices with their start and end apart: 5 -> 5, of which waited for: 3 -> 3; matrix products, arithmetic and copies ran while one was open for 6% -> 8% of each run, Pallas kernels for 5% -> 6%
where the time goes in v3:
time: 139 us; the launch traced here: 138 us
  Pallas kernels  45.1 us (32%)
  waiting for transfers between devices  41.5 us (30%)
  starting transfers between devices  26.9 us (19%)
  local copies, waits for them, and re-layouts  22.6 us (16%)
    pallas_call x1, Pallas kernels, relax(): pl.pallas_call(relax_kernel, grid_spec=pltpu.PrefetchScalarGridSpec(num_s...  26.2 us
    all_to_all x1, waiting for transfers between devices, local(): lax.all_to_all(packed, ('px', 'py'), 0, 0, tiled=True).reshape(-1, 128)  25.4 us
    all_to_all x1, waiting for transfers between devices, local(): lax.all_to_all(solved, ('px', 'py'), 0, 0, tiled=True).reshape(-1, 128)  15.5 us
    unnamed x43, local copies, waits for them, and re-layouts  14.1 us
    all_to_all x1, starting transfers between devices, local(): lax.all_to_all(packed, ('px', 'py'), 0, 0, tiled=True).reshape(-1, 128)  11.5 us
    pallas_call x1, Pallas kernels, solve_planes(): pl.pallas_call(plane_kernel, out_shape=jax.ShapeDtypeStruct((DEV * MODES...  7.85 us
    ppermute x2, starting transfers between devices, from_behind(): lax.ppermute(value, axis, [(source, source + steps) for source in range(i...  6.18 us
    all_to_all x1, starting transfers between devices, local(): lax.all_to_all(solved, ('px', 'py'), 0, 0, tiled=True).reshape(-1, 128)  4.99 us
  transfers between devices with their start and end apart: 5, of which 3 were waited for; matrix products, arithmetic and copies ran while one was open for 8% of the time, Pallas kernels for 6%

profile of v3, /device:TPU:1, one launch (start us, length us, event | category | flops | bytes accessed | tf_op | source)
XLA Modules:
  0.0 137.9 jit_solution(12177524030577997726)
XLA Ops:
  0.6 0.0 copy-start.5
  0.6 1.1 copy-done.5
  1.7 1.5 %copy-done.7 = f32[48,24,384]{2,1,0:T(8,128)S(1)} copy-done((f32[48,24,384]{2,1,0:T(8,128)S(1)}, f32[48,24,384]{2,1,0:T(8,128)}, u32[]{:S(2)}) %copy-start.7) | copy-done | bytes 1769496
  3.2 3.1 %forward_third.1 = f32[3456,128]{1,0:T(8,128)S(1)} custom-call(f32[48,24,384]{2,1,0:T(8,128)S(1)} %copy-done.7, bf16[2,384,384]{2,1,0:T(8,128)(2,1)S(1)} %copy-done.5), custom_call_target="tpu_custom_call" | custom-call | tf_op jit(solution)/shard_map/forward_third/pallas_call | solution.py:158
  6.3 0.0 copy-start.3
  6.3 1.2 copy-done.3
  7.5 0.0 copy-start.15
  7.6 11.5 %all-to-all-start = ((f32[128,1,3456]{2,1,0:T(1,128)}), f32[128,1,3456]{2,1,0:T(1,128)S(1)}, u32[]{:S(2)}, u32[]{:S(2)}) async-start(f32[128,1,3456]{2,1,0:T(1,128)} %bitcast.26), calls=%async_computation | async-start | bytes 3538944 | tf_op jit(solution)/shard_map/all_to_all | solution.py:486
  19.1 0.6 gather_fusion
  19.8 25.4 %all-to-all-done = f32[128,1,3456]{2,1,0:T(1,128)S(1)} async-done(((f32[128,1,3456]{2,1,0:T(1,128)}), f32[128,1,3456]{2,1,0:T(1,128)S(1)}, u32[]{:S(2)}, u32[]{:S(2)}) %all-to-all-start) | async-done | bytes 1769504 | tf_op jit(solution)/shard_map/all_to_all | solution.py:486
  45.1 1.2 copy-done.1
  46.4 1.5 %copy-done.2 = f32[128,1,3456]{2,1,0:T(1,128)S(1)} copy-done((f32[128,1,3456]{2,1,0:T(1,128)S(1)}, f32[128,1,3456]{2,1,0:T(1,128)}, u32[]{:S(2)}) %copy-start.2) | copy-done | bytes 1769496
  47.8 1.0 copy-done.11
  48.9 1.0 copy-done.12
  49.9 7.8 %solve_planes.1 = f32[4224,128]{1,0:T(8,128)S(1)} custom-call(f32[3]{0:T(128)S(1)} %gather_fusion, f32[3456,128]{1,0:T(8,128)S(1)} %bitcast.25, bf16[2,2,256,256]{3,2,1,0:T(8,128)(2,1)S(1)} %copy-done.10, bf16[2,2,192,192]{3,2,1,0:T(8,128)(2,1)S(1)} %copy-done.12, bf16[2,2,224,192]{3,2,1,0:T(8,128)(2,1)S(1)} %copy-done.11, ...), custom_call_target="tpu_custom_call" | custom-call | tf_op jit(solution)/shard_map/solve_planes/pallas_call | solution.py:242
  57.7 0.0 copy-start
  57.7 1.3 copy-done
  59.1 5.0 %all-to-all-start.1 = ((f32[128,1,4224]{2,1,0:T(1,128)}), f32[128,1,4224]{2,1,0:T(1,128)S(1)}, u32[]{:S(2)}, u32[]{:S(2)}) async-start(f32[128,1,4224]{2,1,0:T(1,128)} %bitcast.24), calls=%async_computation.1 | async-start | bytes 4325376 | tf_op jit(solution)/shard_map/all_to_all | solution.py:489
  64.1 0.0 copy-start.19
  64.1 0.0 copy-start.17
  64.1 1.9 %fusion.16 = (f32[16,32,128]{2,1,0:T(8,128)}, f32[16,32,128]{2,1,0:T(8,128)}) fusion(f32[16,32,1024]{2,1,0:T(8,128)} %dens_ref.1), kind=kLoop, calls=%fused_computation.45 | loop fusion | bytes 1048576 | tf_op jit(solution)/shard_map/slice | solution.py:483
  66.0 1.3 collective-permute-start.1
  67.3 4.9 %collective-permute-start = (f32[16,32,128]{2,1,0:T(8,128)}, f32[16,32,128]{2,1,0:T(8,128)}, u32[]{:S(2)}, u32[]{:S(2)}) collective-permute-start(f32[16,32,128]{2,1,0:T(8,128)} %get-tuple-element.8), channel_id=1, source_target_pairs={{0,1},{1,2},{2,3},{3,4},{4,5},{5,6},{6,7},{7,8},{8,9},{9,10},{10,1... | collective-permute-start | bytes 786440 | tf_op jit(solution)/shard_map/ppermute | solution.py:83
  72.2 1.3 copy.45
  73.5 0.1 fusion.3
  73.7 1.8 %gather_fusion.1 = s32[16,3]{1,0:T(8,128)S(1)} fusion(s32[3,2048]{0,1:T(8,128)} %copy.45, s32[1024]{0:T(1024)S(1)} %pad_clamp_fusion.1), kind=kCustom, calls=%fused_computation.1 | custom fusion | bytes 448 | tf_op jit(solution)/shard_map/gather | solution.py:493
  75.5 0.1 copy.46
  75.5 0.1 add_remainder_fusion
  75.6 0.1 rem.73
  75.7 0.1 pad_dynamic-slice_fusion
  75.9 1.7 %gather_fusion.2 = f32[256,384]{1,0:T(8,128)} fusion(f32[384,384]{1,0:T(8,128)S(1)} %copy-done.17, s32[1024]{0:T(1024)S(1)} %pad_clamp_fusion), kind=kCustom, calls=%fused_computation.2 | custom fusion | bytes 787456 | tf_op jit(solution)/shard_map/gather | solution.py:495
  77.6 1.2 copy.47
  78.8 15.5 %all-to-all-done.1 = f32[128,1,4224]{2,1,0:T(1,128)S(1)} async-done(((f32[128,1,4224]{2,1,0:T(1,128)}), f32[128,1,4224]{2,1,0:T(1,128)S(1)}, u32[]{:S(2)}, u32[]{:S(2)}) %all-to-all-start.1) | async-done | bytes 2162720 | tf_op jit(solution)/shard_map/all_to_all | solution.py:489
  94.4 3.5 %cut_patches.1 = f32[256,128]{1,0:T(8,128)} custom-call(s32[2,16]{1,0:T(2,128)S(1)} %pad_add_fusion.start_ref, f32[4224,128]{1,0:T(8,128)S(1)} %bitcast.22, f32[384,256]{1,0:T(8,128)S(1)} %bitcast.27), custom_call_target="tpu_custom_call" | custom-call | tf_op jit(solution)/shard_map/cut_patches/pallas_call | solution.py:285
  97.9 4.2 %all-to-all-start.2 = ((f32[16,16,128]{2,1,0:T(8,128)}), f32[16,16,128]{2,1,0:T(8,128)S(1)}, u32[]{:S(2)}, u32[]{:S(2)}) async-start(f32[16,16,128]{2,1,0:T(8,128)} %bitcast.14), calls=%async_computation.2 | async-start | bytes 262144 | tf_op jit(solution)/shard_map/all_to_all | solution.py:499
  102.2 0.1 copy.42
  102.2 0.1 copy.44
  102.3 0.1 copy.41
  102.4 0.1 copy.43
  102.5 0.6 dynamic_slice.15
  103.1 0.6 fusion.10
  103.7 0.1 stack.62.flag_ref
  103.8 0.0 copy-start.13
  103.8 4.4 %block_of.1 = f32[48,24,384]{2,1,0:T(8,128)} custom-call(f32[4224,128]{1,0:T(8,128)S(1)} %bitcast.23, bf16[2,384,384]{2,1,0:T(8,128)(2,1)S(1)} %copy-done.6), custom_call_target="tpu_custom_call" | custom-call | tf_op jit(solution)/shard_map/block_of/pallas_call | solution.py:306
  108.2 0.6 all-to-all-done.2
  108.8 1.6 %copy-done.4 = f32[16,32,1024]{2,1,0:T(8,128)S(1)} copy-done((f32[16,32,1024]{2,1,0:T(8,128)S(1)}, f32[16,32,1024]{2,1,0:T(8,128)}, u32[]{:S(2)}) %copy-start.4) | copy-done | bytes 2097176
  110.4 1.3 copy-done.8
  111.7 26.2 %relax_and_kick.1 = (f32[16,32,1024]{2,1,0:T(8,128)}, f32[3,16,32,1024]{3,2,1,0:T(8,128)}) custom-call(s32[16,6]{1,0:T(8,128)S(1)} %stack.62.flag_ref, f32[256,128]{1,0:T(8,128)S(1)} %bitcast.28, bf16[640,256]{1,0:T(8,128)(2,1)S(1)} %copy-done.13, bf16[256,2560]{1,0:T(8,128)(2,1)S(1)} %copy-done.8, f32[16,32,1024]{2,1,0:T(8,128)S(1)} %copy-done.4, ...), custom_call_target="tpu_custom_call" | custom-call | tf_op jit(solution)/shard_map/relax_and_kick/pallas_call | solution.py:441
  (37 shorter events, 0.1 us)
Async XLA Ops:
  0.6 1.1 copy-start.5
  1.7 1.5 %copy-start.7 = (f32[48,24,384]{2,1,0:T(8,128)S(1)}, f32[48,24,384]{2,1,0:T(8,128)}, u32[]{:S(2)}) copy-start(f32[48,24,384]{2,1,0:T(8,128)} %in_ref.1) | copy-start | bytes 5308420
  6.3 1.2 copy-start.3
  7.5 11.6 %copy-start.16 = (f32[384]{0:T(512)S(1)}, f32[384]{0:T(512)}, u32[]{:S(2)}) copy-start(f32[384]{0:T(512)} %constant.100.clone) | copy-start | bytes 4612
  7.5 38.8 %copy-start.9 = (bf16[2,2,256,256]{3,2,1,0:T(8,128)(2,1)S(1)}, bf16[2,2,256,256]{3,2,1,0:T(8,128)(2,1)}, u32[]{:S(2)}) copy-start(bf16[2,2,256,256]{3,2,1,0:T(8,128)(2,1)} %constant.130.bx_ref) | copy-start | bytes 1572868
  7.5 38.8 %copy-start.10 = (bf16[2,2,256,256]{3,2,1,0:T(8,128)(2,1)S(1)}, bf16[2,2,256,256]{3,2,1,0:T(8,128)(2,1)}, u32[]{:S(2)}) copy-start(bf16[2,2,256,256]{3,2,1,0:T(8,128)(2,1)} %constant.121.ax_ref) | copy-start | bytes 1572868
  7.5 38.8 %copy-start.14 = (f32[2,192,1]{2,1,0:T(8,128)S(1)}, f32[2,192,1]{2,1,0:T(8,128)}, u32[]{:S(2)}) copy-start(f32[2,192,1]{2,1,0:T(8,128)} %constant.110.clone.ey_ref) | copy-start | bytes 4612
  7.5 38.8 %copy-start.15 = (f32[1,512]{1,0:T(1,128)S(1)}, f32[1,512]{1,0:T(1,128)}, u32[]{:S(2)}) copy-start(f32[1,512]{1,0:T(1,128)} %constant.111.clone.ex_ref) | copy-start | bytes 6148
  7.6 37.6 %all-to-all-start = ((f32[128,1,3456]{2,1,0:T(1,128)}), f32[128,1,3456]{2,1,0:T(1,128)S(1)}, u32[]{:S(2)}, u32[]{:S(2)}) async-start(f32[128,1,3456]{2,1,0:T(1,128)} %bitcast.26), calls=%async_computation | async-start | bytes 3538944 | tf_op jit(solution)/shard_map/all_to_all | solution.py:486
  45.1 1.2 copy-start.1
  46.4 1.5 %copy-start.2 = (f32[128,1,3456]{2,1,0:T(1,128)S(1)}, f32[128,1,3456]{2,1,0:T(1,128)}, u32[]{:S(2)}) copy-start(f32[128,1,3456]{2,1,0:T(1,128)} %copy-done.1) | copy-start | bytes 5308420
  47.8 1.0 copy-start.11
  48.9 1.0 copy-start.12
  57.7 1.3 copy-start
  59.1 13.1 %copy-start.18 = (s32[3,2048]{1,0:T(4,128)S(1)}, s32[3,2048]{1,0:T(4,128)}, u32[]{:S(2)}) copy-start(s32[3,2048]{1,0:T(4,128)} %param.25) | copy-start | bytes 73732
  59.1 35.3 %all-to-all-start.1 = ((f32[128,1,4224]{2,1,0:T(1,128)}), f32[128,1,4224]{2,1,0:T(1,128)S(1)}, u32[]{:S(2)}, u32[]{:S(2)}) async-start(f32[128,1,4224]{2,1,0:T(1,128)} %bitcast.24), calls=%async_computation.1 | async-start | bytes 4325376 | tf_op jit(solution)/shard_map/all_to_all | solution.py:489
  64.1 11.7 %copy-start.19 = (s32[2,2048]{1,0:T(2,128)S(1)}, s32[2,2048]{1,0:T(2,128)}, u32[]{:S(2)}) copy-start(s32[2,2048]{1,0:T(2,128)} %param.27) | copy-start | bytes 49156
  64.1 11.8 %copy-start.17 = (f32[384,384]{1,0:T(8,128)S(1)}, f32[384,384]{1,0:T(8,128)}, u32[]{:S(2)}) copy-start(f32[384,384]{1,0:T(8,128)} %constant.99.clone) | copy-start | bytes 1769476
  66.0 42.2 %collective-permute-start.1 = (f32[16,32,128]{2,1,0:T(8,128)}, f32[16,32,128]{2,1,0:T(8,128)S(1)}, u32[]{:S(2)}, u32[]{:S(2)}) collective-permute-start(f32[16,32,128]{2,1,0:T(8,128)} %get-tuple-element.7), channel_id=1, source_target_pairs={{1,0},{2,1},{3,2},{4,3},{5,4},{6,5},{7,6},{8,7},{9,8},{10,9},{11,1... | collective-permute-start | bytes 786440 | tf_op jit(solution)/shard_map/ppermute | solution.py:83
  67.3 40.9 %collective-permute-start = (f32[16,32,128]{2,1,0:T(8,128)}, f32[16,32,128]{2,1,0:T(8,128)}, u32[]{:S(2)}, u32[]{:S(2)}) collective-permute-start(f32[16,32,128]{2,1,0:T(8,128)} %get-tuple-element.8), channel_id=1, source_target_pairs={{0,1},{1,2},{2,3},{3,4},{4,5},{5,6},{6,7},{7,8},{8,9},{9,10},{10,1... | collective-permute-start | bytes 786440 | tf_op jit(solution)/shard_map/ppermute | solution.py:83
  77.6 24.9 %copy-start.20 = (s32[128]{0:T(128)S(1)}, s32[128]{0:T(128)}, u32[]{:S(2)}) copy-start(s32[128]{0:T(128)} %param.26) | copy-start | bytes 1540
  77.6 26.2 %copy-start.6 = (bf16[2,384,384]{2,1,0:T(8,128)(2,1)S(1)}, bf16[2,384,384]{2,1,0:T(8,128)(2,1)}, u32[]{:S(2)}) copy-start(bf16[2,384,384]{2,1,0:T(8,128)(2,1)} %constant.101.clone.q_ref) | copy-start | bytes 1769476
  97.9 10.9 %all-to-all-start.2 = ((f32[16,16,128]{2,1,0:T(8,128)}), f32[16,16,128]{2,1,0:T(8,128)S(1)}, u32[]{:S(2)}, u32[]{:S(2)}) async-start(f32[16,16,128]{2,1,0:T(8,128)} %bitcast.14), calls=%async_computation.2 | async-start | bytes 262144 | tf_op jit(solution)/shard_map/all_to_all | solution.py:499
  103.8 5.0 %copy-start.13 = (bf16[640,256]{1,0:T(8,128)(2,1)S(1)}, bf16[640,256]{1,0:T(8,128)(2,1)}, u32[]{:S(2)}) copy-start(bf16[640,256]{1,0:T(8,128)(2,1)} %constant.112.clone.rows_ref) | copy-start | bytes 983044
  108.8 1.6 %copy-start.4 = (f32[16,32,1024]{2,1,0:T(8,128)S(1)}, f32[16,32,1024]{2,1,0:T(8,128)}, u32[]{:S(2)}) copy-start(f32[16,32,1024]{2,1,0:T(8,128)} %dens_ref.1) | copy-start | bytes 6291460
  110.4 1.3 copy-start.8

commit v4 on v3

--- a/solution.py
+++ b/solution.py
@@ -83,6 +83,14 @@
     return lax.ppermute(value, axis, [(source, source + steps) for source in range(initial, last)])
 
 
+def in_hbm(x):
+    return pltpu.with_memory_space_constraint(x, pltpu.HBM)
+
+
+def in_vmem(x):
+    return pltpu.with_memory_space_constraint(x, pltpu.VMEM)
+
+
 def split3(x):
     hi = x.astype(jnp.bfloat16)
     rest = x - hi.astype(jnp.float32)
@@ -136,34 +144,39 @@
         begin = end
 
 
-def forward_kernel(in_ref, q_ref, out_ref, rows_ref, sem):
+def forward_kernel(in_ref, q_hbm, out_ref, rows_ref, q_ref, sem):
     copies = [pltpu.make_async_copy(in_ref.at[:, y], rows_ref.at[y], sem.at[y]) for y in range(YB)]
+    table = pltpu.make_async_copy(q_hbm, q_ref, sem.at[YB])
+    table.start()
     for copy in copies:
         copy.start()
-    for copy in copies:
-        copy.wait()
-    hi, low = split2(rows_ref[...].reshape(YB * XB, NR))
+    table.wait()
     contract = (((1,), (1,)), ((), ()))
-    modes = None
-    for left, right in ((q_ref[0], hi), (q_ref[0], low), (q_ref[1], hi)):
-        part = lax.dot_general(left, right, contract, preferred_element_type=jnp.float32)
-        modes = part if modes is None else modes + part
-    for m in range(MODES):
-        for c in range(TILES_IN):
-            out_ref[pl.ds(m * TILES_IN + c, DEV, stride=MODES * TILES_IN), :] = (
-                modes[m * DEV:(m + 1) * DEV, c * 128:(c + 1) * 128])
+    for part in range(3):
+        for copy in copies[part * 8:(part + 1) * 8]:
+            copy.wait()
+        hi, low = split2(rows_ref[part * 8:(part + 1) * 8].reshape(8 * XB, NR))
+        modes = None
+        for left, right in ((q_ref[0], hi), (q_ref[0], low), (q_ref[1], hi)):
+            term = lax.dot_general(left, right, contract, preferred_element_type=jnp.float32)
+            modes = term if modes is None else modes + term
+        for m in range(MODES):
+            for c in range(3):
+                out_ref[pl.ds(m * TILES_IN + part * 3 + c, DEV, stride=MODES * TILES_IN), :] = (
+                    modes[m * DEV:(m + 1) * DEV, c * 128:(c + 1) * 128])
 
 
 def forward_third(density, q):
     return pl.pallas_call(
         forward_kernel,
-        out_shape=jax.ShapeDtypeStruct((DEV * MODES * TILES_IN, 128), jnp.float32),
-        in_specs=[pl.BlockSpec(memory_space=pl.ANY), pl.BlockSpec(memory_space=pltpu.VMEM)],
+        out_shape=pltpu.HBM((DEV * MODES * TILES_IN, 128), jnp.float32),
+        in_specs=[pl.BlockSpec(memory_space=pltpu.HBM), pl.BlockSpec(memory_space=pltpu.HBM)],
         out_specs=pl.BlockSpec(memory_space=pltpu.VMEM),
-        scratch_shapes=[pltpu.VMEM((YB, XB, NR), jnp.float32), pltpu.SemaphoreType.DMA((YB,))],
-        compiler_params=pltpu.CompilerParams(vmem_limit_bytes=48 << 20),
+        scratch_shapes=[pltpu.VMEM((YB, XB, NR), jnp.float32), pltpu.VMEM((2, NR, NR), jnp.bfloat16),
+                        pltpu.SemaphoreType.DMA((YB + 1,))],
+        compiler_params=pltpu.CompilerParams(vmem_limit_bytes=16 << 20),
         name="forward_third",
-    )(density, table_pair(q.T))
+    )(in_hbm(density), in_hbm(table_pair(q.T)))
 
 
 def plane_kernel(mode_ref, in_ref, ax_ref, ay_ref, by_ref, bx_ref, ey_ref, ex_ref, out_ref, x_ref, o_ref):
@@ -241,13 +254,13 @@
     vmem = pl.BlockSpec(memory_space=pltpu.VMEM)
     return pl.pallas_call(
         plane_kernel,
-        out_shape=jax.ShapeDtypeStruct((DEV * MODES * TILES_OUT, 128), jnp.float32),
+        out_shape=pltpu.HBM((DEV * MODES * TILES_OUT, 128), jnp.float32),
         in_specs=[pl.BlockSpec(memory_space=pltpu.SMEM)] + [vmem] * 7,
         out_specs=vmem,
         scratch_shapes=[pltpu.VMEM((MODES, NR, 512), jnp.float32), pltpu.VMEM((MODES, YE * PY, 512), jnp.float32)],
-        compiler_params=pltpu.CompilerParams(vmem_limit_bytes=48 << 20),
+        compiler_params=pltpu.CompilerParams(vmem_limit_bytes=20 << 20),
         name="solve_planes",
-    )(own_eig, got, *tables, jnp.asarray(ey, jnp.float32), jnp.asarray(ex, jnp.float32))
+    )(own_eig, in_vmem(got), *tables, jnp.asarray(ey, jnp.float32), jnp.asarray(ex, jnp.float32))
 
 
 def columns_of(s_ref, pair):
@@ -290,7 +303,7 @@
                   pl.BlockSpec(memory_space=pltpu.VMEM)],
         out_specs=pl.BlockSpec(memory_space=pltpu.VMEM),
         scratch_shapes=[pltpu.VMEM((YE, 56, 256), jnp.float32)],
-        compiler_params=pltpu.CompilerParams(vmem_limit_bytes=48 << 20),
+        compiler_params=pltpu.CompilerParams(vmem_limit_bytes=12 << 20),
         name="cut_patches",
     )(starts, spectrum, columns)
 
@@ -308,14 +321,29 @@
         out_shape=jax.ShapeDtypeStruct((XB, YB, NR), jnp.float32),
         in_specs=[pl.BlockSpec(memory_space=pltpu.VMEM), pl.BlockSpec(memory_space=pltpu.VMEM)],
         out_specs=pl.BlockSpec(memory_space=pltpu.VMEM),
-        compiler_params=pltpu.CompilerParams(vmem_limit_bytes=48 << 20),
+        compiler_params=pltpu.CompilerParams(vmem_limit_bytes=14 << 20),
         name="block_of",
     )(spectrum, table_pair(q.T))
 
 
-def relax_kernel(flag_ref, patch_ref, rows_ref, cols_ref, dens_ref, low_ref, high_ref, vel_ref,
-                 pot_ref, out_ref, grid_ref, v_ref, f_ref):
+def relax_kernel(flag_ref, patch_ref, rows_ref, cols_ref, dens_hbm, low_ref, high_ref, vel_hbm,
+                 pot_hbm, out_hbm, grid_ref, v_ref, f_ref, dens_ref, vel_ref, in_sem, out_sem):
     step = pl.program_id(0)
+    slots = pl.num_programs(0)
+
+    def arrivals(s):
+        return (pltpu.make_async_copy(dens_hbm.at[s], dens_ref.at[s], in_sem.at[0, s]),
+                pltpu.make_async_copy(vel_hbm.at[:, s], vel_ref.at[:, s], in_sem.at[1, s]))
+
+    def departures(s):
+        return (pltpu.make_async_copy(dens_ref.at[s], pot_hbm.at[s], out_sem.at[0, s]),
+                pltpu.make_async_copy(vel_ref.at[:, s], out_hbm.at[:, s], out_sem.at[1, s]))
+
+    @pl.when(step == 0)
+    def _():
+        for s in range(PY):
+            for copy in arrivals(s):
+                copy.start()
 
     @pl.when(step == 0)
     def _():
@@ -327,8 +355,11 @@
             expanded += dot(rows, part)
         pair = jnp.concatenate(split2(expanded), axis=1)
         for n in range(0, 2 * LANES, 256):
-            grid_ref[:, n:n + 256] = dot(pair, cols_ref[:, n:n + 256])
-
+            table = cols_ref[:, n:n + 256]
+            grid_ref[:, n:n + 256] = dot(pair, jnp.concatenate([table, table], axis=0))
+
+    for copy in arrivals(step):
+        copy.wait()
     base = pl.multiple_of(step * 40, 8)
     tiles = LANES // 128
     lane = lax.broadcasted_iota(jnp.int32, (8, 128), 1)
@@ -361,31 +392,24 @@
         for r in range(4):
             rows = slice(r * 8, r * 8 + 8)
             if t == 0:
-                rho = low_ref[0, rows, :]
+                rho = low_ref[step, rows, :]
             elif t == tiles - 1:
-                rho = high_ref[0, rows, :]
+                rho = high_ref[step, rows, :]
             else:
-                rho = dens_ref[0, rows, (t - 1) * 128:t * 128]
+                rho = dens_ref[step, rows, (t - 1) * 128:t * 128]
             f_ref[t, r] = edge(t, r) - rho * (1.0 / (REF * REF))
             row = row_of(0, t, r)
             v_ref[row:row + 8, :] = start(t, r)
 
-    def second_neighbours(value, t, r):
-        here = value(t, r)
-        if t == 0:
-            before = zero
-        else:
-            before = pltpu.roll(value(t - 1, r), CELLS, 1)
-            if t == tiles - 1:
-                before = jnp.where(same_high, before, pltpu.roll(start(t - 1, r), CELLS, 1))
-        if t == tiles - 1:
-            after = zero
-        else:
-            after = pltpu.roll(value(t + 1, r), 128 - CELLS, 1)
-            if t == 0:
-                after = jnp.where(same_low, after, pltpu.roll(start(t + 1, r), 128 - CELLS, 1))
-        return (jnp.where(second_first, before, pltpu.roll(here, CELLS, 1)),
-                jnp.where(second_last, after, pltpu.roll(here, 128 - CELLS, 1)))
+    def second_neighbours(values, r):
+        up = [pltpu.roll(value, CELLS, 1) for value in values]
+        down = [pltpu.roll(value, 128 - CELLS, 1) for value in values]
+        into_high = jnp.where(same_high, up[-2], pltpu.roll(start(tiles - 2, r), CELLS, 1))
+        into_low = jnp.where(same_low, down[1], pltpu.roll(start(1, r), 128 - CELLS, 1))
+        befores = [zero] + up[:-2] + [into_high]
+        afters = [into_low] + down[2:] + [zero]
+        return ([jnp.where(second_first, before, here) for before, here in zip(befores, up)],
+                [jnp.where(second_last, after, here) for after, here in zip(afters, down)])
 
     def first_neighbours(slot, t, r):
         row = row_of(slot, t, r)
@@ -402,10 +426,10 @@
         slot = sweep % 2
         value = reader(slot)
         for r in range(4):
-            for t in range(tiles):
-                here = value(t, r)
-                before, after = second_neighbours(value, t, r)
-                total = here + f_ref[t, r] + (before + after)
+            values = [value(t, r) for t in range(tiles)]
+            befores, afters = second_neighbours(values, r)
+            for t, here in enumerate(values):
+                total = here + f_ref[t, r] + (befores[t] + afters[t])
                 before, after = first_neighbours(slot, t, r)
                 total += before + after
                 before, after = third_neighbours(here, zero, zero)
@@ -421,22 +445,33 @@
     slot = SWEEPS % 2
     value = reader(slot)
     for r in range(4):
+        values = [value(t, r) for t in range(tiles)]
+        befores, afters = second_neighbours(values, r)
         for t in range(1, tiles - 1):
-            here = value(t, r)
+            here = values[t]
             rows = slice(r * 8, r * 8 + 8)
             cols = slice((t - 1) * 128, t * 128)
-            pot_ref[0, rows, cols] = jnp.where(live, here, 0.0)
+            dens_ref[step, rows, cols] = jnp.where(live, here, 0.0)
             wall = edge(t, r)
-            pairs = (first_neighbours(slot, t, r), second_neighbours(value, t, r), third_neighbours(here, wall, wall))
+            pairs = (first_neighbours(slot, t, r), (befores[t], afters[t]), third_neighbours(here, wall, wall))
             for q, (before, after) in enumerate(pairs):
-                out_ref[q, 0, rows, cols] = jnp.where(live, vel_ref[q, 0, rows, cols] - (after - before) * (REF / 2.0), 0.0)
+                kicked = vel_ref[q, step, rows, cols] - (after - before) * (REF / 2.0)
+                vel_ref[q, step, rows, cols] = jnp.where(live, kicked, 0.0)
+    for copy in departures(step):
+        copy.start()
+
+    @pl.when(step == slots - 1)
+    def _():
+        for s in range(PY):
+            for copy in departures(s):
+                copy.wait()
 
 
 def relax(flags, patch, density, low, high, velocity):
     slots = density.shape[0]
     rows, cols = interpolation_tables()
     block_rows = jnp.asarray(np.kron(np.eye(slots), rows), jnp.bfloat16)
-    table = jnp.asarray(np.concatenate([cols, cols]), jnp.bfloat16)
+    table = jnp.asarray(cols, jnp.bfloat16)
     whole = lambda shape: pl.BlockSpec(shape, lambda s, f: (0,) * len(shape), pipeline_mode=pl.Buffered(1))
     return pl.pallas_call(
         relax_kernel,
@@ -446,29 +481,30 @@
             in_specs=[
                 whole((slots * 16, 128)),
                 whole((slots * 40, slots * 16)),
-                whole((256, 2 * LANES)),
-                pl.BlockSpec((1, CELLS, CELLS * CELLS), lambda s, f: (s, 0, 0)),
-                pl.BlockSpec((1, CELLS, EDGE * CELLS), lambda s, f: (s, 0, 0)),
-                pl.BlockSpec((1, CELLS, EDGE * CELLS), lambda s, f: (s, 0, 0)),
-                pl.BlockSpec((3, 1, CELLS, CELLS * CELLS), lambda s, f: (0, s, 0, 0)),
+                whole((128, 2 * LANES)),
+                pl.BlockSpec(memory_space=pltpu.HBM),
+                pl.BlockSpec(memory_space=pltpu.VMEM),
+                pl.BlockSpec(memory_space=pltpu.VMEM),
+                pl.BlockSpec(memory_space=pltpu.HBM),
             ],
-            out_specs=[
-                pl.BlockSpec((1, CELLS, CELLS * CELLS), lambda s, f: (s, 0, 0)),
-                pl.BlockSpec((3, 1, CELLS, CELLS * CELLS), lambda s, f: (0, s, 0, 0)),
-            ],
+            out_specs=[pl.BlockSpec(memory_space=pltpu.HBM), pl.BlockSpec(memory_space=pltpu.HBM)],
             scratch_shapes=[
                 pltpu.VMEM((slots * 40, 2 * LANES), jnp.float32),
                 pltpu.VMEM((2 * (LANES // 128) * ROWS, 128), jnp.float32),
                 pltpu.VMEM((LANES // 128, 4, 8, 128), jnp.float32),
+                pltpu.VMEM((slots, CELLS, CELLS * CELLS), jnp.float32),
+                pltpu.VMEM((3, slots, CELLS, CELLS * CELLS), jnp.float32),
+                pltpu.SemaphoreType.DMA((2, slots)),
+                pltpu.SemaphoreType.DMA((2, slots)),
             ],
         ),
         out_shape=[
-            jax.ShapeDtypeStruct(density.shape, jnp.float32),
-            jax.ShapeDtypeStruct(velocity.shape, jnp.float32),
+            pltpu.HBM((slots, CELLS, CELLS * CELLS), jnp.float32),
+            pltpu.HBM((3, slots, CELLS, CELLS * CELLS), jnp.float32),
         ],
-        compiler_params=pltpu.CompilerParams(vmem_limit_bytes=48 << 20),
+        compiler_params=pltpu.CompilerParams(vmem_limit_bytes=22 << 20),
         name="relax_and_kick",
-    )(flags, patch, block_rows, table, density, low, high, velocity)
+    )(flags, patch, block_rows, table, in_hbm(density), low, high, in_hbm(velocity))
 
 
 def local(root_density, subgrid_density, velocity, slot_anchor, slot_count, neighbour):
@@ -482,7 +518,8 @@
     low = from_behind(subgrid_density[:, :, -EDGE * CELLS:], "py", 1)
     high = from_behind(subgrid_density[:, :, :EDGE * CELLS], "py", -1)
 
-    packed = forward_third(root_density, q).reshape(DEV, 1, MODES * YB * XB)
+    packed = forward_third(root_density, q)
+    packed = packed.reshape(DEV, 1, MODES * YB * XB)
     got = lax.all_to_all(packed, ("px", "py"), 0, 0, tiled=True).reshape(-1, 128)
     own_eig = eigen[jnp.arange(MODES) * DEV + device]
     solved = solve_planes(own_eig, got, q, eig).reshape(DEV, 1, MODES * PLANE)

time: 139 us -> 126 us (0.906)
  local copies, waits for them, and re-layouts: 22.6 us -> 10.1 us
  Pallas kernels: 45.1 us -> 42.7 us
    unnamed x43 -> x31, local copies, waits for them, and re-layouts: 14.1 us -> 3.39 us
    pallas_call x1, Pallas kernels: 26.2 us -> 20.4 us  [relax(): pl.pallas_call(relax_kernel, grid_spec=pltpu.PrefetchScalarGridSpec(num_s...]
    pallas_call x2, Pallas kernels: 11 us -> 14.4 us  [the longest x1 9.2 us: solve_planes(): pl.pallas_call(plane_kernel, out_shape=pltpu.HBM((DEV * MODES * TILES_OUT...]
    gather x2, local copies, waits for them, and re-layouts: 2.94 us -> 1.15 us  [local(): columns = basis[third.reshape(-1)].T]
where the time goes in v4:
time: 126 us; the launch traced here: 125 us
  waiting for transfers between devices  42.8 us (34%)
  Pallas kernels  42.7 us (34%)
  starting transfers between devices  26.9 us (21%)
  local copies, waits for them, and re-layouts  10.1 us (8%)
  other arithmetic  1.44 us (1%)
    all_to_all x1, waiting for transfers between devices, local(): lax.all_to_all(packed, ('px', 'py'), 0, 0, tiled=True).reshape(-1, 128)  25.4 us
    pallas_call x1, Pallas kernels, relax(): pl.pallas_call(relax_kernel, grid_spec=pltpu.PrefetchScalarGridSpec(num_s...  20.4 us
    all_to_all x1, waiting for transfers between devices, local(): lax.all_to_all(solved, ('px', 'py'), 0, 0, tiled=True).reshape(-1, 128)  16.8 us
    all_to_all x1, starting transfers between devices, local(): lax.all_to_all(packed, ('px', 'py'), 0, 0, tiled=True).reshape(-1, 128)  11.5 us
    pallas_call x1, Pallas kernels, solve_planes(): pl.pallas_call(plane_kernel, out_shape=pltpu.HBM((DEV * MODES * TILES_OUT...  9.2 us
    ppermute x2, starting transfers between devices, from_behind(): lax.ppermute(value, axis, [(source, source + steps) for source in range(i...  6.17 us
    pallas_call x1, Pallas kernels, forward_third(): pl.pallas_call(forward_kernel, out_shape=pltpu.HBM((DEV * MODES * TILES_I...  5.23 us
    all_to_all x1, starting transfers between devices, local(): lax.all_to_all(solved, ('px', 'py'), 0, 0, tiled=True).reshape(-1, 128)  4.99 us
  transfers between devices with their start and end apart: 5, of which 3 were waited for; matrix products, arithmetic and copies ran while one was open for 8% of the time, Pallas kernels for 6%

profile of v4, /device:TPU:1, one launch (start us, length us, event | category | flops | bytes accessed | tf_op | source)
XLA Modules:
  0.0 125.1 jit_solution(12831237041810859213)
XLA Ops:
  0.6 5.2 %forward_third.1 = f32[3456,128]{1,0:T(8,128)} custom-call(f32[48,24,384]{2,1,0:T(8,128)} %in_ref.1, bf16[2,384,384]{2,1,0:T(8,128)(2,1)} %constant.101.clone.q_hbm.q_ref), custom_call_target="tpu_custom_call" | custom-call | tf_op jit(solution)/shard_map/forward_third/pallas_call | solution.py:170
  5.9 0.0 copy-start.9
  5.9 0.0 copy-start.2
  5.9 0.0 copy-start.3
  5.9 0.0 copy-start.4
  5.9 0.0 copy-start.7
  5.9 0.0 copy-start.8
  5.9 11.5 %all-to-all-start = ((f32[128,1,3456]{2,1,0:T(1,128)}), f32[128,1,3456]{2,1,0:T(1,128)S(1)}, u32[]{:S(2)}, u32[]{:S(2)}) async-start(f32[128,1,3456]{2,1,0:T(1,128)} %bitcast.28), calls=%async_computation | async-start | bytes 3538944 | tf_op jit(solution)/shard_map/all_to_all | solution.py:523
  17.5 0.6 gather_fusion
  18.1 25.4 %all-to-all-done = f32[128,1,3456]{2,1,0:T(1,128)S(1)} async-done(((f32[128,1,3456]{2,1,0:T(1,128)}), f32[128,1,3456]{2,1,0:T(1,128)S(1)}, u32[]{:S(2)}, u32[]{:S(2)}) %all-to-all-start) | async-done | bytes 1769504 | tf_op jit(solution)/shard_map/all_to_all | solution.py:523
  43.5 0.0 copy-start.5
  43.6 1.0 copy-done.5
  44.5 9.2 %solve_planes.1 = f32[4224,128]{1,0:T(8,128)} custom-call(f32[3]{0:T(128)S(1)} %gather_fusion, f32[3456,128]{1,0:T(8,128)S(1)} %bitcast.24, bf16[2,2,256,256]{3,2,1,0:T(8,128)(2,1)S(1)} %copy-done.3, bf16[2,2,192,192]{3,2,1,0:T(8,128)(2,1)S(1)} %copy-done.5, bf16[2,2,224,192]{3,2,1,0:T(8,128)(2,1)S(1)} %copy-done.4, bf16[2,2,256,256]{3,2,1,0:T(8,128)(2,1)S(1)} %copy-done.2, ...), custom_call_target="tpu_custom_call" | custom-call | tf_op jit(solution)/shard_map/solve_planes/pallas_call | solution.py:255
  53.7 5.0 %all-to-all-start.1 = ((f32[128,1,4224]{2,1,0:T(1,128)}), f32[128,1,4224]{2,1,0:T(1,128)S(1)}, u32[]{:S(2)}, u32[]{:S(2)}) async-start(f32[128,1,4224]{2,1,0:T(1,128)} %bitcast.27), calls=%async_computation.1 | async-start | bytes 4325376 | tf_op jit(solution)/shard_map/all_to_all | solution.py:526
  58.7 0.0 copy-start.12
  58.8 0.0 copy-start.10
  58.8 1.9 %fusion.16 = (f32[16,32,128]{2,1,0:T(8,128)}, f32[16,32,128]{2,1,0:T(8,128)}) fusion(f32[16,32,1024]{2,1,0:T(8,128)} %dens_hbm.1), kind=kLoop, calls=%fused_computation.45 | loop fusion | bytes 1048576 | tf_op jit(solution)/shard_map/slice | solution.py:519
  60.7 1.3 %collective-permute-start.1 = (f32[16,32,128]{2,1,0:T(8,128)}, f32[16,32,128]{2,1,0:T(8,128)}, u32[]{:S(2)}, u32[]{:S(2)}) collective-permute-start(f32[16,32,128]{2,1,0:T(8,128)} %get-tuple-element.7), channel_id=1, source_target_pairs={{1,0},{2,1},{3,2},{4,3},{5,4},{6,5},{7,6},{8,7},{9,8},{10,9},{11,1... | collective-permute-start | bytes 786440 | tf_op jit(solution)/shard_map/ppermute | solution.py:83
  62.0 4.9 %collective-permute-start = (f32[16,32,128]{2,1,0:T(8,128)}, f32[16,32,128]{2,1,0:T(8,128)}, u32[]{:S(2)}, u32[]{:S(2)}) collective-permute-start(f32[16,32,128]{2,1,0:T(8,128)} %get-tuple-element.8), channel_id=1, source_target_pairs={{0,1},{1,2},{2,3},{3,4},{4,5},{5,6},{6,7},{7,8},{8,9},{9,10},{10,1... | collective-permute-start | bytes 786440 | tf_op jit(solution)/shard_map/ppermute | solution.py:83
  66.9 1.3 %copy.45 = s32[3,2048]{0,1:T(8,128)} copy(s32[3,2048]{1,0:T(4,128)S(1)} %copy-done.11) | data formatting | bytes 49152 | tf_op args[3]
  68.2 0.1 fusion.3
  68.4 1.8 %gather_fusion.1 = s32[16,3]{1,0:T(8,128)S(1)} fusion(s32[3,2048]{0,1:T(8,128)} %copy.45, s32[1024]{0:T(1024)S(1)} %pad_clamp_fusion.1), kind=kCustom, calls=%fused_computation.1 | custom fusion | bytes 448 | tf_op jit(solution)/shard_map/gather | solution.py:530
  70.1 0.1 copy.46
  70.2 0.1 add_remainder_fusion
  70.3 0.1 rem.73
  70.4 0.1 pad_dynamic-slice_fusion
  70.5 0.5 fusion.14
  71.0 1.0 gather_fusion.2
  72.0 0.0 copy-start
  72.0 0.2 copy.47
  72.2 0.0 copy-start.13
  72.2 0.0 copy-start.14
  72.2 16.8 %all-to-all-done.1 = f32[128,1,4224]{2,1,0:T(1,128)S(1)} async-done(((f32[128,1,4224]{2,1,0:T(1,128)}), f32[128,1,4224]{2,1,0:T(1,128)S(1)}, u32[]{:S(2)}, u32[]{:S(2)}) %all-to-all-start.1) | async-done | bytes 2162720 | tf_op jit(solution)/shard_map/all_to_all | solution.py:526
  89.0 3.5 %cut_patches.1 = f32[256,128]{1,0:T(8,128)} custom-call(s32[2,16]{1,0:T(2,128)S(1)} %pad_add_fusion.start_ref, f32[4224,128]{1,0:T(8,128)S(1)} %bitcast.22, f32[384,256]{1,0:T(8,128)S(1)} %bitcast.25), custom_call_target="tpu_custom_call" | custom-call | tf_op jit(solution)/shard_map/cut_patches/pallas_call | solution.py:298
  92.6 4.2 %all-to-all-start.2 = ((f32[16,16,128]{2,1,0:T(8,128)}), f32[16,16,128]{2,1,0:T(8,128)S(1)}, u32[]{:S(2)}, u32[]{:S(2)}) async-start(f32[16,16,128]{2,1,0:T(8,128)} %bitcast.14), calls=%async_computation.2 | async-start | bytes 262144 | tf_op jit(solution)/shard_map/all_to_all | solution.py:536
  96.9 0.1 copy.42
  96.9 0.1 copy.44
  97.0 0.1 copy.41
  97.1 0.1 copy.43
  97.2 0.6 dynamic_slice.15
  97.8 0.6 fusion.10
  98.4 0.1 stack.62.flag_ref
  98.5 0.0 copy-start.1
  98.5 4.4 %block_of.1 = f32[48,24,384]{2,1,0:T(8,128)} custom-call(f32[4224,128]{1,0:T(8,128)S(1)} %bitcast.23, bf16[2,384,384]{2,1,0:T(8,128)(2,1)S(1)} %copy-done), custom_call_target="tpu_custom_call" | custom-call | tf_op jit(solution)/shard_map/block_of/pallas_call | solution.py:319
  102.9 0.0 collective-permute-done.1.high_ref
  102.9 0.6 all-to-all-done.2
  103.5 1.0 copy-done.6
  104.5 20.4 %relax_and_kick.1 = (f32[16,32,1024]{2,1,0:T(8,128)}, f32[3,16,32,1024]{3,2,1,0:T(8,128)}) custom-call(s32[16,6]{1,0:T(8,128)S(1)} %stack.62.flag_ref, f32[256,128]{1,0:T(8,128)S(1)} %bitcast.26, bf16[640,256]{1,0:T(8,128)(2,1)S(1)} %copy-done.6, bf16[128,2560]{1,0:T(8,128)(2,1)S(1)} %copy-done.1, f32[16,32,1024]{2,1,0:T(8,128)} %dens_hbm.1, ...), custom_call_target="tpu_custom_call" | custom-call | tf_op jit(solution)/shard_map/relax_and_kick/pallas_call | solution.py:476
  (25 shorter events, 0.1 us)
Async XLA Ops:
  5.9 11.6 %copy-start.9 = (f32[384]{0:T(512)S(1)}, f32[384]{0:T(512)}, u32[]{:S(2)}) copy-start(f32[384]{0:T(512)} %constant.100.clone) | copy-start | bytes 4612
  5.9 37.6 %copy-start.2 = (bf16[2,2,256,256]{3,2,1,0:T(8,128)(2,1)S(1)}, bf16[2,2,256,256]{3,2,1,0:T(8,128)(2,1)}, u32[]{:S(2)}) copy-start(bf16[2,2,256,256]{3,2,1,0:T(8,128)(2,1)} %constant.130.bx_ref) | copy-start | bytes 1572868
  5.9 37.6 %copy-start.3 = (bf16[2,2,256,256]{3,2,1,0:T(8,128)(2,1)S(1)}, bf16[2,2,256,256]{3,2,1,0:T(8,128)(2,1)}, u32[]{:S(2)}) copy-start(bf16[2,2,256,256]{3,2,1,0:T(8,128)(2,1)} %constant.121.ax_ref) | copy-start | bytes 1572868
  5.9 37.6 %copy-start.4 = (bf16[2,2,224,192]{3,2,1,0:T(8,128)(2,1)S(1)}, bf16[2,2,224,192]{3,2,1,0:T(8,128)(2,1)}, u32[]{:S(2)}) copy-start(bf16[2,2,224,192]{3,2,1,0:T(8,128)(2,1)} %constant.127.by_ref) | copy-start | bytes 1032196
  5.9 37.6 %copy-start.7 = (f32[2,192,1]{2,1,0:T(8,128)S(1)}, f32[2,192,1]{2,1,0:T(8,128)}, u32[]{:S(2)}) copy-start(f32[2,192,1]{2,1,0:T(8,128)} %constant.110.clone.ey_ref) | copy-start | bytes 4612
  5.9 37.6 %copy-start.8 = (f32[1,512]{1,0:T(1,128)S(1)}, f32[1,512]{1,0:T(1,128)}, u32[]{:S(2)}) copy-start(f32[1,512]{1,0:T(1,128)} %constant.111.clone.ex_ref) | copy-start | bytes 6148
  5.9 37.6 %all-to-all-start = ((f32[128,1,3456]{2,1,0:T(1,128)}), f32[128,1,3456]{2,1,0:T(1,128)S(1)}, u32[]{:S(2)}, u32[]{:S(2)}) async-start(f32[128,1,3456]{2,1,0:T(1,128)} %bitcast.28), calls=%async_computation | async-start | bytes 3538944 | tf_op jit(solution)/shard_map/all_to_all | solution.py:523
  43.5 1.0 copy-start.5
  53.7 13.1 %copy-start.11 = (s32[3,2048]{1,0:T(4,128)S(1)}, s32[3,2048]{1,0:T(4,128)}, u32[]{:S(2)}) copy-start(s32[3,2048]{1,0:T(4,128)} %param.25) | copy-start | bytes 73732
  53.7 35.3 %all-to-all-start.1 = ((f32[128,1,4224]{2,1,0:T(1,128)}), f32[128,1,4224]{2,1,0:T(1,128)S(1)}, u32[]{:S(2)}, u32[]{:S(2)}) async-start(f32[128,1,4224]{2,1,0:T(1,128)} %bitcast.27), calls=%async_computation.1 | async-start | bytes 4325376 | tf_op jit(solution)/shard_map/all_to_all | solution.py:526
  58.7 11.6 %copy-start.12 = (s32[2,2048]{1,0:T(2,128)S(1)}, s32[2,2048]{1,0:T(2,128)}, u32[]{:S(2)}) copy-start(s32[2,2048]{1,0:T(2,128)} %param.27) | copy-start | bytes 49156
  58.8 12.3 %copy-start.10 = (f32[384,384]{1,0:T(8,128)S(1)}, f32[384,384]{1,0:T(8,128)}, u32[]{:S(2)}) copy-start(f32[384,384]{1,0:T(8,128)} %constant.99.clone) | copy-start | bytes 1769476
  60.7 42.2 %collective-permute-start.1 = (f32[16,32,128]{2,1,0:T(8,128)}, f32[16,32,128]{2,1,0:T(8,128)}, u32[]{:S(2)}, u32[]{:S(2)}) collective-permute-start(f32[16,32,128]{2,1,0:T(8,128)} %get-tuple-element.7), channel_id=1, source_target_pairs={{1,0},{2,1},{3,2},{4,3},{5,4},{6,5},{7,6},{8,7},{9,8},{10,9},{11,1... | collective-permute-start | bytes 786440 | tf_op jit(solution)/shard_map/ppermute | solution.py:83
  62.0 40.9 %collective-permute-start = (f32[16,32,128]{2,1,0:T(8,128)}, f32[16,32,128]{2,1,0:T(8,128)}, u32[]{:S(2)}, u32[]{:S(2)}) collective-permute-start(f32[16,32,128]{2,1,0:T(8,128)} %get-tuple-element.8), channel_id=1, source_target_pairs={{0,1},{1,2},{2,3},{3,4},{4,5},{5,6},{6,7},{7,8},{8,9},{9,10},{10,1... | collective-permute-start | bytes 786440 | tf_op jit(solution)/shard_map/ppermute | solution.py:83
  72.0 26.5 %copy-start = (bf16[2,384,384]{2,1,0:T(8,128)(2,1)S(1)}, bf16[2,384,384]{2,1,0:T(8,128)(2,1)}, u32[]{:S(2)}) copy-start(bf16[2,384,384]{2,1,0:T(8,128)(2,1)} %constant.101.clone.q_hbm.q_ref) | copy-start | bytes 1769476
  72.2 24.7 %copy-start.13 = (s32[16,1]{0,1:T(1,128)S(1)}, s32[16,1]{0,1:T(1,128)}, u32[]{:S(2)}) copy-start(s32[16,1]{0,1:T(1,128)} %fusion.14) | copy-start | bytes 196
  72.2 25.0 %copy-start.14 = (s32[128]{0:T(128)S(1)}, s32[128]{0:T(128)}, u32[]{:S(2)}) copy-start(s32[128]{0:T(128)} %param.26) | copy-start | bytes 1540
  92.6 10.9 %all-to-all-start.2 = ((f32[16,16,128]{2,1,0:T(8,128)}), f32[16,16,128]{2,1,0:T(8,128)S(1)}, u32[]{:S(2)}, u32[]{:S(2)}) async-start(f32[16,16,128]{2,1,0:T(8,128)} %bitcast.14), calls=%async_computation.2 | async-start | bytes 262144 | tf_op jit(solution)/shard_map/all_to_all | solution.py:536
  98.5 5.0 %copy-start.1 = (bf16[128,2560]{1,0:T(8,128)(2,1)S(1)}, bf16[128,2560]{1,0:T(8,128)(2,1)}, u32[]{:S(2)}) copy-start(bf16[128,2560]{1,0:T(8,128)(2,1)} %constant.113.clone.cols_ref) | copy-start | bytes 1966084
  103.5 1.0 copy-start.6

commit v5 on v4

--- a/solution.py
+++ b/solution.py
@@ -22,6 +22,7 @@
 YE = YB + 4
 PLANE = 1408
 ROWS = 48
+GROUP = 4
 TILES_IN = XB * YB // 128
 TILES_OUT = PLANE // 128
 EDGE = 4
@@ -203,20 +204,21 @@
                 row = y * PY + h * 8
                 for t, tile in enumerate(even + odd):
                     x_ref[m, row:row + 8, t * 128:(t + 1) * 128] = tile
+    second = [jnp.broadcast_to(ey_ref[i:i + 1, :], (128, 256)).T[:NR // 2, :1] for i in range(2)]
     for m in range(MODES):
-        z = jnp.concatenate([right_product(x_ref[m, :, i * 256:(i + 1) * 256], ax_ref.at[i]) for i in range(2)], axis=1)
+        z = jnp.concatenate([right_product(x_ref[m, :, i * 256:i * 256 + NR // 2], ax_ref.at[i]) for i in range(2)], axis=1)
         z = z.reshape(YB, PY, 512)
         near = z[:, :8].reshape(YB * 8, 512)
         far = z[:, 8:].reshape(YB * 8, 512)
         halves = []
         for i, z in enumerate((near + far, near - far)):
             z = left_product(ay_ref.at[i], z)
-            total = mode_ref[m] + ey_ref[i] + ex_ref[...]
+            total = mode_ref[m] + second[i] + ex_ref[...]
             is_zero = total == 0.0
             z = jnp.where(is_zero, 0.0, z / jnp.where(is_zero, -1.0, total))
             halves.append(left_product(by_ref.at[i], z))
         z = jnp.concatenate([halves[0] + halves[1], halves[0] - halves[1]], axis=0)
-        even, odd = (right_product(z[:, i * 256:(i + 1) * 256], bx_ref.at[i]) for i in range(2))
+        even, odd = (right_product(z[:, i * 256:i * 256 + NR // 2], bx_ref.at[i]) for i in range(2))
         o_ref[m, :, :256] = even + odd
         o_ref[m, :, 256:] = even - odd
     for m in range(MODES):
@@ -237,18 +239,18 @@
     wide = ((np.arange(YE)[:, None] - 2 + np.arange(8)[None, :] * YB) % NR).reshape(-1)
     half = NR // 2
     tables = [[], [], [], []]
-    ey = np.zeros((2, half, 1))
+    ey = np.zeros((2, 256))
     ex = np.full((1, 512), -1.0)
     for i in range(2):
         part = q[:, k % 2 == i]
-        ey[i, :, 0] = eig[k % 2 == i]
+        ey[i, :half] = eig[k % 2 == i]
         ex[0, i * 256:i * 256 + half] = eig[k % 2 == i]
-        ax = np.zeros((256, 256))
+        ax = np.zeros((half, 256))
         ax[:half, :half] = part[:half]
-        bx = np.zeros((256, PX // 2, 64))
+        bx = np.zeros((half, PX // 2, 64))
         for p in range(PX // 2):
             bx[:half, p, :XE] = part[(p * XB + np.arange(XE) - 1) % NR].T
-        for bucket, table in zip(tables, (ax, part[order].T, part[wide], bx.reshape(256, 256))):
+        for bucket, table in zip(tables, (ax, part[order].T, part[wide], bx.reshape(half, 256))):
             bucket.append(table_pair(table))
     tables = [jnp.stack(bucket) for bucket in tables]
     vmem = pl.BlockSpec(memory_space=pltpu.VMEM)
@@ -308,7 +310,10 @@
     )(starts, spectrum, columns)
 
 
-def block_kernel(s_ref, q_ref, out_ref):
+def block_kernel(s_ref, q_hbm, out_ref, q_ref, sem):
+    copy = pltpu.make_async_copy(q_hbm, q_ref, sem)
+    copy.start()
+    copy.wait()
     cells = columns_of(s_ref, q_ref)
     for y in range(YB):
         first = (y + 2) * XE + 1
@@ -319,17 +324,17 @@
     return pl.pallas_call(
         block_kernel,
         out_shape=jax.ShapeDtypeStruct((XB, YB, NR), jnp.float32),
-        in_specs=[pl.BlockSpec(memory_space=pltpu.VMEM), pl.BlockSpec(memory_space=pltpu.VMEM)],
+        in_specs=[pl.BlockSpec(memory_space=pltpu.VMEM), pl.BlockSpec(memory_space=pltpu.HBM)],
         out_specs=pl.BlockSpec(memory_space=pltpu.VMEM),
+        scratch_shapes=[pltpu.VMEM((2, NR, NR), jnp.bfloat16), pltpu.SemaphoreType.DMA],
         compiler_params=pltpu.CompilerParams(vmem_limit_bytes=14 << 20),
         name="block_of",
-    )(spectrum, table_pair(q.T))
+    )(spectrum, in_hbm(table_pair(q.T)))
 
 
 def relax_kernel(flag_ref, patch_ref, rows_ref, cols_ref, dens_hbm, low_ref, high_ref, vel_hbm,
-                 pot_hbm, out_hbm, grid_ref, v_ref, f_ref, dens_ref, vel_ref, in_sem, out_sem):
+                 pot_hbm, out_hbm, grid_ref, v_ref, f_ref, dens_ref, vel_ref, beside_ref, in_sem, out_sem):
     step = pl.program_id(0)
-    slots = pl.num_programs(0)
 
     def arrivals(s):
         return (pltpu.make_async_copy(dens_hbm.at[s], dens_ref.at[s], in_sem.at[0, s]),
@@ -347,6 +352,11 @@
 
     @pl.when(step == 0)
     def _():
+        source = lax.broadcasted_iota(jnp.int32, (512, 256), 0) % 256
+        target = lax.broadcasted_iota(jnp.int32, (512, 256), 1)
+        apart = jnp.abs(source - target)
+        near = (apart == CELLS) | ((apart == 1) & (source // CELLS == target // CELLS))
+        beside_ref[...] = jnp.where(near, 1.0, 0.0).astype(jnp.bfloat16)
         rows = rows_ref[...]
         ordered = jnp.concatenate(
             [patch_ref[pl.ds(pl.multiple_of(flag_ref[j, 5] * 16, 16), 16), :] for j in range(PY)], axis=0)
@@ -358,9 +368,6 @@
             table = cols_ref[:, n:n + 256]
             grid_ref[:, n:n + 256] = dot(pair, jnp.concatenate([table, table], axis=0))
 
-    for copy in arrivals(step):
-        copy.wait()
-    base = pl.multiple_of(step * 40, 8)
     tiles = LANES // 128
     lane = lax.broadcasted_iota(jnp.int32, (8, 128), 1)
     third_first = lane % CELLS == 0
@@ -368,99 +375,129 @@
     second_first = lane < CELLS
     second_last = lane >= 128 - CELLS
     zero = jnp.zeros((8, 128), jnp.float32)
-    use_low = jnp.broadcast_to(flag_ref[step, 0], (8, 128)) > 0
-    use_high = jnp.broadcast_to(flag_ref[step, 1], (8, 128)) > 0
-    same_low = jnp.broadcast_to(flag_ref[step, 2], (8, 128)) > 0
-    same_high = jnp.broadcast_to(flag_ref[step, 3], (8, 128)) > 0
-    live = jnp.broadcast_to(flag_ref[step, 4], (8, 128)) > 0
-
-    def start(t, r):
-        return grid_ref[pl.ds(base + r * 8, 8), t * 128:(t + 1) * 128]
-
-    def edge(t, r):
-        return grid_ref[pl.ds(base + r * 8, 8), LANES + t * 128:LANES + (t + 1) * 128]
-
-    def row_of(slot, t, r):
-        return (slot * tiles + t) * ROWS + 8 + r * 8
-
-    for t in range(tiles):
-        faces = grid_ref[pl.ds(base + 32, 8), t * 128:(t + 1) * 128]
-        for slot in range(2):
-            row = row_of(slot, t, 0)
-            v_ref[row - 1:row, :] = faces[0:1]
-            v_ref[row + CELLS:row + CELLS + 1, :] = faces[1:2]
+    slot_of = [step * GROUP + g for g in range(GROUP)]
+    bases = [pl.multiple_of(s * 40, 8) for s in slot_of]
+    flag = lambda g, i: jnp.broadcast_to(flag_ref[slot_of[g], i], (8, 128)) > 0
+    use_low, use_high, same_low, same_high, live = ([flag(g, i) for g in range(GROUP)] for i in range(5))
+
+    def start(g, t, r):
+        return grid_ref[pl.ds(bases[g] + r * 8, 8), t * 128:(t + 1) * 128]
+
+    def edge(g, t, r):
+        return grid_ref[pl.ds(bases[g] + r * 8, 8), LANES + t * 128:LANES + (t + 1) * 128]
+
+    def row_of(buffer, g, t, r):
+        return ((buffer * GROUP + g) * tiles + t) * ROWS + 8 + r * 8
+
+    def value(buffer, g, t, r):
+        row = row_of(buffer, g, t, r)
+        return v_ref[row:row + 8, :]
+
+    def first_neighbours(buffer, g, t, r):
+        row = row_of(buffer, g, t, r)
+        return v_ref[row - 1:row + 7, :], v_ref[row + 1:row + 9, :]
+
+    def prepare(g):
+        s = slot_of[g]
+        for copy in arrivals(s):
+            copy.wait()
+        for t in range(tiles):
+            faces = grid_ref[pl.ds(bases[g] + 32, 8), t * 128:(t + 1) * 128]
+            for buffer in range(2):
+                row = row_of(buffer, g, t, 0)
+                v_ref[row - 1:row, :] = faces[0:1]
+                v_ref[row + CELLS:row + CELLS + 1, :] = faces[1:2]
+            for r in range(4):
+                rows = slice(r * 8, r * 8 + 8)
+                if t == 0:
+                    rho = low_ref[s, rows, :]
+                elif t == tiles - 1:
+                    rho = high_ref[s, rows, :]
+                else:
+                    rho = dens_ref[s, rows, (t - 1) * 128:t * 128]
+                fixed = edge(g, t, r) - rho * (1.0 / (REF * REF))
+                if t == 0:
+                    fixed -= jnp.where(second_first, pltpu.roll(start(g, tiles - 1, r), CELLS, 1), zero)
+                if t == tiles - 1:
+                    fixed -= jnp.where(second_last, pltpu.roll(start(g, 0, r), 128 - CELLS, 1), zero)
+                f_ref[g, t, r] = fixed
+                row = row_of(0, g, t, r)
+                v_ref[row:row + 8, :] = start(g, t, r)
+
+    pairs = [(tiles - 1, 0)] + [(t, t + 1) for t in range(1, tiles - 1, 2)]
+    beside = beside_ref[...]
+
+    def around_of(buffer, members):
+        stacked = jnp.concatenate([
+            jnp.concatenate([v_ref[row_of(buffer, g, t, 0):row_of(buffer, g, t, 4), :] for t in pair], axis=1)
+            for g in members for pair in pairs
+        ], axis=0)
+        return dot(jnp.concatenate(split2(stacked), axis=1), beside)
+
+    def update(buffer, members, around):
+        for m, g in enumerate(members):
+            for p, pair in enumerate(pairs):
+                for side, t in enumerate(pair):
+                    for r in range(4):
+                        here = value(buffer, g, t, r)
+                        if side == 0:
+                            other = pltpu.roll(value(buffer, g, t - 1, r), CELLS, 1)
+                            if t == tiles - 1:
+                                other = jnp.where(same_high[g], other, pltpu.roll(start(g, t - 1, r), CELLS, 1))
+                            other = jnp.where(second_first, other, zero)
+                        else:
+                            other = pltpu.roll(value(buffer, g, t + 1, r), 128 - CELLS, 1)
+                            if t == 0:
+                                other = jnp.where(same_low[g], other, pltpu.roll(start(g, t + 1, r), 128 - CELLS, 1))
+                            other = jnp.where(second_last, other, zero)
+                        before, after = first_neighbours(buffer, g, t, r)
+                        row = (m * len(pairs) + p) * CELLS + r * 8
+                        total = (here + f_ref[g, t, r]) + (before + after) + (
+                            around[row:row + 8, side * 128:(side + 1) * 128] + other)
+                        new = total * (1.0 - RELAX)
+                        if t == 0:
+                            new = jnp.where(use_low[g], new, here)
+                        if t == tiles - 1:
+                            new = jnp.where(use_high[g], new, here)
+                        row = row_of(1 - buffer, g, t, r)
+                        v_ref[row:row + 8, :] = new
+
+    def kick(buffer, g):
+        s = slot_of[g]
         for r in range(4):
-            rows = slice(r * 8, r * 8 + 8)
-            if t == 0:
-                rho = low_ref[step, rows, :]
-            elif t == tiles - 1:
-                rho = high_ref[step, rows, :]
-            else:
-                rho = dens_ref[step, rows, (t - 1) * 128:t * 128]
-            f_ref[t, r] = edge(t, r) - rho * (1.0 / (REF * REF))
-            row = row_of(0, t, r)
-            v_ref[row:row + 8, :] = start(t, r)
-
-    def second_neighbours(values, r):
-        up = [pltpu.roll(value, CELLS, 1) for value in values]
-        down = [pltpu.roll(value, 128 - CELLS, 1) for value in values]
-        into_high = jnp.where(same_high, up[-2], pltpu.roll(start(tiles - 2, r), CELLS, 1))
-        into_low = jnp.where(same_low, down[1], pltpu.roll(start(1, r), 128 - CELLS, 1))
-        befores = [zero] + up[:-2] + [into_high]
-        afters = [into_low] + down[2:] + [zero]
-        return ([jnp.where(second_first, before, here) for before, here in zip(befores, up)],
-                [jnp.where(second_last, after, here) for after, here in zip(afters, down)])
-
-    def first_neighbours(slot, t, r):
-        row = row_of(slot, t, r)
-        return v_ref[row - 1:row + 7, :], v_ref[row + 1:row + 9, :]
-
-    def third_neighbours(here, low, high):
-        return (jnp.where(third_first, low, pltpu.roll(here, 1, 1)),
-                jnp.where(third_last, high, pltpu.roll(here, 127, 1)))
-
-    def reader(slot):
-        return lambda t, r: v_ref[row_of(slot, t, r):row_of(slot, t, r) + 8, :]
-
+            values = [value(buffer, g, t, r) for t in range(tiles)]
+            up = [pltpu.roll(here, CELLS, 1) for here in values]
+            down = [pltpu.roll(here, 128 - CELLS, 1) for here in values]
+            for t in range(1, tiles - 1):
+                here = values[t]
+                rows = slice(r * 8, r * 8 + 8)
+                cols = slice((t - 1) * 128, t * 128)
+                dens_ref[s, rows, cols] = jnp.where(live[g], here, 0.0)
+                wall = edge(g, t, r)
+                ends = (
+                    first_neighbours(buffer, g, t, r),
+                    (jnp.where(second_first, up[t - 1], up[t]), jnp.where(second_last, down[t + 1], down[t])),
+                    (jnp.where(third_first, wall, pltpu.roll(here, 1, 1)),
+                     jnp.where(third_last, wall, pltpu.roll(here, 127, 1))),
+                )
+                for q, (before, after) in enumerate(ends):
+                    kicked = vel_ref[q, s, rows, cols] - (after - before) * (REF / 2.0)
+                    vel_ref[q, s, rows, cols] = jnp.where(live[g], kicked, 0.0)
+        for copy in departures(s):
+            copy.start()
+
+    halves = [range(0, GROUP // 2), range(GROUP // 2, GROUP)]
+    for g in range(GROUP):
+        prepare(g)
     for sweep in range(SWEEPS):
-        slot = sweep % 2
-        value = reader(slot)
-        for r in range(4):
-            values = [value(t, r) for t in range(tiles)]
-            befores, afters = second_neighbours(values, r)
-            for t, here in enumerate(values):
-                total = here + f_ref[t, r] + (befores[t] + afters[t])
-                before, after = first_neighbours(slot, t, r)
-                total += before + after
-                before, after = third_neighbours(here, zero, zero)
-                total += before + after
-                new = total * (1.0 - RELAX)
-                if t == 0:
-                    new = jnp.where(use_low, new, here)
-                if t == tiles - 1:
-                    new = jnp.where(use_high, new, here)
-                row = row_of(1 - slot, t, r)
-                v_ref[row:row + 8, :] = new
-
-    slot = SWEEPS % 2
-    value = reader(slot)
-    for r in range(4):
-        values = [value(t, r) for t in range(tiles)]
-        befores, afters = second_neighbours(values, r)
-        for t in range(1, tiles - 1):
-            here = values[t]
-            rows = slice(r * 8, r * 8 + 8)
-            cols = slice((t - 1) * 128, t * 128)
-            dens_ref[step, rows, cols] = jnp.where(live, here, 0.0)
-            wall = edge(t, r)
-            pairs = (first_neighbours(slot, t, r), (befores[t], afters[t]), third_neighbours(here, wall, wall))
-            for q, (before, after) in enumerate(pairs):
-                kicked = vel_ref[q, step, rows, cols] - (after - before) * (REF / 2.0)
-                vel_ref[q, step, rows, cols] = jnp.where(live, kicked, 0.0)
-    for copy in departures(step):
-        copy.start()
-
-    @pl.when(step == slots - 1)
+        buffer = sweep % 2
+        arounds = [around_of(buffer, members) for members in halves]
+        for members, around in zip(halves, arounds):
+            update(buffer, members, around)
+    for g in range(GROUP):
+        kick(SWEEPS % 2, g)
+
+    @pl.when(step == pl.num_programs(0) - 1)
     def _():
         for s in range(PY):
             for copy in departures(s):
@@ -477,7 +514,7 @@
         relax_kernel,
         grid_spec=pltpu.PrefetchScalarGridSpec(
             num_scalar_prefetch=1,
-            grid=(slots,),
+            grid=(slots // GROUP,),
             in_specs=[
                 whole((slots * 16, 128)),
                 whole((slots * 40, slots * 16)),
@@ -490,10 +527,11 @@
             out_specs=[pl.BlockSpec(memory_space=pltpu.HBM), pl.BlockSpec(memory_space=pltpu.HBM)],
             scratch_shapes=[
                 pltpu.VMEM((slots * 40, 2 * LANES), jnp.float32),
-                pltpu.VMEM((2 * (LANES // 128) * ROWS, 128), jnp.float32),
-                pltpu.VMEM((LANES // 128, 4, 8, 128), jnp.float32),
+                pltpu.VMEM((2 * GROUP * (LANES // 128) * ROWS, 128), jnp.float32),
+                pltpu.VMEM((GROUP, LANES // 128, 4, 8, 128), jnp.float32),
                 pltpu.VMEM((slots, CELLS, CELLS * CELLS), jnp.float32),
                 pltpu.VMEM((3, slots, CELLS, CELLS * CELLS), jnp.float32),
+                pltpu.VMEM((512, 256), jnp.bfloat16),
                 pltpu.SemaphoreType.DMA((2, slots)),
                 pltpu.SemaphoreType.DMA((2, slots)),
             ],
@@ -502,7 +540,7 @@
             pltpu.HBM((slots, CELLS, CELLS * CELLS), jnp.float32),
             pltpu.HBM((3, slots, CELLS, CELLS * CELLS), jnp.float32),
         ],
-        compiler_params=pltpu.CompilerParams(vmem_limit_bytes=22 << 20),
+        compiler_params=pltpu.CompilerParams(vmem_limit_bytes=26 << 20),
         name="relax_and_kick",
     )(flags, patch, block_rows, table, in_hbm(density), low, high, in_hbm(velocity))
 

time: 126 us -> 119 us (0.944)
  Pallas kernels: 42.7 us -> 38.4 us
  waiting for transfers between devices: 42.8 us -> 41 us
    pallas_call x1, Pallas kernels: 20.4 us -> 15 us  [relax(): pl.pallas_call(relax_kernel, grid_spec=pltpu.PrefetchScalarGridSpec(num_s...]
    unnamed x31 -> x27, local copies, waits for them, and re-layouts: 3.39 us -> 1.42 us
    gather x2, local copies, waits for them, and re-layouts: 1.15 us -> 2.89 us  [local(): columns = basis[third.reshape(-1)].T]
  transfers between devices with their start and end apart: 5 -> 5, of which waited for: 3 -> 2; matrix products, arithmetic and copies ran while one was open for 8% -> 9% of each run, Pallas kernels for 6% -> 8%
where the time goes in v5:
time: 119 us; the launch traced here: 118 us
  waiting for transfers between devices  41 us (34%)
  Pallas kernels  38.4 us (32%)
  starting transfers between devices  26.9 us (23%)
  local copies, waits for them, and re-layouts  9.91 us (8%)
    all_to_all x1, waiting for transfers between devices, local(): lax.all_to_all(packed, ('px', 'py'), 0, 0, tiled=True).reshape(-1, 128)  25.4 us
    all_to_all x1, waiting for transfers between devices, local(): lax.all_to_all(solved, ('px', 'py'), 0, 0, tiled=True).reshape(-1, 128)  15.6 us
    pallas_call x1, Pallas kernels, relax(): pl.pallas_call(relax_kernel, grid_spec=pltpu.PrefetchScalarGridSpec(num_s...  15 us
    all_to_all x1, starting transfers between devices, local(): lax.all_to_all(packed, ('px', 'py'), 0, 0, tiled=True).reshape(-1, 128)  11.5 us
    pallas_call x1, Pallas kernels, solve_planes(): pl.pallas_call(plane_kernel, out_shape=pltpu.HBM((DEV * MODES * TILES_OUT...  9.09 us
    ppermute x2, starting transfers between devices, from_behind(): lax.ppermute(value, axis, [(source, source + steps) for source in range(i...  6.16 us
    pallas_call x1, Pallas kernels, block_of(): pl.pallas_call(block_kernel, out_shape=jax.ShapeDtypeStruct((XB, YB, NR),...  5.53 us
    pallas_call x1, Pallas kernels, forward_third(): pl.pallas_call(forward_kernel, out_shape=pltpu.HBM((DEV * MODES * TILES_I...  5.23 us
  transfers between devices with their start and end apart: 5, of which 2 were waited for; matrix products, arithmetic and copies ran while one was open for 9% of the time, Pallas kernels for 8%

profile of v5, /device:TPU:1, one launch (start us, length us, event | category | flops | bytes accessed | tf_op | source)
XLA Modules:
  0.0 118.2 jit_solution(10632899152957824660)
XLA Ops:
  0.6 5.2 %forward_third.1 = f32[3456,128]{1,0:T(8,128)} custom-call(f32[48,24,384]{2,1,0:T(8,128)} %in_ref.1, bf16[2,384,384]{2,1,0:T(8,128)(2,1)} %constant.101.clone.q_hbm), custom_call_target="tpu_custom_call" | custom-call | tf_op jit(solution)/shard_map/forward_third/pallas_call | solution.py:171
  5.9 0.0 copy-start.8
  5.9 0.0 copy-start.1
  5.9 0.0 copy-start.2
  5.9 0.0 copy-start.3
  5.9 0.0 copy-start.4
  5.9 0.0 copy-start.6
  5.9 0.0 copy-start.7
  6.0 11.5 %all-to-all-start = ((f32[128,1,3456]{2,1,0:T(1,128)}), f32[128,1,3456]{2,1,0:T(1,128)S(1)}, u32[]{:S(2)}, u32[]{:S(2)}) async-start(f32[128,1,3456]{2,1,0:T(1,128)} %bitcast.28), calls=%async_computation | async-start | bytes 3538944 | tf_op jit(solution)/shard_map/all_to_all | solution.py:561
  17.5 0.0 copy-done.8
  17.5 0.6 gather_fusion
  18.1 25.4 %all-to-all-done = f32[128,1,3456]{2,1,0:T(1,128)S(1)} async-done(((f32[128,1,3456]{2,1,0:T(1,128)}), f32[128,1,3456]{2,1,0:T(1,128)S(1)}, u32[]{:S(2)}, u32[]{:S(2)}) %all-to-all-start) | async-done | bytes 1769504 | tf_op jit(solution)/shard_map/all_to_all | solution.py:561
  43.5 0.0 copy-done.1
  43.5 0.0 copy-done.2
  43.5 0.0 copy-done.3
  43.6 9.1 %solve_planes.1 = f32[4224,128]{1,0:T(8,128)} custom-call(f32[3]{0:T(128)S(1)} %gather_fusion, f32[3456,128]{1,0:T(8,128)S(1)} %bitcast.24, bf16[2,2,192,256]{3,2,1,0:T(8,128)(2,1)S(1)} %copy-done.4, bf16[2,2,192,192]{3,2,1,0:T(8,128)(2,1)S(1)} %copy-done.3, bf16[2,2,224,192]{3,2,1,0:T(8,128)(2,1)S(1)} %copy-done.1, bf16[2,2,192,256]{3,2,1,0:T(8,128)(2,1)S(1)} %copy-done.2, ...), custom_call_target="tpu_custom_call" | custom-call | tf_op jit(solution)/shard_map/solve_planes/pallas_call | solution.py:257
  52.7 5.0 %all-to-all-start.1 = ((f32[128,1,4224]{2,1,0:T(1,128)}), f32[128,1,4224]{2,1,0:T(1,128)S(1)}, u32[]{:S(2)}, u32[]{:S(2)}) async-start(f32[128,1,4224]{2,1,0:T(1,128)} %bitcast.27), calls=%async_computation.1 | async-start | bytes 4325376 | tf_op jit(solution)/shard_map/all_to_all | solution.py:564
  57.6 0.0 copy-start.11
  57.7 0.0 copy-start.9
  57.7 1.9 %fusion.16 = (f32[16,32,128]{2,1,0:T(8,128)}, f32[16,32,128]{2,1,0:T(8,128)}) fusion(f32[16,32,1024]{2,1,0:T(8,128)} %dens_hbm.1), kind=kLoop, calls=%fused_computation.45 | loop fusion | bytes 1048576 | tf_op jit(solution)/shard_map/slice | solution.py:557
  59.6 1.3 %collective-permute-start.1 = (f32[16,32,128]{2,1,0:T(8,128)}, f32[16,32,128]{2,1,0:T(8,128)S(1)}, u32[]{:S(2)}, u32[]{:S(2)}) collective-permute-start(f32[16,32,128]{2,1,0:T(8,128)} %get-tuple-element.7), channel_id=1, source_target_pairs={{1,0},{2,1},{3,2},{4,3},{5,4},{6,5},{7,6},{8,7},{9,8},{10,9},{11,1... | collective-permute-start | bytes 786440 | tf_op jit(solution)/shard_map/ppermute | solution.py:84
  60.9 4.9 %collective-permute-start = (f32[16,32,128]{2,1,0:T(8,128)}, f32[16,32,128]{2,1,0:T(8,128)}, u32[]{:S(2)}, u32[]{:S(2)}) collective-permute-start(f32[16,32,128]{2,1,0:T(8,128)} %get-tuple-element.8), channel_id=1, source_target_pairs={{0,1},{1,2},{2,3},{3,4},{4,5},{5,6},{6,7},{7,8},{8,9},{9,10},{10,1... | collective-permute-start | bytes 786440 | tf_op jit(solution)/shard_map/ppermute | solution.py:84
  65.8 1.3 %copy.45 = s32[3,2048]{0,1:T(8,128)} copy(s32[3,2048]{1,0:T(4,128)S(1)} %copy-done.10) | data formatting | bytes 49152 | tf_op args[3]
  67.1 0.1 fusion.3
  67.2 1.8 %gather_fusion.1 = s32[16,3]{1,0:T(8,128)S(1)} fusion(s32[3,2048]{0,1:T(8,128)} %copy.45, s32[1024]{0:T(1024)S(1)} %pad_clamp_fusion.1), kind=kCustom, calls=%fused_computation.1 | custom fusion | bytes 448 | tf_op jit(solution)/shard_map/gather | solution.py:568
  69.0 0.1 copy.46
  69.1 0.1 add_remainder_fusion
  69.2 0.1 rem.73
  69.3 0.1 pad_dynamic-slice_fusion
  69.4 1.7 %gather_fusion.2 = f32[256,384]{1,0:T(8,128)} fusion(f32[384,384]{1,0:T(8,128)S(1)} %copy-done.9, s32[1024]{0:T(1024)S(1)} %pad_clamp_fusion), kind=kCustom, calls=%fused_computation.2 | custom fusion | bytes 787456 | tf_op jit(solution)/shard_map/gather | solution.py:570
  71.2 1.2 copy.47
  72.3 15.6 %all-to-all-done.1 = f32[128,1,4224]{2,1,0:T(1,128)S(1)} async-done(((f32[128,1,4224]{2,1,0:T(1,128)}), f32[128,1,4224]{2,1,0:T(1,128)S(1)}, u32[]{:S(2)}, u32[]{:S(2)}) %all-to-all-start.1) | async-done | bytes 2162720 | tf_op jit(solution)/shard_map/all_to_all | solution.py:564
  87.9 3.5 %cut_patches.1 = f32[256,128]{1,0:T(8,128)} custom-call(s32[2,16]{1,0:T(2,128)S(1)} %pad_add_fusion.start_ref, f32[4224,128]{1,0:T(8,128)S(1)} %bitcast.22, f32[384,256]{1,0:T(8,128)S(1)} %bitcast.25), custom_call_target="tpu_custom_call" | custom-call | tf_op jit(solution)/shard_map/cut_patches/pallas_call | solution.py:300
  91.5 4.2 %all-to-all-start.2 = ((f32[16,16,128]{2,1,0:T(8,128)}), f32[16,16,128]{2,1,0:T(8,128)S(1)}, u32[]{:S(2)}, u32[]{:S(2)}) async-start(f32[16,16,128]{2,1,0:T(8,128)} %bitcast.14), calls=%async_computation.2 | async-start | bytes 262144 | tf_op jit(solution)/shard_map/all_to_all | solution.py:574
  95.8 0.1 copy.42
  95.8 0.1 copy.44
  95.9 0.1 copy.41
  96.0 0.1 copy.43
  96.1 0.6 dynamic_slice.15
  96.7 0.6 fusion.10
  97.3 0.1 stack.62.flag_ref
  97.4 0.0 copy-start
  97.4 0.0 copy-start.5
  97.4 5.5 %block_of.1 = f32[48,24,384]{2,1,0:T(8,128)} custom-call(f32[4224,128]{1,0:T(8,128)S(1)} %bitcast.23, bf16[2,384,384]{2,1,0:T(8,128)(2,1)} %constant.101.clone.q_hbm), custom_call_target="tpu_custom_call" | custom-call | tf_op jit(solution)/shard_map/block_of/pallas_call | solution.py:324
  103.0 0.0 collective-permute-done.1.high_ref
  103.0 0.0 collective-permute-done.low_ref
  103.0 0.0 all-to-all-done.2
  103.0 15.0 %relax_and_kick.1 = (f32[16,32,1024]{2,1,0:T(8,128)}, f32[3,16,32,1024]{3,2,1,0:T(8,128)}) custom-call(s32[16,6]{1,0:T(8,128)S(1)} %stack.62.flag_ref, f32[256,128]{1,0:T(8,128)S(1)} %bitcast.26, bf16[640,256]{1,0:T(8,128)(2,1)S(1)} %copy-done.5, bf16[128,2560]{1,0:T(8,128)(2,1)S(1)} %copy-done, f32[16,32,1024]{2,1,0:T(8,128)} %dens_hbm.1, ...), custom_call_target="tpu_custom_call" | custom-call | tf_op jit(solution)/shard_map/relax_and_kick/pallas_call | solution.py:513
  (21 shorter events, 0.1 us)
Async XLA Ops:
  5.9 11.6 %copy-start.8 = (f32[384]{0:T(512)S(1)}, f32[384]{0:T(512)}, u32[]{:S(2)}) copy-start(f32[384]{0:T(512)} %constant.100.clone) | copy-start | bytes 4612
  5.9 37.7 %copy-start.1 = (bf16[2,2,224,192]{3,2,1,0:T(8,128)(2,1)S(1)}, bf16[2,2,224,192]{3,2,1,0:T(8,128)(2,1)}, u32[]{:S(2)}) copy-start(bf16[2,2,224,192]{3,2,1,0:T(8,128)(2,1)} %constant.127.by_ref) | copy-start | bytes 1032196
  5.9 37.6 %copy-start.2 = (bf16[2,2,192,256]{3,2,1,0:T(8,128)(2,1)S(1)}, bf16[2,2,192,256]{3,2,1,0:T(8,128)(2,1)}, u32[]{:S(2)}) copy-start(bf16[2,2,192,256]{3,2,1,0:T(8,128)(2,1)} %constant.130.bx_ref) | copy-start | bytes 1179652
  5.9 37.6 %copy-start.3 = (bf16[2,2,192,192]{3,2,1,0:T(8,128)(2,1)S(1)}, bf16[2,2,192,192]{3,2,1,0:T(8,128)(2,1)}, u32[]{:S(2)}) copy-start(bf16[2,2,192,192]{3,2,1,0:T(8,128)(2,1)} %constant.124.ay_ref) | copy-start | bytes 884740
  5.9 37.6 %copy-start.4 = (bf16[2,2,192,256]{3,2,1,0:T(8,128)(2,1)S(1)}, bf16[2,2,192,256]{3,2,1,0:T(8,128)(2,1)}, u32[]{:S(2)}) copy-start(bf16[2,2,192,256]{3,2,1,0:T(8,128)(2,1)} %constant.121.ax_ref) | copy-start | bytes 1179652
  5.9 37.6 %copy-start.6 = (f32[1,512]{1,0:T(1,128)S(1)}, f32[1,512]{1,0:T(1,128)}, u32[]{:S(2)}) copy-start(f32[1,512]{1,0:T(1,128)} %constant.111.clone.ex_ref) | copy-start | bytes 6148
  5.9 37.6 %copy-start.7 = (f32[2,256]{1,0:T(2,128)S(1)}, f32[2,256]{1,0:T(2,128)}, u32[]{:S(2)}) copy-start(f32[2,256]{1,0:T(2,128)} %constant.110.clone.ey_ref) | copy-start | bytes 6148
  6.0 37.6 %all-to-all-start = ((f32[128,1,3456]{2,1,0:T(1,128)}), f32[128,1,3456]{2,1,0:T(1,128)S(1)}, u32[]{:S(2)}, u32[]{:S(2)}) async-start(f32[128,1,3456]{2,1,0:T(1,128)} %bitcast.28), calls=%async_computation | async-start | bytes 3538944 | tf_op jit(solution)/shard_map/all_to_all | solution.py:561
  52.7 13.1 %copy-start.10 = (s32[3,2048]{1,0:T(4,128)S(1)}, s32[3,2048]{1,0:T(4,128)}, u32[]{:S(2)}) copy-start(s32[3,2048]{1,0:T(4,128)} %param.25) | copy-start | bytes 73732
  52.7 35.3 %all-to-all-start.1 = ((f32[128,1,4224]{2,1,0:T(1,128)}), f32[128,1,4224]{2,1,0:T(1,128)S(1)}, u32[]{:S(2)}, u32[]{:S(2)}) async-start(f32[128,1,4224]{2,1,0:T(1,128)} %bitcast.27), calls=%async_computation.1 | async-start | bytes 4325376 | tf_op jit(solution)/shard_map/all_to_all | solution.py:564
  57.6 11.6 %copy-start.11 = (s32[2,2048]{1,0:T(2,128)S(1)}, s32[2,2048]{1,0:T(2,128)}, u32[]{:S(2)}) copy-start(s32[2,2048]{1,0:T(2,128)} %param.27) | copy-start | bytes 49156
  57.7 11.8 %copy-start.9 = (f32[384,384]{1,0:T(8,128)S(1)}, f32[384,384]{1,0:T(8,128)}, u32[]{:S(2)}) copy-start(f32[384,384]{1,0:T(8,128)} %constant.99.clone) | copy-start | bytes 1769476
  59.6 43.4 %collective-permute-start.1 = (f32[16,32,128]{2,1,0:T(8,128)}, f32[16,32,128]{2,1,0:T(8,128)S(1)}, u32[]{:S(2)}, u32[]{:S(2)}) collective-permute-start(f32[16,32,128]{2,1,0:T(8,128)} %get-tuple-element.7), channel_id=1, source_target_pairs={{1,0},{2,1},{3,2},{4,3},{5,4},{6,5},{7,6},{8,7},{9,8},{10,9},{11,1... | collective-permute-start | bytes 786440 | tf_op jit(solution)/shard_map/ppermute | solution.py:84
  60.9 42.1 %collective-permute-start = (f32[16,32,128]{2,1,0:T(8,128)}, f32[16,32,128]{2,1,0:T(8,128)}, u32[]{:S(2)}, u32[]{:S(2)}) collective-permute-start(f32[16,32,128]{2,1,0:T(8,128)} %get-tuple-element.8), channel_id=1, source_target_pairs={{0,1},{1,2},{2,3},{3,4},{4,5},{5,6},{6,7},{7,8},{8,9},{9,10},{10,1... | collective-permute-start | bytes 786440 | tf_op jit(solution)/shard_map/ppermute | solution.py:84
  71.2 24.9 %copy-start.12 = (s32[128]{0:T(128)S(1)}, s32[128]{0:T(128)}, u32[]{:S(2)}) copy-start(s32[128]{0:T(128)} %param.26) | copy-start | bytes 1540
  91.5 11.5 %all-to-all-start.2 = ((f32[16,16,128]{2,1,0:T(8,128)}), f32[16,16,128]{2,1,0:T(8,128)S(1)}, u32[]{:S(2)}, u32[]{:S(2)}) async-start(f32[16,16,128]{2,1,0:T(8,128)} %bitcast.14), calls=%async_computation.2 | async-start | bytes 262144 | tf_op jit(solution)/shard_map/all_to_all | solution.py:574
  97.4 5.6 %copy-start = (bf16[128,2560]{1,0:T(8,128)(2,1)S(1)}, bf16[128,2560]{1,0:T(8,128)(2,1)}, u32[]{:S(2)}) copy-start(bf16[128,2560]{1,0:T(8,128)(2,1)} %constant.113.clone.cols_ref) | copy-start | bytes 1966084
  97.4 5.6 %copy-start.5 = (bf16[640,256]{1,0:T(8,128)(2,1)S(1)}, bf16[640,256]{1,0:T(8,128)(2,1)}, u32[]{:S(2)}) copy-start(bf16[640,256]{1,0:T(8,128)(2,1)} %constant.112.clone.rows_ref) | copy-start | bytes 983044

commit v6 on v5

--- a/solution.py
+++ b/solution.py
@@ -22,7 +22,7 @@
 YE = YB + 4
 PLANE = 1408
 ROWS = 48
-GROUP = 4
+GROUP = 8
 TILES_IN = XB * YB // 128
 TILES_OUT = PLANE // 128
 EDGE = 4
@@ -115,14 +115,20 @@
     return jnp.asarray(np.stack([hi, low]))
 
 
+def padded(x):
+    rows = -x.shape[0] % 256
+    return jnp.concatenate([x, jnp.zeros((rows, x.shape[1]), x.dtype)], axis=0) if rows else x
+
+
 def right_product(x, pair):
     hi, low = split2(x)
-    return dot(hi, pair[0]) + dot(low, pair[0]) + dot(hi, pair[1])
+    first, second = padded(pair[0]), padded(pair[1])
+    return dot(jnp.concatenate([hi, low, hi], axis=1), jnp.concatenate([first, first, second], axis=0))
 
 
 def left_product(pair, x):
-    hi, low = split2(x)
-    return dot(pair[0], hi) + dot(pair[0], low) + dot(pair[1], hi)
+    hi, low = (padded(part) for part in split2(x))
+    return dot(jnp.concatenate([pair[0], pair[0], pair[1]], axis=1), jnp.concatenate([hi, low, hi], axis=0))
 
 
 def moved(tiles, source, target, width, lane, out):
@@ -157,10 +163,9 @@
         for copy in copies[part * 8:(part + 1) * 8]:
             copy.wait()
         hi, low = split2(rows_ref[part * 8:(part + 1) * 8].reshape(8 * XB, NR))
-        modes = None
-        for left, right in ((q_ref[0], hi), (q_ref[0], low), (q_ref[1], hi)):
-            term = lax.dot_general(left, right, contract, preferred_element_type=jnp.float32)
-            modes = term if modes is None else modes + term
+        modes = lax.dot_general(
+            jnp.concatenate([q_ref[0], q_ref[0], q_ref[1]], axis=1), jnp.concatenate([hi, low, hi], axis=1),
+            contract, preferred_element_type=jnp.float32)
         for m in range(MODES):
             for c in range(3):
                 out_ref[pl.ds(m * TILES_IN + part * 3 + c, DEV, stride=MODES * TILES_IN), :] = (
@@ -184,7 +189,8 @@
     lane = lax.broadcasted_iota(jnp.int32, (8, 128), 1)
     stride_in = MODES * TILES_IN
     stride_out = MODES * TILES_OUT
-    for m in range(MODES):
+    second = [jnp.broadcast_to(ey_ref[i:i + 1, :], (128, 256)).T[:NR // 2, :1] for i in range(2)]
+    def unpack(m):
         for y in range(YB):
             for h in range(2):
                 even, odd = [None, None], [None, None]
@@ -204,9 +210,9 @@
                 row = y * PY + h * 8
                 for t, tile in enumerate(even + odd):
                     x_ref[m, row:row + 8, t * 128:(t + 1) * 128] = tile
-    second = [jnp.broadcast_to(ey_ref[i:i + 1, :], (128, 256)).T[:NR // 2, :1] for i in range(2)]
-    for m in range(MODES):
-        z = jnp.concatenate([right_product(x_ref[m, :, i * 256:i * 256 + NR // 2], ax_ref.at[i]) for i in range(2)], axis=1)
+
+    def transform(m):
+        z = jnp.concatenate([right_product(x_ref[m, :, i * 256:(i + 1) * 256], ax_ref.at[i]) for i in range(2)], axis=1)
         z = z.reshape(YB, PY, 512)
         near = z[:, :8].reshape(YB * 8, 512)
         far = z[:, 8:].reshape(YB * 8, 512)
@@ -218,10 +224,11 @@
             z = jnp.where(is_zero, 0.0, z / jnp.where(is_zero, -1.0, total))
             halves.append(left_product(by_ref.at[i], z))
         z = jnp.concatenate([halves[0] + halves[1], halves[0] - halves[1]], axis=0)
-        even, odd = (right_product(z[:, i * 256:i * 256 + NR // 2], bx_ref.at[i]) for i in range(2))
+        even, odd = (right_product(z[:, i * 256:(i + 1) * 256], bx_ref.at[i]) for i in range(2))
         o_ref[m, :, :256] = even + odd
         o_ref[m, :, 256:] = even - odd
-    for m in range(MODES):
+
+    def pack(m):
         for p in range(PX):
             for h in range(2):
                 out = [None] * TILES_OUT
@@ -230,6 +237,16 @@
                     moved(lambda t: o_ref[m, row:row + 8, t * 128:(t + 1) * 128], p * 64, y * XE, XE, lane, out)
                 for t in range(TILES_OUT):
                     out_ref[pl.ds((p * PY + h * 8) * stride_out + m * TILES_OUT + t, 8, stride=stride_out), :] = out[t]
+
+    unpack(0)
+    transform(0)
+    unpack(1)
+    transform(1)
+    pack(0)
+    unpack(2)
+    transform(2)
+    pack(1)
+    pack(2)
 
 
 def solve_planes(own_eig, got, q, eig):
@@ -250,7 +267,8 @@
         bx = np.zeros((half, PX // 2, 64))
         for p in range(PX // 2):
             bx[:half, p, :XE] = part[(p * XB + np.arange(XE) - 1) % NR].T
-        for bucket, table in zip(tables, (ax, part[order].T, part[wide], bx.reshape(half, 256))):
+        for bucket, table in zip(tables, (ax, np.pad(part[order].T, ((0, 0), (0, 256 - half))),
+                                          np.pad(part[wide], ((0, 0), (0, 256 - half))), bx.reshape(half, 256))):
             bucket.append(table_pair(table))
     tables = [jnp.stack(bucket) for bucket in tables]
     vmem = pl.BlockSpec(memory_space=pltpu.VMEM)
@@ -265,21 +283,24 @@
     )(own_eig, in_vmem(got), *tables, jnp.asarray(ey, jnp.float32), jnp.asarray(ex, jnp.float32))
 
 
-def columns_of(s_ref, pair):
-    total = None
+def stacked_parts(s_ref):
+    his, lows = [], []
     for m in range(MODES):
         rows = jnp.concatenate(
             [s_ref[pl.ds(m * TILES_OUT + c, DEV, stride=MODES * TILES_OUT), :] for c in range(TILES_OUT)], axis=1)
         hi, low = split2(rows)
-        rows = slice(m * DEV, (m + 1) * DEV)
-        for left, right in ((hi, pair[0, rows]), (low, pair[0, rows]), (hi, pair[1, rows])):
-            part = lax.dot_general(left, right, (((0,), (0,)), ((), ())), preferred_element_type=jnp.float32)
-            total = part if total is None else total + part
-    return total
+        his.append(hi)
+        lows.append(low)
+    return jnp.concatenate(his + lows + his, axis=0)
+
+
+def columns_of(stacked, hi, low):
+    right = jnp.concatenate([hi, hi, low], axis=0)
+    return lax.dot_general(stacked, right, (((0,), (0,)), ((), ())), preferred_element_type=jnp.float32)
 
 
 def cut_kernel(start_ref, s_ref, g_ref, out_ref, p_ref):
-    cells = columns_of(s_ref, jnp.stack(split2(g_ref[...])))
+    cells = columns_of(stacked_parts(s_ref), *split2(g_ref[...]))
     for y in range(YE):
         p_ref[y, :XE, :] = cells[y * XE:(y + 1) * XE, :]
     lane = lax.broadcasted_iota(jnp.int32, (16, 128), 1)
@@ -287,8 +308,8 @@
     for t in range(PY):
         acc = jnp.zeros((16, 128), jnp.float32)
         for b in range(12):
-            first = pl.multiple_of(start_ref[0, t], 8)
-            tile = p_ref[start_ref[1, t] + b, pl.ds(first, 16), (t // 8) * 128:(t // 8 + 1) * 128]
+            first = pl.multiple_of(start_ref[t, 0], 8)
+            tile = p_ref[start_ref[t, 1] + b, pl.ds(first, 16), (t // 8) * 128:(t // 8 + 1) * 128]
             shift = (b * 10 - (t % 8) * 16) % 128
             if shift:
                 tile = pltpu.roll(tile, shift, 1)
@@ -313,8 +334,9 @@
 def block_kernel(s_ref, q_hbm, out_ref, q_ref, sem):
     copy = pltpu.make_async_copy(q_hbm, q_ref, sem)
     copy.start()
+    stacked = stacked_parts(s_ref)
     copy.wait()
-    cells = columns_of(s_ref, q_ref)
+    cells = columns_of(stacked, q_ref[0], q_ref[1])
     for y in range(YB):
         first = (y + 2) * XE + 1
         out_ref[:, y, :] = cells[first:first + XB, :]
@@ -359,7 +381,7 @@
         beside_ref[...] = jnp.where(near, 1.0, 0.0).astype(jnp.bfloat16)
         rows = rows_ref[...]
         ordered = jnp.concatenate(
-            [patch_ref[pl.ds(pl.multiple_of(flag_ref[j, 5] * 16, 16), 16), :] for j in range(PY)], axis=0)
+            [patch_ref[pl.ds(pl.multiple_of(flag_ref[j, 7] * 16, 16), 16), :] for j in range(PY)], axis=0)
         expanded = jnp.zeros((640, 128), jnp.float32)
         for part in split3(ordered):
             expanded += dot(rows, part)
@@ -377,7 +399,7 @@
     zero = jnp.zeros((8, 128), jnp.float32)
     slot_of = [step * GROUP + g for g in range(GROUP)]
     bases = [pl.multiple_of(s * 40, 8) for s in slot_of]
-    flag = lambda g, i: jnp.broadcast_to(flag_ref[slot_of[g], i], (8, 128)) > 0
+    flag = lambda g, i: jnp.broadcast_to(flag_ref[slot_of[g], i + 2], (8, 128)) > 0
     use_low, use_high, same_low, same_high, live = ([flag(g, i) for g in range(GROUP)] for i in range(5))
 
     def start(g, t, r):
@@ -540,7 +562,7 @@
             pltpu.HBM((slots, CELLS, CELLS * CELLS), jnp.float32),
             pltpu.HBM((3, slots, CELLS, CELLS * CELLS), jnp.float32),
         ],
-        compiler_params=pltpu.CompilerParams(vmem_limit_bytes=26 << 20),
+        compiler_params=pltpu.CompilerParams(vmem_limit_bytes=34 << 20),
         name="relax_and_kick",
     )(flags, patch, block_rows, table, in_hbm(density), low, high, in_hbm(velocity))
 
@@ -570,21 +592,22 @@
     columns = basis[third.reshape(-1)].T
     start_first = jnp.clip(anchors[0] - place_first * XB, 0, XB - REG)
     start_second = jnp.clip(anchors[1] - place_second * YB, 0, YB - REG)
-    sending = cut_patches(back, columns, jnp.stack([start_first, start_second]))
-    arrived = lax.all_to_all(sending, "py", 0, 0, tiled=True)
     positions = jnp.arange(slots, dtype=jnp.int32)
-
-    coarse_potential = block_of(back, q)
-
     first_slot = device * slots
     padded = jnp.pad(neighbour, ((0, 0), (slots, slots)), constant_values=-1)
     nearby = lax.dynamic_slice_in_dim(neighbour, first_slot, slots, 1)
     below = lax.dynamic_slice_in_dim(padded, first_slot, slots, 1)
     above = lax.dynamic_slice_in_dim(padded, first_slot + 2 * slots, slots, 1)
     flags = jnp.stack([
+        start_first, start_second,
         nearby[0] >= 0, nearby[1] >= 0, below[1] >= 0, above[0] >= 0,
         positions < slot_count[device], (place_second + positions) % PY,
     ], axis=1).astype(jnp.int32)
+    sending = cut_patches(back, columns, flags)
+    arrived = lax.all_to_all(sending, "py", 0, 0, tiled=True)
+
+    coarse_potential = block_of(back, q)
+
     subgrid_potential, kicked = relax(flags, arrived, subgrid_density, low, high, velocity)
     return coarse_potential, subgrid_potential, kicked
 

time: 119 us -> 117 us (0.983)
  Pallas kernels: 38.4 us -> 36 us
    all_to_all x1, waiting for transfers between devices: 0.01 us -> 1.88 us  [local(): arrived = lax.all_to_all(sending, 'py', 0, 0, tiled=True)]
    all_to_all x1, waiting for transfers between devices: 15.6 us -> 13.8 us  [local(): lax.all_to_all(solved, ('px', 'py'), 0, 0, tiled=True).reshape(-1, 128)]
    gather x2, local copies, waits for them, and re-layouts: 2.89 us -> 1.15 us  [local(): columns = basis[third.reshape(-1)].T]
    unnamed x27 -> x28, local copies, waits for them, and re-layouts: 1.42 us -> 2.77 us
  transfers between devices with their start and end apart: 5 -> 5, of which waited for: 2 -> 3; matrix products, arithmetic and copies ran while one was open for 9% -> 9% of each run, Pallas kernels for 8% -> 7%
where the time goes in v6:
time: 117 us; the launch traced here: 116 us
  waiting for transfers between devices  41.1 us (35%)
  Pallas kernels  36 us (31%)
  starting transfers between devices  26.9 us (23%)
  local copies, waits for them, and re-layouts  9.02 us (8%)
  other arithmetic  1.93 us (2%)
    all_to_all x1, waiting for transfers between devices, local(): lax.all_to_all(packed, ('px', 'py'), 0, 0, tiled=True).reshape(-1, 128)  25.4 us
    pallas_call x1, Pallas kernels, relax(): pl.pallas_call(relax_kernel, grid_spec=pltpu.PrefetchScalarGridSpec(num_s...  14.5 us
    all_to_all x1, waiting for transfers between devices, local(): lax.all_to_all(solved, ('px', 'py'), 0, 0, tiled=True).reshape(-1, 128)  13.8 us
    all_to_all x1, starting transfers between devices, local(): lax.all_to_all(packed, ('px', 'py'), 0, 0, tiled=True).reshape(-1, 128)  11.5 us
    pallas_call x1, Pallas kernels, solve_planes(): pl.pallas_call(plane_kernel, out_shape=pltpu.HBM((DEV * MODES * TILES_OUT...  8.98 us
    ppermute x2, starting transfers between devices, from_behind(): lax.ppermute(value, axis, [(source, source + steps) for source in range(i...  6.16 us
    all_to_all x1, starting transfers between devices, local(): lax.all_to_all(solved, ('px', 'py'), 0, 0, tiled=True).reshape(-1, 128)  4.99 us
    pallas_call x1, Pallas kernels, forward_third(): pl.pallas_call(forward_kernel, out_shape=pltpu.HBM((DEV * MODES * TILES_I...  4.88 us
  transfers between devices with their start and end apart: 5, of which 3 were waited for; matrix products, arithmetic and copies ran while one was open for 9% of the time, Pallas kernels for 7%

profile of v6, /device:TPU:1, one launch (start us, length us, event | category | flops | bytes accessed | tf_op | source)
XLA Modules:
  0.0 116.0 jit_solution(7473421455492632267)
XLA Ops:
  0.6 4.9 %forward_third.1 = f32[3456,128]{1,0:T(8,128)} custom-call(f32[48,24,384]{2,1,0:T(8,128)} %in_ref.1, bf16[2,384,384]{2,1,0:T(8,128)(2,1)} %constant.101.clone.q_hbm), custom_call_target="tpu_custom_call" | custom-call | tf_op jit(solution)/shard_map/forward_third/pallas_call | solution.py:176
  5.5 0.0 copy-start.8
  5.5 0.0 copy-start.1
  5.5 0.0 copy-start.2
  5.6 0.0 copy-start.3
  5.6 0.0 copy-start.4
  5.6 0.0 copy-start.6
  5.6 0.0 copy-start.7
  5.6 11.5 %all-to-all-start = ((f32[128,1,3456]{2,1,0:T(1,128)}), f32[128,1,3456]{2,1,0:T(1,128)S(1)}, u32[]{:S(2)}, u32[]{:S(2)}) async-start(f32[128,1,3456]{2,1,0:T(1,128)} %bitcast.30), calls=%async_computation | async-start | bytes 3538944 | tf_op jit(solution)/shard_map/all_to_all | solution.py:583
  17.2 0.6 gather_fusion
  17.8 25.4 %all-to-all-done = f32[128,1,3456]{2,1,0:T(1,128)S(1)} async-done(((f32[128,1,3456]{2,1,0:T(1,128)}), f32[128,1,3456]{2,1,0:T(1,128)S(1)}, u32[]{:S(2)}, u32[]{:S(2)}) %all-to-all-start) | async-done | bytes 1769504 | tf_op jit(solution)/shard_map/all_to_all | solution.py:583
  43.2 0.0 copy-done.3
  43.2 0.0 copy-done.4
  43.2 0.0 copy-done.6
  43.2 0.0 copy-done.7
  43.2 9.0 %solve_planes.1 = f32[4224,128]{1,0:T(8,128)} custom-call(f32[3]{0:T(128)S(1)} %gather_fusion, f32[3456,128]{1,0:T(8,128)S(1)} %bitcast.26, bf16[2,2,192,256]{3,2,1,0:T(8,128)(2,1)S(1)} %copy-done.4, bf16[2,2,192,256]{3,2,1,0:T(8,128)(2,1)S(1)} %copy-done.3, bf16[2,2,224,256]{3,2,1,0:T(8,128)(2,1)S(1)} %copy-done.1, bf16[2,2,192,256]{3,2,1,0:T(8,128)(2,1)S(1)} %copy-done.2, ...), custom_call_target="tpu_custom_call" | custom-call | tf_op jit(solution)/shard_map/solve_planes/pallas_call | solution.py:275
  52.2 5.0 %all-to-all-start.1 = ((f32[128,1,4224]{2,1,0:T(1,128)}), f32[128,1,4224]{2,1,0:T(1,128)S(1)}, u32[]{:S(2)}, u32[]{:S(2)}) async-start(f32[128,1,4224]{2,1,0:T(1,128)} %bitcast.29), calls=%async_computation.1 | async-start | bytes 4325376 | tf_op jit(solution)/shard_map/all_to_all | solution.py:586
  57.2 0.0 copy-start.12
  57.2 0.0 copy-start.9
  57.2 1.9 %fusion.19 = (f32[16,32,128]{2,1,0:T(8,128)}, f32[16,32,128]{2,1,0:T(8,128)}) fusion(f32[16,32,1024]{2,1,0:T(8,128)} %dens_hbm.1), kind=kLoop, calls=%fused_computation.48 | loop fusion | bytes 1048576 | tf_op jit(solution)/shard_map/slice | solution.py:579
  59.1 1.3 %collective-permute-start.1 = (f32[16,32,128]{2,1,0:T(8,128)}, f32[16,32,128]{2,1,0:T(8,128)S(1)}, u32[]{:S(2)}, u32[]{:S(2)}) collective-permute-start(f32[16,32,128]{2,1,0:T(8,128)} %get-tuple-element.7), channel_id=1, source_target_pairs={{1,0},{2,1},{3,2},{4,3},{5,4},{6,5},{7,6},{8,7},{9,8},{10,9},{11,1... | collective-permute-start | bytes 786440 | tf_op jit(solution)/shard_map/ppermute | solution.py:84
  60.4 4.9 %collective-permute-start = (f32[16,32,128]{2,1,0:T(8,128)}, f32[16,32,128]{2,1,0:T(8,128)}, u32[]{:S(2)}, u32[]{:S(2)}) collective-permute-start(f32[16,32,128]{2,1,0:T(8,128)} %get-tuple-element.8), channel_id=1, source_target_pairs={{0,1},{1,2},{2,3},{3,4},{4,5},{5,6},{6,7},{7,8},{8,9},{9,10},{10,1... | collective-permute-start | bytes 786440 | tf_op jit(solution)/shard_map/ppermute | solution.py:84
  65.3 0.0 copy-done.10
  65.3 1.3 %copy.47 = s32[3,2048]{0,1:T(8,128)} copy(s32[3,2048]{1,0:T(4,128)S(1)} %copy-done.10) | data formatting | bytes 49152 | tf_op args[3]
  66.6 0.1 fusion.3
  66.8 1.8 %gather_fusion.1 = s32[16,3]{1,0:T(8,128)S(1)} fusion(s32[3,2048]{0,1:T(8,128)} %copy.47, s32[1024]{0:T(1024)S(1)} %pad_clamp_fusion.1), kind=kCustom, calls=%fused_computation.1 | custom fusion | bytes 448 | tf_op jit(solution)/shard_map/gather | solution.py:590
  68.6 0.2 fusion.4
  68.8 0.1 add_remainder_fusion
  68.8 0.1 rem.70
  68.9 0.6 dynamic_slice.15
  69.5 0.7 fusion.17
  70.2 0.0 copy-done.9
  70.2 0.0 copy-start.11
  70.2 1.0 gather_fusion.2
  71.2 0.2 copy.56
  71.4 1.3 %copy.48 = s32[2,2048]{0,1:T(8,128)} copy(s32[2,2048]{1,0:T(2,128)S(1)} %copy-done.11) | data formatting | bytes 32768 | tf_op args[5]
  72.8 0.9 convert_bitcast_fusion
  73.6 0.1 stack.59.start_ref.flag_ref
  73.7 13.8 %all-to-all-done.1 = f32[128,1,4224]{2,1,0:T(1,128)S(1)} async-done(((f32[128,1,4224]{2,1,0:T(1,128)}), f32[128,1,4224]{2,1,0:T(1,128)S(1)}, u32[]{:S(2)}, u32[]{:S(2)}) %all-to-all-start.1) | async-done | bytes 2162720 | tf_op jit(solution)/shard_map/all_to_all | solution.py:586
  87.5 2.9 %cut_patches.1 = f32[256,128]{1,0:T(8,128)} custom-call(s32[16,8]{1,0:T(8,128)S(1)} %stack.59.start_ref.flag_ref, f32[4224,128]{1,0:T(8,128)S(1)} %bitcast.24, f32[384,256]{1,0:T(8,128)S(1)} %bitcast.27), custom_call_target="tpu_custom_call" | custom-call | tf_op jit(solution)/shard_map/cut_patches/pallas_call | solution.py:321
  90.4 4.2 %all-to-all-start.2 = ((f32[16,16,128]{2,1,0:T(8,128)}), f32[16,16,128]{2,1,0:T(8,128)S(1)}, u32[]{:S(2)}, u32[]{:S(2)}) async-start(f32[16,16,128]{2,1,0:T(8,128)} %bitcast.15), calls=%async_computation.2 | async-start | bytes 262144 | tf_op jit(solution)/shard_map/all_to_all | solution.py:607
  94.7 0.0 copy-start
  94.7 0.0 copy-start.5
  94.7 4.8 %block_of.1 = f32[48,24,384]{2,1,0:T(8,128)} custom-call(f32[4224,128]{1,0:T(8,128)S(1)} %bitcast.25, bf16[2,384,384]{2,1,0:T(8,128)(2,1)} %constant.101.clone.q_hbm), custom_call_target="tpu_custom_call" | custom-call | tf_op jit(solution)/shard_map/block_of/pallas_call | solution.py:346
  99.5 0.0 collective-permute-done.1.high_ref
  99.5 0.0 collective-permute-done.low_ref
  99.5 1.9 %all-to-all-done.2 = f32[16,16,128]{2,1,0:T(8,128)S(1)} async-done(((f32[16,16,128]{2,1,0:T(8,128)}), f32[16,16,128]{2,1,0:T(8,128)S(1)}, u32[]{:S(2)}, u32[]{:S(2)}) %all-to-all-start.2) | async-done | bytes 131104 | tf_op jit(solution)/shard_map/all_to_all | solution.py:607
  101.4 14.5 %relax_and_kick.1 = (f32[16,32,1024]{2,1,0:T(8,128)}, f32[3,16,32,1024]{3,2,1,0:T(8,128)}) custom-call(s32[16,8]{1,0:T(8,128)S(1)} %stack.59.start_ref.flag_ref, f32[256,128]{1,0:T(8,128)S(1)} %bitcast.28, bf16[640,256]{1,0:T(8,128)(2,1)S(1)} %copy-done.5, bf16[128,2560]{1,0:T(8,128)(2,1)S(1)} %copy-done, f32[16,32,1024]{2,1,0:T(8,128)} %dens_hbm.1, ...), custom_call_target="tpu_custom_call" | custom-call | tf_op jit(solution)/shard_map/relax_and_kick/pallas_call | solution.py:535
  (14 shorter events, 0.1 us)
Async XLA Ops:
  5.5 11.6 %copy-start.8 = (f32[384]{0:T(512)S(1)}, f32[384]{0:T(512)}, u32[]{:S(2)}) copy-start(f32[384]{0:T(512)} %constant.100.clone) | copy-start | bytes 4612
  5.5 37.7 %copy-start.1 = (bf16[2,2,224,256]{3,2,1,0:T(8,128)(2,1)S(1)}, bf16[2,2,224,256]{3,2,1,0:T(8,128)(2,1)}, u32[]{:S(2)}) copy-start(bf16[2,2,224,256]{3,2,1,0:T(8,128)(2,1)} %constant.127.by_ref) | copy-start | bytes 1376260
  5.5 37.6 %copy-start.2 = (bf16[2,2,192,256]{3,2,1,0:T(8,128)(2,1)S(1)}, bf16[2,2,192,256]{3,2,1,0:T(8,128)(2,1)}, u32[]{:S(2)}) copy-start(bf16[2,2,192,256]{3,2,1,0:T(8,128)(2,1)} %constant.130.bx_ref) | copy-start | bytes 1179652
  5.6 37.6 %copy-start.3 = (bf16[2,2,192,256]{3,2,1,0:T(8,128)(2,1)S(1)}, bf16[2,2,192,256]{3,2,1,0:T(8,128)(2,1)}, u32[]{:S(2)}) copy-start(bf16[2,2,192,256]{3,2,1,0:T(8,128)(2,1)} %constant.124.ay_ref) | copy-start | bytes 1179652
  5.6 37.6 %copy-start.4 = (bf16[2,2,192,256]{3,2,1,0:T(8,128)(2,1)S(1)}, bf16[2,2,192,256]{3,2,1,0:T(8,128)(2,1)}, u32[]{:S(2)}) copy-start(bf16[2,2,192,256]{3,2,1,0:T(8,128)(2,1)} %constant.121.ax_ref) | copy-start | bytes 1179652
  5.6 37.6 %copy-start.6 = (f32[1,512]{1,0:T(1,128)S(1)}, f32[1,512]{1,0:T(1,128)}, u32[]{:S(2)}) copy-start(f32[1,512]{1,0:T(1,128)} %constant.111.clone.ex_ref) | copy-start | bytes 6148
  5.6 37.6 %copy-start.7 = (f32[2,256]{1,0:T(2,128)S(1)}, f32[2,256]{1,0:T(2,128)}, u32[]{:S(2)}) copy-start(f32[2,256]{1,0:T(2,128)} %constant.110.clone.ey_ref) | copy-start | bytes 6148
  5.6 37.6 %all-to-all-start = ((f32[128,1,3456]{2,1,0:T(1,128)}), f32[128,1,3456]{2,1,0:T(1,128)S(1)}, u32[]{:S(2)}, u32[]{:S(2)}) async-start(f32[128,1,3456]{2,1,0:T(1,128)} %bitcast.30), calls=%async_computation | async-start | bytes 3538944 | tf_op jit(solution)/shard_map/all_to_all | solution.py:583
  52.2 13.1 %copy-start.10 = (s32[3,2048]{1,0:T(4,128)S(1)}, s32[3,2048]{1,0:T(4,128)}, u32[]{:S(2)}) copy-start(s32[3,2048]{1,0:T(4,128)} %param.25) | copy-start | bytes 73732
  52.2 35.3 %all-to-all-start.1 = ((f32[128,1,4224]{2,1,0:T(1,128)}), f32[128,1,4224]{2,1,0:T(1,128)S(1)}, u32[]{:S(2)}, u32[]{:S(2)}) async-start(f32[128,1,4224]{2,1,0:T(1,128)} %bitcast.29), calls=%async_computation.1 | async-start | bytes 4325376 | tf_op jit(solution)/shard_map/all_to_all | solution.py:586
  57.2 11.7 %copy-start.12 = (s32[128]{0:T(128)S(1)}, s32[128]{0:T(128)}, u32[]{:S(2)}) copy-start(s32[128]{0:T(128)} %param.26) | copy-start | bytes 1540
  57.2 13.0 %copy-start.9 = (f32[384,384]{1,0:T(8,128)S(1)}, f32[384,384]{1,0:T(8,128)}, u32[]{:S(2)}) copy-start(f32[384,384]{1,0:T(8,128)} %constant.99.clone) | copy-start | bytes 1769476
  59.1 40.3 %collective-permute-start.1 = (f32[16,32,128]{2,1,0:T(8,128)}, f32[16,32,128]{2,1,0:T(8,128)S(1)}, u32[]{:S(2)}, u32[]{:S(2)}) collective-permute-start(f32[16,32,128]{2,1,0:T(8,128)} %get-tuple-element.7), channel_id=1, source_target_pairs={{1,0},{2,1},{3,2},{4,3},{5,4},{6,5},{7,6},{8,7},{9,8},{10,9},{11,1... | collective-permute-start | bytes 786440 | tf_op jit(solution)/shard_map/ppermute | solution.py:84
  60.4 39.1 %collective-permute-start = (f32[16,32,128]{2,1,0:T(8,128)}, f32[16,32,128]{2,1,0:T(8,128)}, u32[]{:S(2)}, u32[]{:S(2)}) collective-permute-start(f32[16,32,128]{2,1,0:T(8,128)} %get-tuple-element.8), channel_id=1, source_target_pairs={{0,1},{1,2},{2,3},{3,4},{4,5},{5,6},{6,7},{7,8},{8,9},{9,10},{10,1... | collective-permute-start | bytes 786440 | tf_op jit(solution)/shard_map/ppermute | solution.py:84
  70.2 1.2 %copy-start.11 = (s32[2,2048]{1,0:T(2,128)S(1)}, s32[2,2048]{1,0:T(2,128)}, u32[]{:S(2)}) copy-start(s32[2,2048]{1,0:T(2,128)} %param.27) | copy-start | bytes 49156
  90.4 10.9 %all-to-all-start.2 = ((f32[16,16,128]{2,1,0:T(8,128)}), f32[16,16,128]{2,1,0:T(8,128)S(1)}, u32[]{:S(2)}, u32[]{:S(2)}) async-start(f32[16,16,128]{2,1,0:T(8,128)} %bitcast.15), calls=%async_computation.2 | async-start | bytes 262144 | tf_op jit(solution)/shard_map/all_to_all | solution.py:607
  94.7 6.7 %copy-start = (bf16[128,2560]{1,0:T(8,128)(2,1)S(1)}, bf16[128,2560]{1,0:T(8,128)(2,1)}, u32[]{:S(2)}) copy-start(bf16[128,2560]{1,0:T(8,128)(2,1)} %constant.113.clone.cols_ref) | copy-start | bytes 1966084
  94.7 6.7 %copy-start.5 = (bf16[640,256]{1,0:T(8,128)(2,1)S(1)}, bf16[640,256]{1,0:T(8,128)(2,1)}, u32[]{:S(2)}) copy-start(bf16[640,256]{1,0:T(8,128)(2,1)} %constant.112.clone.rows_ref) | copy-start | bytes 983044

commit v7 on v6

--- a/solution.py
+++ b/solution.py
@@ -154,8 +154,10 @@
 def forward_kernel(in_ref, q_hbm, out_ref, rows_ref, q_ref, sem):
     copies = [pltpu.make_async_copy(in_ref.at[:, y], rows_ref.at[y], sem.at[y]) for y in range(YB)]
     table = pltpu.make_async_copy(q_hbm, q_ref, sem.at[YB])
+    for copy in copies[:8]:
+        copy.start()
     table.start()
-    for copy in copies:
+    for copy in copies[8:]:
         copy.start()
     table.wait()
     contract = (((1,), (1,)), ((), ()))

time: 117 us -> 117 us (level)
  no operation moved by 1% of the time
where the time goes in v7:
time: 117 us; the launch traced here: 116 us
  waiting for transfers between devices  41.1 us (35%)
  Pallas kernels  36.2 us (31%)
  starting transfers between devices  26.9 us (23%)
  local copies, waits for them, and re-layouts  9.02 us (8%)
  other arithmetic  1.93 us (2%)
    all_to_all x1, waiting for transfers between devices, local(): lax.all_to_all(packed, ('px', 'py'), 0, 0, tiled=True).reshape(-1, 128)  25.4 us
    pallas_call x1, Pallas kernels, relax(): pl.pallas_call(relax_kernel, grid_spec=pltpu.PrefetchScalarGridSpec(num_s...  14.5 us
    all_to_all x1, waiting for transfers between devices, local(): lax.all_to_all(solved, ('px', 'py'), 0, 0, tiled=True).reshape(-1, 128)  13.8 us
    all_to_all x1, starting transfers between devices, local(): lax.all_to_all(packed, ('px', 'py'), 0, 0, tiled=True).reshape(-1, 128)  11.5 us
    pallas_call x1, Pallas kernels, solve_planes(): pl.pallas_call(plane_kernel, out_shape=pltpu.HBM((DEV * MODES * TILES_OUT...  8.98 us
    ppermute x2, starting transfers between devices, from_behind(): lax.ppermute(value, axis, [(source, source + steps) for source in range(i...  6.16 us
    pallas_call x1, Pallas kernels, forward_third(): pl.pallas_call(forward_kernel, out_shape=pltpu.HBM((DEV * MODES * TILES_I...  5.02 us
    all_to_all x1, starting transfers between devices, local(): lax.all_to_all(solved, ('px', 'py'), 0, 0, tiled=True).reshape(-1, 128)  4.99 us
  transfers between devices with their start and end apart: 5, of which 3 were waited for; matrix products, arithmetic and copies ran while one was open for 9% of the time, Pallas kernels for 7%

profile of v7, /device:TPU:1, one launch (start us, length us, event | category | flops | bytes accessed | tf_op | source)
XLA Modules:
  0.0 116.2 jit_solution(16946385561174264325)
XLA Ops:
  0.6 5.0 %forward_third.1 = f32[3456,128]{1,0:T(8,128)} custom-call(f32[48,24,384]{2,1,0:T(8,128)} %in_ref.1, bf16[2,384,384]{2,1,0:T(8,128)(2,1)} %constant.101.clone.q_hbm), custom_call_target="tpu_custom_call" | custom-call | tf_op jit(solution)/shard_map/forward_third/pallas_call | solution.py:178
  5.7 0.0 copy-start.8
  5.7 0.0 copy-start.1
  5.7 0.0 copy-start.2
  5.7 0.0 copy-start.3
  5.7 0.0 copy-start.4
  5.7 0.0 copy-start.6
  5.7 0.0 copy-start.7
  5.7 11.5 %all-to-all-start = ((f32[128,1,3456]{2,1,0:T(1,128)}), f32[128,1,3456]{2,1,0:T(1,128)S(1)}, u32[]{:S(2)}, u32[]{:S(2)}) async-start(f32[128,1,3456]{2,1,0:T(1,128)} %bitcast.30), calls=%async_computation | async-start | bytes 3538944 | tf_op jit(solution)/shard_map/all_to_all | solution.py:585
  17.3 0.0 copy-done.8
  17.3 0.6 gather_fusion
  17.9 25.4 %all-to-all-done = f32[128,1,3456]{2,1,0:T(1,128)S(1)} async-done(((f32[128,1,3456]{2,1,0:T(1,128)}), f32[128,1,3456]{2,1,0:T(1,128)S(1)}, u32[]{:S(2)}, u32[]{:S(2)}) %all-to-all-start) | async-done | bytes 1769504 | tf_op jit(solution)/shard_map/all_to_all | solution.py:585
  43.3 0.0 copy-done.1
  43.3 0.0 copy-done.2
  43.3 0.0 copy-done.3
  43.3 0.0 copy-done.4
  43.3 0.0 copy-done.6
  43.4 9.0 %solve_planes.1 = f32[4224,128]{1,0:T(8,128)} custom-call(f32[3]{0:T(128)S(1)} %gather_fusion, f32[3456,128]{1,0:T(8,128)S(1)} %bitcast.26, bf16[2,2,192,256]{3,2,1,0:T(8,128)(2,1)S(1)} %copy-done.4, bf16[2,2,192,256]{3,2,1,0:T(8,128)(2,1)S(1)} %copy-done.3, bf16[2,2,224,256]{3,2,1,0:T(8,128)(2,1)S(1)} %copy-done.1, bf16[2,2,192,256]{3,2,1,0:T(8,128)(2,1)S(1)} %copy-done.2, ...), custom_call_target="tpu_custom_call" | custom-call | tf_op jit(solution)/shard_map/solve_planes/pallas_call | solution.py:277
  52.3 5.0 %all-to-all-start.1 = ((f32[128,1,4224]{2,1,0:T(1,128)}), f32[128,1,4224]{2,1,0:T(1,128)S(1)}, u32[]{:S(2)}, u32[]{:S(2)}) async-start(f32[128,1,4224]{2,1,0:T(1,128)} %bitcast.29), calls=%async_computation.1 | async-start | bytes 4325376 | tf_op jit(solution)/shard_map/all_to_all | solution.py:588
  57.3 0.0 copy-start.12
  57.4 0.0 copy-start.9
  57.4 1.9 %fusion.19 = (f32[16,32,128]{2,1,0:T(8,128)}, f32[16,32,128]{2,1,0:T(8,128)}) fusion(f32[16,32,1024]{2,1,0:T(8,128)} %dens_hbm.1), kind=kLoop, calls=%fused_computation.48 | loop fusion | bytes 1048576 | tf_op jit(solution)/shard_map/slice | solution.py:581
  59.3 1.3 %collective-permute-start.1 = (f32[16,32,128]{2,1,0:T(8,128)}, f32[16,32,128]{2,1,0:T(8,128)S(1)}, u32[]{:S(2)}, u32[]{:S(2)}) collective-permute-start(f32[16,32,128]{2,1,0:T(8,128)} %get-tuple-element.7), channel_id=1, source_target_pairs={{1,0},{2,1},{3,2},{4,3},{5,4},{6,5},{7,6},{8,7},{9,8},{10,9},{11,1... | collective-permute-start | bytes 786440 | tf_op jit(solution)/shard_map/ppermute | solution.py:84
  60.6 4.9 %collective-permute-start = (f32[16,32,128]{2,1,0:T(8,128)}, f32[16,32,128]{2,1,0:T(8,128)}, u32[]{:S(2)}, u32[]{:S(2)}) collective-permute-start(f32[16,32,128]{2,1,0:T(8,128)} %get-tuple-element.8), channel_id=1, source_target_pairs={{0,1},{1,2},{2,3},{3,4},{4,5},{5,6},{6,7},{7,8},{8,9},{9,10},{10,1... | collective-permute-start | bytes 786440 | tf_op jit(solution)/shard_map/ppermute | solution.py:84
  65.4 1.3 %copy.47 = s32[3,2048]{0,1:T(8,128)} copy(s32[3,2048]{1,0:T(4,128)S(1)} %copy-done.10) | data formatting | bytes 49152 | tf_op args[3]
  66.8 0.1 fusion.3
  66.9 1.8 %gather_fusion.1 = s32[16,3]{1,0:T(8,128)S(1)} fusion(s32[3,2048]{0,1:T(8,128)} %copy.47, s32[1024]{0:T(1024)S(1)} %pad_clamp_fusion.1), kind=kCustom, calls=%fused_computation.1 | custom fusion | bytes 448 | tf_op jit(solution)/shard_map/gather | solution.py:592
  68.7 0.2 fusion.4
  68.9 0.1 add_remainder_fusion
  69.0 0.1 rem.70
  69.1 0.6 dynamic_slice.15
  69.7 0.7 fusion.17
  70.4 0.0 copy-start.11
  70.4 1.0 gather_fusion.2
  71.4 0.2 copy.56
  71.6 1.3 %copy.48 = s32[2,2048]{0,1:T(8,128)} copy(s32[2,2048]{1,0:T(2,128)S(1)} %copy-done.11) | data formatting | bytes 32768 | tf_op args[5]
  72.9 0.9 convert_bitcast_fusion
  73.8 0.1 stack.59.start_ref.flag_ref
  73.8 13.8 %all-to-all-done.1 = f32[128,1,4224]{2,1,0:T(1,128)S(1)} async-done(((f32[128,1,4224]{2,1,0:T(1,128)}), f32[128,1,4224]{2,1,0:T(1,128)S(1)}, u32[]{:S(2)}, u32[]{:S(2)}) %all-to-all-start.1) | async-done | bytes 2162720 | tf_op jit(solution)/shard_map/all_to_all | solution.py:588
  87.6 2.9 %cut_patches.1 = f32[256,128]{1,0:T(8,128)} custom-call(s32[16,8]{1,0:T(8,128)S(1)} %stack.59.start_ref.flag_ref, f32[4224,128]{1,0:T(8,128)S(1)} %bitcast.24, f32[384,256]{1,0:T(8,128)S(1)} %bitcast.27), custom_call_target="tpu_custom_call" | custom-call | tf_op jit(solution)/shard_map/cut_patches/pallas_call | solution.py:323
  90.6 4.2 %all-to-all-start.2 = ((f32[16,16,128]{2,1,0:T(8,128)}), f32[16,16,128]{2,1,0:T(8,128)S(1)}, u32[]{:S(2)}, u32[]{:S(2)}) async-start(f32[16,16,128]{2,1,0:T(8,128)} %bitcast.15), calls=%async_computation.2 | async-start | bytes 262144 | tf_op jit(solution)/shard_map/all_to_all | solution.py:609
  94.8 0.0 copy-start
  94.8 0.0 copy-start.5
  94.8 4.8 %block_of.1 = f32[48,24,384]{2,1,0:T(8,128)} custom-call(f32[4224,128]{1,0:T(8,128)S(1)} %bitcast.25, bf16[2,384,384]{2,1,0:T(8,128)(2,1)} %constant.101.clone.q_hbm), custom_call_target="tpu_custom_call" | custom-call | tf_op jit(solution)/shard_map/block_of/pallas_call | solution.py:348
  99.6 0.0 collective-permute-done.1.high_ref
  99.6 0.0 collective-permute-done.low_ref
  99.6 1.9 %all-to-all-done.2 = f32[16,16,128]{2,1,0:T(8,128)S(1)} async-done(((f32[16,16,128]{2,1,0:T(8,128)}), f32[16,16,128]{2,1,0:T(8,128)S(1)}, u32[]{:S(2)}, u32[]{:S(2)}) %all-to-all-start.2) | async-done | bytes 131104 | tf_op jit(solution)/shard_map/all_to_all | solution.py:609
  101.5 14.5 %relax_and_kick.1 = (f32[16,32,1024]{2,1,0:T(8,128)}, f32[3,16,32,1024]{3,2,1,0:T(8,128)}) custom-call(s32[16,8]{1,0:T(8,128)S(1)} %stack.59.start_ref.flag_ref, f32[256,128]{1,0:T(8,128)S(1)} %bitcast.28, bf16[640,256]{1,0:T(8,128)(2,1)S(1)} %copy-done.5, bf16[128,2560]{1,0:T(8,128)(2,1)S(1)} %copy-done, f32[16,32,1024]{2,1,0:T(8,128)} %dens_hbm.1, ...), custom_call_target="tpu_custom_call" | custom-call | tf_op jit(solution)/shard_map/relax_and_kick/pallas_call | solution.py:537
  (14 shorter events, 0.1 us)
Async XLA Ops:
  5.7 11.6 %copy-start.8 = (f32[384]{0:T(512)S(1)}, f32[384]{0:T(512)}, u32[]{:S(2)}) copy-start(f32[384]{0:T(512)} %constant.100.clone) | copy-start | bytes 4612
  5.7 37.7 %copy-start.1 = (bf16[2,2,224,256]{3,2,1,0:T(8,128)(2,1)S(1)}, bf16[2,2,224,256]{3,2,1,0:T(8,128)(2,1)}, u32[]{:S(2)}) copy-start(bf16[2,2,224,256]{3,2,1,0:T(8,128)(2,1)} %constant.127.by_ref) | copy-start | bytes 1376260
  5.7 37.6 %copy-start.2 = (bf16[2,2,192,256]{3,2,1,0:T(8,128)(2,1)S(1)}, bf16[2,2,192,256]{3,2,1,0:T(8,128)(2,1)}, u32[]{:S(2)}) copy-start(bf16[2,2,192,256]{3,2,1,0:T(8,128)(2,1)} %constant.130.bx_ref) | copy-start | bytes 1179652
  5.7 37.6 %copy-start.3 = (bf16[2,2,192,256]{3,2,1,0:T(8,128)(2,1)S(1)}, bf16[2,2,192,256]{3,2,1,0:T(8,128)(2,1)}, u32[]{:S(2)}) copy-start(bf16[2,2,192,256]{3,2,1,0:T(8,128)(2,1)} %constant.124.ay_ref) | copy-start | bytes 1179652
  5.7 37.6 %copy-start.4 = (bf16[2,2,192,256]{3,2,1,0:T(8,128)(2,1)S(1)}, bf16[2,2,192,256]{3,2,1,0:T(8,128)(2,1)}, u32[]{:S(2)}) copy-start(bf16[2,2,192,256]{3,2,1,0:T(8,128)(2,1)} %constant.121.ax_ref) | copy-start | bytes 1179652
  5.7 37.6 %copy-start.6 = (f32[1,512]{1,0:T(1,128)S(1)}, f32[1,512]{1,0:T(1,128)}, u32[]{:S(2)}) copy-start(f32[1,512]{1,0:T(1,128)} %constant.111.clone.ex_ref) | copy-start | bytes 6148
  5.7 37.6 %copy-start.7 = (f32[2,256]{1,0:T(2,128)S(1)}, f32[2,256]{1,0:T(2,128)}, u32[]{:S(2)}) copy-start(f32[2,256]{1,0:T(2,128)} %constant.110.clone.ey_ref) | copy-start | bytes 6148
  5.7 37.6 %all-to-all-start = ((f32[128,1,3456]{2,1,0:T(1,128)}), f32[128,1,3456]{2,1,0:T(1,128)S(1)}, u32[]{:S(2)}, u32[]{:S(2)}) async-start(f32[128,1,3456]{2,1,0:T(1,128)} %bitcast.30), calls=%async_computation | async-start | bytes 3538944 | tf_op jit(solution)/shard_map/all_to_all | solution.py:585
  52.3 13.1 %copy-start.10 = (s32[3,2048]{1,0:T(4,128)S(1)}, s32[3,2048]{1,0:T(4,128)}, u32[]{:S(2)}) copy-start(s32[3,2048]{1,0:T(4,128)} %param.25) | copy-start | bytes 73732
  52.3 35.3 %all-to-all-start.1 = ((f32[128,1,4224]{2,1,0:T(1,128)}), f32[128,1,4224]{2,1,0:T(1,128)S(1)}, u32[]{:S(2)}, u32[]{:S(2)}) async-start(f32[128,1,4224]{2,1,0:T(1,128)} %bitcast.29), calls=%async_computation.1 | async-start | bytes 4325376 | tf_op jit(solution)/shard_map/all_to_all | solution.py:588
  57.3 11.7 %copy-start.12 = (s32[128]{0:T(128)S(1)}, s32[128]{0:T(128)}, u32[]{:S(2)}) copy-start(s32[128]{0:T(128)} %param.26) | copy-start | bytes 1540
  57.4 13.0 %copy-start.9 = (f32[384,384]{1,0:T(8,128)S(1)}, f32[384,384]{1,0:T(8,128)}, u32[]{:S(2)}) copy-start(f32[384,384]{1,0:T(8,128)} %constant.99.clone) | copy-start | bytes 1769476
  59.3 40.3 %collective-permute-start.1 = (f32[16,32,128]{2,1,0:T(8,128)}, f32[16,32,128]{2,1,0:T(8,128)S(1)}, u32[]{:S(2)}, u32[]{:S(2)}) collective-permute-start(f32[16,32,128]{2,1,0:T(8,128)} %get-tuple-element.7), channel_id=1, source_target_pairs={{1,0},{2,1},{3,2},{4,3},{5,4},{6,5},{7,6},{8,7},{9,8},{10,9},{11,1... | collective-permute-start | bytes 786440 | tf_op jit(solution)/shard_map/ppermute | solution.py:84
  60.6 39.1 %collective-permute-start = (f32[16,32,128]{2,1,0:T(8,128)}, f32[16,32,128]{2,1,0:T(8,128)}, u32[]{:S(2)}, u32[]{:S(2)}) collective-permute-start(f32[16,32,128]{2,1,0:T(8,128)} %get-tuple-element.8), channel_id=1, source_target_pairs={{0,1},{1,2},{2,3},{3,4},{4,5},{5,6},{6,7},{7,8},{8,9},{9,10},{10,1... | collective-permute-start | bytes 786440 | tf_op jit(solution)/shard_map/ppermute | solution.py:84
  70.4 1.2 %copy-start.11 = (s32[2,2048]{1,0:T(2,128)S(1)}, s32[2,2048]{1,0:T(2,128)}, u32[]{:S(2)}) copy-start(s32[2,2048]{1,0:T(2,128)} %param.27) | copy-start | bytes 49156
  90.6 10.9 %all-to-all-start.2 = ((f32[16,16,128]{2,1,0:T(8,128)}), f32[16,16,128]{2,1,0:T(8,128)S(1)}, u32[]{:S(2)}, u32[]{:S(2)}) async-start(f32[16,16,128]{2,1,0:T(8,128)} %bitcast.15), calls=%async_computation.2 | async-start | bytes 262144 | tf_op jit(solution)/shard_map/all_to_all | solution.py:609
  94.8 6.7 %copy-start = (bf16[128,2560]{1,0:T(8,128)(2,1)S(1)}, bf16[128,2560]{1,0:T(8,128)(2,1)}, u32[]{:S(2)}) copy-start(bf16[128,2560]{1,0:T(8,128)(2,1)} %constant.113.clone.cols_ref) | copy-start | bytes 1966084
  94.8 6.7 %copy-start.5 = (bf16[640,256]{1,0:T(8,128)(2,1)S(1)}, bf16[640,256]{1,0:T(8,128)(2,1)}, u32[]{:S(2)}) copy-start(bf16[640,256]{1,0:T(8,128)(2,1)} %constant.112.clone.rows_ref) | copy-start | bytes 983044
